TPU v7x, 32 devices: a whole 2x2x4 slice. The times are simulated.
32 devices in a mesh: tm: 16 (over z, y, x), feat: 2 (over core).
Axes of the slice: x: 2, y: 2, z: 4, core: 2. Of those that a mesh axis runs over, the one named last changes fastest.
Arguments:
- margins: float32 [32, 24576], P('feat', 'tm'), may hold values from -6 to 256
- events: int32 [32, 24576], P('feat', 'tm'), may hold values 0 or 1
- tie_group: int32 [24576], P('tm'), may hold values from 0 to 24575, as said below
- in_node: int32 [24576], P('tm'), may hold values 0 or 1
- bins: int32 [512, 24576], P('feat', 'tm'), may hold values from 0 to 255
Outputs:
- grad: bfloat16 [32, 24576], P('feat', 'tm')
- hess: bfloat16 [32, 24576], P('feat', 'tm')
- gain: float32 [2, 256, 256], P('feat', 'tm')
Inputs may be any that keep to these rules, and one draw needn't show every extreme that they name: `tie_group`: group ids never fall; a group's id is the position of its first row; a new group begins at the first row of each block of 1536 rows and at the last row, so no group holds rows of two devices.
All inputs are finite; a program needn't handle non-finite values. No bound on the sum of `events` or of `in_node` on one device may be relied on, other than what follows from the above.
Results may differ from a plain program's by a relative error of at most 0.0034.
Values may be sent and summed in bfloat16 or wider, within the bound.
No kernel may reach another device: no remote copies, remote signals or barrier semaphores. Data moves between devices by JAX's collectives and lax.ppermute only.
A program may use at most 128 MiB of HBM per device.

v0:
```python
import jax
import jax.numpy as jnp
from jax import lax
from jax.sharding import PartitionSpec as P

BINS = 256


log_floor = -1e30


def carried_in(part, axis, combine, identity, reverse):
    count = lax.axis_size(axis)
    place = lax.axis_index(axis)
    ahead = count - 1 - place if reverse else place
    gathered = jax.tree.map(lambda a: lax.all_gather(a, axis), part)
    state = jax.tree.map(lambda a, e: jnp.zeros_like(a) + jnp.asarray(e, a.dtype), part, identity)

    def one(hop, state):
        source = count - 1 - hop if reverse else hop
        return combine(
            state, jax.tree.map(lambda a: lax.dynamic_index_in_dim(a, source, 0, False), gathered)
        )

    return lax.fori_loop(0, ahead, one, state)


def log_add(earlier, later):
    peak = jnp.maximum(earlier[0], later[0])
    return (peak, earlier[1] * jnp.exp(earlier[0] - peak) + later[1] * jnp.exp(later[0] - peak))


def log_add_pair(earlier, later):
    peak = jnp.maximum(earlier[0], later[0])
    early_scale = jnp.exp(earlier[0] - peak)
    late_scale = jnp.exp(later[0] - peak)
    return (
        peak,
        earlier[1] * early_scale + later[1] * late_scale,
        earlier[2] * early_scale * early_scale + later[2] * late_scale * late_scale,
    )


def group_bounds(tie_group):
    length = tie_group.shape[0]
    position = jnp.arange(length, dtype=jnp.int32)
    change = tie_group[1:] != tie_group[:-1]
    group_open = jnp.concatenate([jnp.ones((1,), jnp.bool_), change])
    group_close = jnp.concatenate([change, jnp.ones((1,), jnp.bool_)])
    start_pos = lax.cummax(jnp.where(group_open, position, 0), axis=0)
    end_pos = lax.cummin(jnp.where(group_close, position, length - 1), axis=0, reverse=True)
    return (start_pos, end_pos)


def bin_histogram(code_block, pair_block):
    feature_count, length = code_block.shape
    endpoint_count = pair_block.shape[1]
    group_size = max(1, min(feature_count, 16384 // length))
    while feature_count % group_size != 0:
        group_size = group_size - 1
    levels = jnp.arange(BINS, dtype=jnp.int32)
    span_count = length // length
    code_spans = code_block.reshape(
        feature_count // group_size, group_size, span_count, length
    ).transpose(2, 0, 1, 3)
    pair_spans = pair_block.reshape(2, endpoint_count, span_count, length).transpose(2, 0, 1, 3)

    def one_span(running, span_inputs):
        code_span, pair_span = span_inputs

        def one_group(group_codes):
            onehot = (group_codes[:, None, :] == levels[None, :, None]).astype(jnp.bfloat16)
            return jnp.einsum(
                "gkr,fbr->fgkb", pair_span, onehot, preferred_element_type=jnp.float32
            )

        portion = lax.map(one_group, code_span)
        return (running + portion.reshape(feature_count, 2, endpoint_count, BINS), None)

    initial = jnp.zeros((feature_count, 2, endpoint_count, BINS), jnp.float32)
    running, _ = lax.scan(one_span, initial, (code_spans, pair_spans))
    return running


def split_gain(histogram):
    left = jnp.cumsum(histogram, axis=3)
    whole = left[:, :, :, -1:]
    right = whole - left

    def ratio_term(portion):
        return portion[:, 0] * portion[:, 0] / (portion[:, 1] + 1.0)

    return jnp.mean(ratio_term(left) + ratio_term(right) - ratio_term(whole), axis=1)


def on_device(margins, events, tie_group, in_node, bins):
    endpoint_count = margins.shape[0]
    start_pos, end_pos = group_bounds(tie_group)
    unit_mass = jnp.ones_like(margins)
    risk_max, risk_sum = lax.associative_scan(log_add, (margins, unit_mass), reverse=True, axis=1)
    empty_max = jnp.full((endpoint_count,), log_floor, jnp.float32)
    nothing = jnp.zeros((endpoint_count,), jnp.float32)
    suffix_max, suffix_sum = carried_in(
        (risk_max[:, 0], risk_sum[:, 0]), "tm", log_add, (empty_max, nothing), True
    )
    whole_max, whole_sum = log_add((risk_max, risk_sum), (suffix_max[:, None], suffix_sum[:, None]))
    risk_log = jnp.take(whole_max + jnp.log(whole_sum), start_pos, axis=1)
    happened = events == 1
    event_mass = happened.astype(jnp.float32)
    event_log = jnp.where(happened, -risk_log, log_floor)
    local_max, local_first, local_second = lax.associative_scan(
        log_add_pair, (event_log, event_mass, event_mass), axis=1
    )
    prefix_max, prefix_first, prefix_second = carried_in(
        (local_max[:, -1], local_first[:, -1], local_second[:, -1]),
        "tm",
        log_add_pair,
        (empty_max, nothing, nothing),
        False,
    )
    event_max, first_sum, second_sum = log_add_pair(
        (prefix_max[:, None], prefix_first[:, None], prefix_second[:, None]),
        (local_max, local_first, local_second),
    )
    event_max = jnp.take(event_max, end_pos, axis=1)
    first_sum = jnp.take(first_sum, end_pos, axis=1)
    second_sum = jnp.take(second_sum, end_pos, axis=1)
    scaled = jnp.exp(margins + event_max)
    grad = (scaled * first_sum - event_mass).astype(jnp.bfloat16)
    hess = (scaled * first_sum - scaled * scaled * second_sum).astype(jnp.bfloat16)
    chosen = (in_node == 1)[None, :]
    zero = jnp.zeros_like(grad)
    pairs = jnp.stack([jnp.where(chosen, grad, zero), jnp.where(chosen, hess, zero)])
    pair_all = lax.all_gather(pairs, "feat", axis=1, tiled=True)
    histogram = lax.psum_scatter(
        bin_histogram(bins, pair_all), "tm", scatter_dimension=0, tiled=True
    )
    return (grad, hess, split_gain(histogram)[None])


def solution(mesh):
    in_specs = (P("feat", "tm"), P("feat", "tm"), P("tm"), P("tm"), P("feat", "tm"))
    out_specs = (P("feat", "tm"), P("feat", "tm"), P("feat", "tm", None))
    return jax.shard_map(
        on_device, mesh=mesh, in_specs=in_specs, out_specs=out_specs, check_vma=False
    )
```

profile of v0, /device:TPU:0, one launch (start us, length us, event | category | flops | bytes accessed | tf_op | source)
XLA Modules:
  0.0 713.1 jit_solution(8909099449665323683)
XLA Ops:
  51.1 43.5 %all-reduce.107 = (f32[256]{0:T(256)S(1)}, f32[256]{0:T(256)S(1)}) all-reduce(f32[256]{0:T(256)S(1)} %dynamic-update-slice, f32[256]{0:T(256)S(1)} %dynamic-update-slice.1), channel_id=2, replica_groups=mesh['tm'=16,'feat'=2] {'tm'}, use_global_device_ids=true, to_apply=%add.101 | all-reduce | flops 512 | bytes 4096
  99.1 3.1 gather_fusion
  162.0 36.5 %all-reduce.106 = (f32[256]{0:T(256)S(1)}, f32[256]{0:T(256)S(1)}, f32[256]{0:T(256)S(1)}) all-reduce(f32[256]{0:T(256)S(1)} %dynamic-update-slice.2, f32[256]{0:T(256)S(1)} %dynamic-update-slice.3, f32[256]{0:T(256)S(1)} %dynamic-update-slice.4), channel_id=4, replica_groups=mesh['tm'=16,'feat'=2] {'tm'}, use_global_device_ids=true, to_apply=%add.103 | all-reduce | flops 768 | bytes 6144
  213.9 123.0 %while.48 = (s32[]{:T(128)}, f32[32,8,2,32,256]{4,3,2,1,0:T(8,128)}, s32[32,8,1536]{2,1,0:T(8,128)}, bf16[2,32,1536]{2,1,0:T(8,128)(2,1)S(1)}, s32[]{:T(128)}) while((s32[]{:T(128)}, f32[32,8,2,32,256]{4,3,2,1,0:T(8,128)}, s32[32,8,1536]{2,1,0:T(8,128)}, bf16[2,32,1536]{2,1,0:T(8,128)(2,1)S(1)}, s32[]{:T(128)}) %tuple.152), condition=%wide.region_9.11_spmd.clone, body=%wide.region_8.10_spmd.clone.sunk | while | flops 405798912 | bytes 868929 | solution.py:77
  214.7 3.0 fusion.140
  218.5 3.0 fusion.140
  222.4 3.1 fusion.140
  226.2 3.0 fusion.140
  230.1 3.0 fusion.140
  233.9 3.0 fusion.140
  245.4 3.0 fusion.140
  249.2 3.0 fusion.140
  253.1 3.1 fusion.140
  256.9 3.0 fusion.140
  260.8 3.1 fusion.140
  264.6 3.0 fusion.140
  272.3 3.1 fusion.140
  276.2 3.1 fusion.140
  280.0 3.1 fusion.140
  283.9 3.0 fusion.140
  291.6 3.1 fusion.140
  295.4 3.0 fusion.140
  303.1 3.0 fusion.140
  307.0 3.1 fusion.140
  310.8 3.1 fusion.140
  314.7 3.0 fusion.140
  322.3 3.0 fusion.140
  326.2 3.0 fusion.140
  330.0 3.0 fusion.140
  333.9 3.0 fusion.140
  336.9 345.6 %reduce-scatter.2.cloned.1.call-done = f32[16,2,32,256]{3,2,1,0:T(8,128)} async-done(((f32[256,2,32,256]{3,2,1,0:T(8,128)}), f32[16,2,32,256]{3,2,1,0:T(8,128)}) %reduce-scatter.2.cloned.1.call-update) | async-done | bytes 1048592 | tf_op jit(solution)/shard_map/reduce_scatter | solution.py:135
  683.9 18.4 %reduce-window.36 = f32[16,2,32,2,128]{4,2,3,1,0:T(8,128)S(1)} reduce-window(f32[16,2,32,2,128]{4,2,3,1,0:T(8,128)S(1)} %copy_bitcast_fusion.1, f32[]{:T(128)} %constant.100.clone.1), window={size=1x1x1x1x128 pad=0_0x0_0x0_0x0_0x127_0}, to_apply=%region_11.13 | reduce-window | flops 33292288 | bytes 2097156 | tf_op jit(solution)/shard_map/reduce-window.4
  (534 shorter events, 170.1 us)
Async XLA Ops:
  7.2 203.9 %copy-start = (f32[16,1536]{1,0:T(8,128)S(1)}, f32[16,1536]{1,0:T(8,128)}, u32[]{:S(2)}) copy-start(f32[16,1536]{1,0:T(8,128)} %param.13) | copy-start | bytes 294916
  7.2 194.7 %copy-start.1 = (s32[1536]{0:T(1024)S(1)}, s32[1536]{0:T(1024)}, u32[]{:S(2)}) copy-start(s32[1536]{0:T(1024)} %param.16) | copy-start | bytes 18436
  7.2 675.4 %reduce-scatter.2.cloned.1.call-start = ((), (), s32[]{:S(2)}) async-start(), calls=%async_computation.1 | async-start | bytes 17825792 | tf_op jit(solution)/shard_map/reduce_scatter | solution.py:135
Sparse Core Ops, SparseCore 0:
  337.1 345.4 reduce-scatter.1
where the time goes:
time: 727 us; the launch traced here: 713 us
  waiting for transfers between devices  346 us (48%)
  local copies, waits for them, and re-layouts  137 us (19%)
  matrix products  97.3 us (13%)
  blocking collectives  82 us (11%)
  other arithmetic  33.5 us (5%)
  between operations  17 us (2%)
    reduce_scatter x1, waiting for transfers between devices, on_device(): lax.psum_scatter(bin_histogram(bins, pair_all), 'tm', scatter_dimension=0...  346 us
    dot_general x32, matrix products, one_group(): jnp.einsum('gkr,fbr->fgkb', pair_span, onehot, preferred_element_type=jnp...  97.3 us
    unnamed x2, blocking collectives  80 us
    slice x89, local copies, waits for them, and re-layouts, on_device(): lax.associative_scan(log_add_pair, (event_log, event_mass, event_mass), a...  29.6 us
    eq x32, local copies, waits for them, and re-layouts, one_group(): group_codes[:, None, :] == levels[None, :, None]  25.7 us
    pad x57, local copies, waits for them, and re-layouts, on_device(): lax.associative_scan(log_add_pair, (event_log, event_mass, event_mass), a...  23 us
    slice x60, local copies, waits for them, and re-layouts, on_device(): lax.associative_scan(log_add, (margins, unit_mass), reverse=True, axis=1)  22.3 us
    another operation x8, other arithmetic  21.6 us
  transfers between devices with their start and end apart: 1, of which 1 were waited for; matrix products, arithmetic and copies ran while one was open for 0% of the time, Pallas kernels for 0%

commit v1 on v0

v1 whole, which is shorter than its diff:
```python
import functools

import jax
import jax.numpy as jnp
from jax import lax
from jax.experimental import pallas as pl
from jax.experimental.pallas import tpu as pltpu
from jax.sharding import PartitionSpec as P

BINS = 256
HALF = BINS // 2
LANES = 128
log_floor = -1e30
NT = (((1,), (1,)), ((), ()))
f32 = jnp.float32
bf16 = jnp.bfloat16


def ahead(x, step, fill):
    length = x.shape[1]
    pad = jnp.full((x.shape[0], step), fill, x.dtype)
    if step % LANES == 0:
        return jnp.concatenate([x[:, step:], pad], axis=1)
    lane = lax.broadcasted_iota(jnp.int32, x.shape, 1)
    return jnp.where(lane < length - step, pltpu.roll(x, length - step, 1), fill)


def behind(x, step, fill):
    length = x.shape[1]
    pad = jnp.full((x.shape[0], step), fill, x.dtype)
    if step % LANES == 0:
        return jnp.concatenate([pad, x[:, : length - step]], axis=1)
    lane = lax.broadcasted_iota(jnp.int32, x.shape, 1)
    return jnp.where(lane >= step, pltpu.roll(x, step, 1), fill)


def steps(length):
    step = 1
    while step < length:
        yield step
        step *= 2


def log_sum(a, b):
    peak = jnp.maximum(a, b)
    return peak + jnp.log(1.0 + jnp.exp(-jnp.abs(a - b)))


def risk_kernel(margins_ref, tie_ref, local_ref, total_ref):
    peak = margins_ref[...]
    length = peak.shape[1]
    mass = jnp.ones_like(peak)
    for step in steps(length):
        far_peak = ahead(peak, step, log_floor)
        far_mass = ahead(mass, step, 0.0)
        gap = peak - far_peak
        shrink = jnp.exp(-jnp.abs(gap))
        mass = jnp.where(gap >= 0, mass + far_mass * shrink, mass * shrink + far_mass)
        peak = jnp.maximum(peak, far_peak)
    risk = peak + jnp.log(mass)
    total_ref[...] = jnp.broadcast_to(risk[:, 0:1], (risk.shape[0], LANES))
    tie = jnp.broadcast_to(tie_ref[...], risk.shape)
    lane = lax.broadcasted_iota(jnp.int32, risk.shape, 1)
    opens = (lane == 0) | (tie != pltpu.roll(tie, 1, 1))
    filled = jnp.where(opens, risk, -log_floor)
    for step in steps(length):
        filled = jnp.minimum(filled, behind(filled, step, -log_floor))
    local_ref[...] = filled


def carried(place, parts, later, endpoints):
    count = parts.shape[0] // endpoints
    held = [parts[k * endpoints : (k + 1) * endpoints] for k in range(count)]
    held = [jnp.where((place < k) if later else (place > k), h, log_floor) for k, h in enumerate(held)]
    peak = functools.reduce(jnp.maximum, held)
    mass = functools.reduce(jnp.add, [jnp.exp(h - peak) for h in held])
    return jnp.where(peak > 0.5 * log_floor, peak + jnp.log(mass), log_floor)


def event_kernel(place_ref, local_ref, parts_ref, events_ref, tie_ref, first_ref, second_ref, total_ref):
    local = local_ref[...]
    endpoints, length = local.shape
    carry = carried(place_ref[0], parts_ref[...], True, endpoints)
    risk = log_sum(local, carry[:, 0:1])
    happened = events_ref[...] == 1
    peak = jnp.where(happened, -risk, log_floor)
    first = happened.astype(f32)
    second = first
    for step in steps(length):
        far_peak = behind(peak, step, log_floor)
        far_first = behind(first, step, 0.0)
        far_second = behind(second, step, 0.0)
        gap = peak - far_peak
        shrink = jnp.exp(-jnp.abs(gap))
        near = gap >= 0
        square = shrink * shrink
        first = jnp.where(near, first + far_first * shrink, first * shrink + far_first)
        second = jnp.where(near, second + far_second * square, second * square + far_second)
        peak = jnp.maximum(peak, far_peak)
    some = first > 0
    first_log = jnp.where(some, peak + jnp.log(first), log_floor)
    second_log = jnp.where(some, 2.0 * peak + jnp.log(second), log_floor)
    end = length - 1
    total_ref[0:endpoints] = jnp.broadcast_to(first_log[:, end:], (endpoints, LANES))
    total_ref[endpoints:] = jnp.broadcast_to(second_log[:, end:], (endpoints, LANES))
    tie = jnp.broadcast_to(tie_ref[...], local.shape)
    lane = lax.broadcasted_iota(jnp.int32, local.shape, 1)
    closes = (lane == end) | (tie != pltpu.roll(tie, length - 1, 1))
    first_fill = jnp.where(closes, first_log, -log_floor)
    second_fill = jnp.where(closes, second_log, -log_floor)
    for step in steps(length):
        first_fill = jnp.minimum(first_fill, ahead(first_fill, step, -log_floor))
        second_fill = jnp.minimum(second_fill, ahead(second_fill, step, -log_floor))
    first_ref[...] = first_fill
    second_ref[...] = second_fill


def grad_kernel(place_ref, margins_ref, events_ref, node_ref, first_ref, second_ref, parts_ref, grad_ref, hess_ref, pair_ref):
    margins = margins_ref[...]
    endpoints = margins.shape[0]
    carry = carried(place_ref[0], parts_ref[...], False, 2 * endpoints)
    first_log = log_sum(first_ref[...], carry[0:endpoints, 0:1])
    second_log = log_sum(second_ref[...], carry[endpoints:, 0:1])
    first = jnp.exp(margins + first_log)
    second = jnp.exp(2.0 * margins + second_log)
    grad = first - (events_ref[...] == 1).astype(f32)
    hess = first - second
    grad_ref[...] = grad.astype(bf16)
    hess_ref[...] = hess.astype(bf16)
    chosen = jnp.broadcast_to(node_ref[...], margins.shape) == 1
    pair_ref[0:endpoints] = jnp.where(chosen, grad, 0.0).astype(bf16)
    pair_ref[endpoints:] = jnp.where(chosen, hess, 0.0).astype(bf16)


def hist_kernel(blocks, feature_count, order_ref, bins_ref, pairs_ref, gain_ref, sums_ref):
    block = pl.program_id(0)
    channels = pairs_ref.shape[1]
    length = pairs_ref.shape[2]

    @pl.when(block == 0)
    def _():
        sums_ref[...] = jnp.zeros_like(sums_ref)

    level = lax.broadcasted_iota(jnp.int32, (HALF, length), 0).astype(bf16)
    pairs = pairs_ref[0]
    nothing = jnp.zeros_like(pairs)
    codes = bins_ref[0]
    upper = codes >= bf16(HALF)
    low = jnp.where(upper, codes - bf16(HALF), codes)
    high = jnp.where(upper, bf16(1), bf16(0))
    for f in range(feature_count):
        up = jnp.broadcast_to(high[f : f + 1], pairs.shape) == bf16(1)
        left = jnp.concatenate([jnp.where(up, nothing, pairs), jnp.where(up, pairs, nothing)], axis=0)
        reach = jnp.where(level >= low[f : f + 1], bf16(1), bf16(0))
        sums_ref[f] += lax.dot_general(left, reach, NT, preferred_element_type=f32)

    @pl.when(block == blocks - 1)
    def _():
        quarter = channels // 4

        def split(x):
            grad = jnp.concatenate([x[0:quarter], x[2 * quarter : 3 * quarter]], axis=0)
            hess = jnp.concatenate([x[quarter : 2 * quarter], x[3 * quarter :]], axis=0)
            return grad, hess

        def part(x):
            grad, hess = split(x)
            return grad * grad / (hess + 1.0)

        for f in range(feature_count):
            lower = sums_ref[f, 0:channels]
            under = lower[:, HALF - 1 :]
            uppers = sums_ref[f, channels:] + under
            whole = uppers[:, HALF - 1 :]
            whole_part = part(whole)
            for side, left in enumerate((lower, uppers)):
                value = part(left) + part(whole - left) - whole_part
                gain_ref[f : f + 1, side * HALF : (side + 1) * HALF] = jnp.mean(value, axis=0, keepdims=True)


def call(kernel, out_shape, name, **kw):
    return pl.pallas_call(kernel, out_shape=out_shape, name=name, **kw)


def shape(*dims, dtype=f32):
    return jax.ShapeDtypeStruct(dims, dtype)


VMEM = pl.BlockSpec(memory_space=pltpu.VMEM)
SMEM = pl.BlockSpec(memory_space=pltpu.SMEM)


def gather_rows(mine, devices):
    place = lax.axis_index("tm")
    if devices % 4 or devices > 16:
        return lax.all_gather(mine, "tm"), jnp.arange(devices, dtype=jnp.int32)
    planes = devices // 4
    column = [mine]
    origin = [place]
    for d in range(1, planes):
        ring = [(i, (i + 4 * d) % devices) for i in range(devices)]
        column.append(lax.ppermute(mine, "tm", ring))
        origin.append((place + devices - 4 * d) % devices)
    column = jnp.stack(column)
    origin = jnp.stack(origin)
    every = [column]
    order = [origin]
    for d in range(1, 4):
        every.append(lax.ppermute(column, "tm", [(i, i ^ d) for i in range(devices)]))
        order.append(origin ^ d)
    return jnp.concatenate(every, axis=0), jnp.concatenate(order)


def on_device(devices, margins, events, tie_group, in_node, bins):
    endpoints, length = margins.shape
    place = lax.axis_index("tm")
    here = place[None].astype(jnp.int32)
    tie = tie_group[None]
    mine = bins.shape[0] // devices
    codes = lax.all_to_all(bins.astype(bf16).reshape(devices, mine, length), "tm", 0, 0)

    def exchange(total):
        rows = total.shape[0]
        sent = lax.all_to_all(jnp.broadcast_to(total[None], (devices, rows, LANES)), "tm", 0, 0)
        return sent.reshape(devices * rows, LANES)

    local, total = call(
        risk_kernel, (shape(endpoints, length), shape(endpoints, LANES)), "risk",
        in_specs=[VMEM] * 2, out_specs=(VMEM,) * 2,
    )(margins, tie)
    first, second, total = call(
        event_kernel,
        (shape(endpoints, length), shape(endpoints, length), shape(2 * endpoints, LANES)), "events",
        in_specs=[SMEM] + [VMEM] * 4, out_specs=(VMEM,) * 3,
    )(here, local, exchange(total), events, tie)
    grad, hess, pairs = call(
        grad_kernel,
        (
            shape(endpoints, length, dtype=bf16),
            shape(endpoints, length, dtype=bf16),
            shape(2 * endpoints, length, dtype=bf16),
        ), "grads",
        in_specs=[SMEM] + [VMEM] * 6, out_specs=(VMEM,) * 3,
    )(here, margins, events, in_node[None], first, second, exchange(total))

    rows, order = gather_rows(pairs, devices)
    other = lax.ppermute(rows, "feat", [(0, 1), (1, 0)])
    rows = jnp.concatenate([rows, other], axis=1)

    gain = call(
        functools.partial(hist_kernel, devices, mine),
        shape(mine, BINS), "hist",
        grid_spec=pltpu.PrefetchScalarGridSpec(
            num_scalar_prefetch=1,
            grid=(devices,),
            in_specs=[
                pl.BlockSpec((1, mine, length), lambda i, order: (order[i], 0, 0)),
                pl.BlockSpec((1, 4 * endpoints, length), lambda i, order: (i, 0, 0)),
            ],
            out_specs=pl.BlockSpec((mine, BINS), lambda i, order: (0, 0)),
            scratch_shapes=[pltpu.VMEM((mine, 8 * endpoints, HALF), f32)],
        ),
        compiler_params=pltpu.CompilerParams(dimension_semantics=("arbitrary",), vmem_limit_bytes=48 << 20),
    )(order, codes, rows)
    return (grad, hess, gain[None])


def solution(mesh):
    in_specs = (P("feat", "tm"), P("feat", "tm"), P("tm"), P("tm"), P("feat", "tm"))
    out_specs = (P("feat", "tm"), P("feat", "tm"), P("feat", "tm", None))
    return jax.shard_map(
        functools.partial(on_device, mesh.shape["tm"]),
        mesh=mesh, in_specs=in_specs, out_specs=out_specs, check_vma=False,
    )
```

time: 727 us -> 129 us (0.18); the launches traced: 713 us -> 129 us
  waiting for transfers between devices: 346 us -> 49.6 us
  local copies, waits for them, and re-layouts: 137 us -> 7.33 us
  matrix products: 97.3 us -> 0 us
  blocking collectives: 82 us -> 0 us
  Pallas kernels: 0 us -> 40.9 us
  other arithmetic: 33.5 us -> 4.28 us
  starting transfers between devices: 0.04 us -> 25.8 us
  between operations: 17 us -> 0.8 us
    reduce_scatter x1 -> x0, waiting for transfers between devices: 346 us -> none  [on_device(): lax.psum_scatter(bin_histogram(bins, pair_all), 'tm', scatter_dimension=0...]
    dot_general x32 -> x0, matrix products: 97.3 us -> none  [one_group(): jnp.einsum('gkr,fbr->fgkb', pair_span, onehot, preferred_element_type=jnp...]
    unnamed x2 -> x0, blocking collectives: 80 us -> none
    slice x152 -> x0, local copies, waits for them, and re-layouts: 52.5 us -> none  [the longest x89 29.6 us: on_device(): lax.associative_scan(log_add_pair, (event_log, event_mass, event_mass), a...]
    pallas_call x0 -> x4, Pallas kernels: none -> 40.9 us  [the longest x1 32.7 us: on_device(): call(functools.partial(hist_kernel, devices, mine), shape(mine, BINS), 'h...]
    pad x95 -> x0, local copies, waits for them, and re-layouts: 38.3 us -> none  [the longest x57 23 us: on_device(): lax.associative_scan(log_add_pair, (event_log, event_mass, event_mass), a...]
    all_to_all x0 -> x3, waiting for transfers between devices: none -> 33.4 us  [the longest x1 17.8 us: on_device(): lax.all_to_all(bins.astype(bf16).reshape(devices, mine, length), 'tm', 0, 0)]
    eq x32 -> x0, local copies, waits for them, and re-layouts: 25.7 us -> none  [one_group(): group_codes[:, None, :] == levels[None, :, None]]
  transfers between devices with their start and end apart: 1 -> 10, of which waited for: 1 -> 7; matrix products, arithmetic and copies ran while one was open for 0% -> 4% of each run, Pallas kernels for 0% -> 0%
where the time goes in v1:
time: 129 us
  waiting for transfers between devices  49.6 us (38%)
  Pallas kernels  40.9 us (32%)
  starting transfers between devices  25.8 us (20%)
  local copies, waits for them, and re-layouts  7.33 us (6%)
  other arithmetic  4.28 us (3%)
    pallas_call x1, Pallas kernels, on_device(): call(functools.partial(hist_kernel, devices, mine), shape(mine, BINS), 'h...  32.7 us
    all_to_all x1, waiting for transfers between devices, on_device(): lax.all_to_all(bins.astype(bf16).reshape(devices, mine, length), 'tm', 0, 0)  17.8 us
    all_to_all x2, waiting for transfers between devices, exchange(): lax.all_to_all(jnp.broadcast_to(total[None], (devices, rows, LANES)), 'tm...  15.7 us
    ppermute x3, waiting for transfers between devices, gather_rows(): lax.ppermute(column, 'tm', [(i, i ^ d) for i in range(devices)])  12.2 us
    all_to_all x2, starting transfers between devices, exchange(): lax.all_to_all(jnp.broadcast_to(total[None], (devices, rows, LANES)), 'tm...  11.8 us
    all_to_all x1, starting transfers between devices, on_device(): lax.all_to_all(bins.astype(bf16).reshape(devices, mine, length), 'tm', 0, 0)  6.35 us
    ppermute x3, starting transfers between devices, gather_rows(): column.append(lax.ppermute(mine, 'tm', ring))  4.01 us
    ppermute x3, waiting for transfers between devices, gather_rows(): column.append(lax.ppermute(mine, 'tm', ring))  3.92 us
  transfers between devices with their start and end apart: 10, of which 7 were waited for; matrix products, arithmetic and copies ran while one was open for 4% of the time, Pallas kernels for 0%

profile of v1, /device:TPU:0, one launch (start us, length us, event | category | flops | bytes accessed | tf_op | source)
XLA Modules:
  0.0 128.7 jit_solution(14789547967022233892)
XLA Ops:
  0.6 1.3 %broadcast_in_dim.26.tie_ref = s32[1,1536]{1,0:T(1,128)} reshape(s32[1536]{0:T(1024)} %param.7) | data formatting | bytes 12288 | tf_op jit(solution)/shard_map/broadcast_in_dim | solution.py:218
  1.9 2.8 %risk.1 = (f32[16,1536]{1,0:T(8,128)}, f32[16,128]{1,0:T(8,128)}) custom-call(f32[16,1536]{1,0:T(8,128)} %margins_ref.3, s32[1,1536]{1,0:T(1,128)} %broadcast_in_dim.26.tie_ref), custom_call_target="tpu_custom_call" | custom-call | tf_op jit(solution)/shard_map/risk/pallas_call | solution.py:227
  4.7 1.4 %broadcast_in_dim.27 = f32[16,16,128]{2,1,0:T(8,128)} broadcast(f32[16,128]{1,0:T(8,128)} %get-tuple-element.12), dimensions={1,2} | broadcast | bytes 139264 | tf_op jit(solution)/shard_map/broadcast_in_dim | solution.py:224
  6.1 8.3 %all-to-all-start = ((f32[16,16,128]{2,1,0:T(8,128)}), f32[16,16,128]{2,1,0:T(8,128)S(1)}, u32[]{:S(2)}, u32[]{:S(2)}) async-start(f32[16,16,128]{2,1,0:T(8,128)} %broadcast_in_dim.27), calls=%async_computation | async-start | bytes 262144 | tf_op jit(solution)/shard_map/all_to_all | solution.py:224
  14.4 7.8 %all-to-all-done = f32[16,16,128]{2,1,0:T(8,128)S(1)} async-done(((f32[16,16,128]{2,1,0:T(8,128)}), f32[16,16,128]{2,1,0:T(8,128)S(1)}, u32[]{:S(2)}, u32[]{:S(2)}) %all-to-all-start) | async-done | bytes 131104 | tf_op jit(solution)/shard_map/all_to_all | solution.py:224
  22.2 0.6 copy-done.3
  22.9 3.2 %events.1 = (f32[16,1536]{1,0:T(8,128)}, f32[16,1536]{1,0:T(8,128)}, f32[32,128]{1,0:T(8,128)}) custom-call(s32[1]{0:T(128)} %bitcast.place_ref, f32[16,1536]{1,0:T(8,128)} %get-tuple-element.11.local_ref, f32[256,128]{1,0:T(8,128)} %bitcast.17, s32[16,1536]{1,0:T(8,128)} %events_ref.3, s32[1,1536]{1,0:T(1,128)} %broadcast_in_dim.26.tie_ref), custom_call_target="tpu_custom_call" | custom-call | tf_op jit(solution)/shard_map/events/pallas_call | solution.py:231
  26.1 1.4 %broadcast_in_dim.28 = f32[16,32,128]{2,1,0:T(8,128)} broadcast(f32[32,128]{1,0:T(8,128)} %get-tuple-element.15), dimensions={1,2} | broadcast | bytes 278528 | tf_op jit(solution)/shard_map/broadcast_in_dim | solution.py:224
  27.6 3.5 %all-to-all-start.1 = ((f32[16,32,128]{2,1,0:T(8,128)}), f32[16,32,128]{2,1,0:T(8,128)S(1)}, u32[]{:S(2)}, u32[]{:S(2)}) async-start(f32[16,32,128]{2,1,0:T(8,128)} %broadcast_in_dim.28), calls=%async_computation.1 | async-start | bytes 524288 | tf_op jit(solution)/shard_map/all_to_all | solution.py:224
  31.1 0.6 broadcast_in_dim.25.node_ref
  31.7 7.9 %all-to-all-done.1 = f32[16,32,128]{2,1,0:T(8,128)S(1)} async-done(((f32[16,32,128]{2,1,0:T(8,128)}), f32[16,32,128]{2,1,0:T(8,128)S(1)}, u32[]{:S(2)}, u32[]{:S(2)}) %all-to-all-start.1) | async-done | bytes 262176 | tf_op jit(solution)/shard_map/all_to_all | solution.py:224
  39.6 0.7 copy-done.2
  40.3 2.1 %grads.1 = (bf16[16,1536]{1,0:T(8,128)(2,1)}, bf16[16,1536]{1,0:T(8,128)(2,1)}, bf16[32,1536]{1,0:T(8,128)(2,1)}) custom-call(s32[1]{0:T(128)} %bitcast.place_ref, f32[16,1536]{1,0:T(8,128)} %margins_ref.3, s32[16,1536]{1,0:T(8,128)} %events_ref.3, s32[1,1536]{1,0:T(1,128)} %broadcast_in_dim.25.node_ref, f32[16,1536]{1,0:T(8,128)} %get-tuple-element.13.first_ref, ...), custom_call_target="tpu_custom_call" | custom-call | tf_op jit(solution)/shard_map/grads/pallas_call | solution.py:236
  42.3 1.1 collective-permute-start
  43.4 1.4 %collective-permute-start.1 = (bf16[32,1536]{1,0:T(8,128)(2,1)}, bf16[32,1536]{1,0:T(8,128)(2,1)S(1)}, u32[]{:S(2)}, u32[]{:S(2)}) collective-permute-start(bf16[32,1536]{1,0:T(8,128)(2,1)} %get-tuple-element.18), channel_id=1, source_target_pairs={{0,16},{2,18},{4,20},{6,22},{8,24},{10,26},{12,28},{14,30},{16,0},... | collective-permute-start | bytes 294920 | tf_op jit(solution)/shard_map/ppermute | solution.py:202
  44.9 1.5 %collective-permute-start.2 = (bf16[32,1536]{1,0:T(8,128)(2,1)}, bf16[32,1536]{1,0:T(8,128)(2,1)S(1)}, u32[]{:S(2)}, u32[]{:S(2)}) collective-permute-start(bf16[32,1536]{1,0:T(8,128)(2,1)} %get-tuple-element.18), channel_id=1, source_target_pairs={{0,24},{2,26},{4,28},{6,30},{8,0},{10,2},{12,4},{14,6},{16,8},{18,... | collective-permute-start | bytes 294920 | tf_op jit(solution)/shard_map/ppermute | solution.py:202
  46.4 0.9 constant_dynamic-update-slice_fusion.6
  47.3 1.8 %collective-permute-done = bf16[32,1536]{1,0:T(8,128)(2,1)S(1)} collective-permute-done((bf16[32,1536]{1,0:T(8,128)(2,1)}, bf16[32,1536]{1,0:T(8,128)(2,1)S(1)}, u32[]{:S(2)}, u32[]{:S(2)}) %collective-permute-start) | collective-permute-done | bytes 98336 | tf_op jit(solution)/shard_map/ppermute | solution.py:202
  49.1 2.1 %collective-permute-done.1 = bf16[32,1536]{1,0:T(8,128)(2,1)S(1)} collective-permute-done((bf16[32,1536]{1,0:T(8,128)(2,1)}, bf16[32,1536]{1,0:T(8,128)(2,1)S(1)}, u32[]{:S(2)}, u32[]{:S(2)}) %collective-permute-start.1) | collective-permute-done | bytes 98336 | tf_op jit(solution)/shard_map/ppermute | solution.py:202
  51.2 0.9 pad_maximum_fusion.1
  52.2 1.0 collective-permute-start.3
  53.1 1.0 collective-permute-start.4
  54.2 1.6 %collective-permute-start.5 = (bf16[4,32,1536]{2,1,0:T(8,128)(2,1)S(1)}, bf16[4,32,1536]{2,1,0:T(8,128)(2,1)S(1)}, u32[]{:S(2)}, u32[]{:S(2)}) collective-permute-start(bf16[4,32,1536]{2,1,0:T(8,128)(2,1)S(1)} %pad_maximum_fusion.1), channel_id=1, source_target_pairs={{0,6},{2,4},{4,2},{6,0},{8,14},{10,12},{12,10},{14,8},{16,22},{18,... | collective-permute-start | bytes 1179656 | tf_op jit(solution)/shard_map/ppermute | solution.py:209
  55.8 7.4 %collective-permute-done.3 = bf16[4,32,1536]{2,1,0:T(8,128)(2,1)S(1)} collective-permute-done((bf16[4,32,1536]{2,1,0:T(8,128)(2,1)S(1)}, bf16[4,32,1536]{2,1,0:T(8,128)(2,1)S(1)}, u32[]{:S(2)}, u32[]{:S(2)}) %collective-permute-start.3) | collective-permute-done | bytes 393248 | tf_op jit(solution)/shard_map/ppermute | solution.py:209
  63.1 4.9 %collective-permute-done.4 = bf16[4,32,1536]{2,1,0:T(8,128)(2,1)S(1)} collective-permute-done((bf16[4,32,1536]{2,1,0:T(8,128)(2,1)S(1)}, bf16[4,32,1536]{2,1,0:T(8,128)(2,1)S(1)}, u32[]{:S(2)}, u32[]{:S(2)}) %collective-permute-start.4) | collective-permute-done | bytes 393248 | tf_op jit(solution)/shard_map/ppermute | solution.py:209
  68.2 1.2 convert_element_type.3
  69.4 0.2 copy-done
  69.5 6.4 %all-to-all-start.2 = ((bf16[16,16,1536]{2,1,0:T(8,128)(2,1)}), bf16[16,16,1536]{2,1,0:T(8,128)(2,1)}, u32[]{:S(2)}, u32[]{:S(2)}) async-start(bf16[16,16,1536]{2,1,0:T(8,128)(2,1)} %bitcast.6), calls=%async_computation.2 | async-start | bytes 1572864 | tf_op jit(solution)/shard_map/all_to_all | solution.py:220
  75.9 0.1 broadcast_xor_fusion
  76.1 2.1 %pad_maximum_fusion.pairs_ref = bf16[16,64,1536]{2,1,0:T(8,128)(2,1)S(1)} fusion(bf16[16,32,1536]{2,1,0:T(8,128)(2,1)} %collective-permute-done.6, bf16[16,32,1536]{2,1,0:T(8,128)(2,1)} %copy-done), kind=kLoop, calls=%fused_computation | loop fusion | flops 6291456 | bytes 6291456 | tf_op jit(solution)/shard_map/concatenate | solution.py:248
  78.2 17.8 %all-to-all-done.2.bins_ref = bf16[16,16,1536]{2,1,0:T(8,128)(2,1)} async-done(((bf16[16,16,1536]{2,1,0:T(8,128)(2,1)}), bf16[16,16,1536]{2,1,0:T(8,128)(2,1)}, u32[]{:S(2)}, u32[]{:S(2)}) %all-to-all-start.2) | async-done | bytes 786464 | tf_op jit(solution)/shard_map/all_to_all | solution.py:220
  96.0 32.7 %hist.1 = f32[16,256]{1,0:T(8,128)} custom-call(s32[16]{0:T(128)S(1)} %concatenate.11.order_ref, bf16[16,16,1536]{2,1,0:T(8,128)(2,1)} %all-to-all-done.2.bins_ref, bf16[16,64,1536]{2,1,0:T(8,128)(2,1)S(1)} %pad_maximum_fusion.pairs_ref), custom_call_target="tpu_custom_call" | custom-call | tf_op jit(solution)/shard_map/hist/pallas_call | solution.py:250
  (19 shorter events, 0.3 us)
Async XLA Ops:
  0.6 30.5 %copy-start.4 = (s32[1536]{0:T(1024)S(1)}, s32[1536]{0:T(1024)}, u32[]{:S(2)}) copy-start(s32[1536]{0:T(1024)} %param.8) | copy-start | bytes 18436
  6.1 16.1 %all-to-all-start = ((f32[16,16,128]{2,1,0:T(8,128)}), f32[16,16,128]{2,1,0:T(8,128)S(1)}, u32[]{:S(2)}, u32[]{:S(2)}) async-start(f32[16,16,128]{2,1,0:T(8,128)} %broadcast_in_dim.27), calls=%async_computation | async-start | bytes 262144 | tf_op jit(solution)/shard_map/all_to_all | solution.py:224
  22.2 0.6 copy-start.3
  27.6 12.0 %all-to-all-start.1 = ((f32[16,32,128]{2,1,0:T(8,128)}), f32[16,32,128]{2,1,0:T(8,128)S(1)}, u32[]{:S(2)}, u32[]{:S(2)}) async-start(f32[16,32,128]{2,1,0:T(8,128)} %broadcast_in_dim.28), calls=%async_computation.1 | async-start | bytes 524288 | tf_op jit(solution)/shard_map/all_to_all | solution.py:224
  39.6 0.7 copy-start.2
  42.3 6.8 %collective-permute-start = (bf16[32,1536]{1,0:T(8,128)(2,1)}, bf16[32,1536]{1,0:T(8,128)(2,1)S(1)}, u32[]{:S(2)}, u32[]{:S(2)}) collective-permute-start(bf16[32,1536]{1,0:T(8,128)(2,1)} %get-tuple-element.18), channel_id=1, source_target_pairs={{0,8},{2,10},{4,12},{6,14},{8,16},{10,18},{12,20},{14,22},{16,24},... | collective-permute-start | bytes 294920 | tf_op jit(solution)/shard_map/ppermute | solution.py:202
  43.4 7.8 %collective-permute-start.1 = (bf16[32,1536]{1,0:T(8,128)(2,1)}, bf16[32,1536]{1,0:T(8,128)(2,1)S(1)}, u32[]{:S(2)}, u32[]{:S(2)}) collective-permute-start(bf16[32,1536]{1,0:T(8,128)(2,1)} %get-tuple-element.18), channel_id=1, source_target_pairs={{0,16},{2,18},{4,20},{6,22},{8,24},{10,26},{12,28},{14,30},{16,0},... | collective-permute-start | bytes 294920 | tf_op jit(solution)/shard_map/ppermute | solution.py:202
  44.9 6.3 %collective-permute-start.2 = (bf16[32,1536]{1,0:T(8,128)(2,1)}, bf16[32,1536]{1,0:T(8,128)(2,1)S(1)}, u32[]{:S(2)}, u32[]{:S(2)}) collective-permute-start(bf16[32,1536]{1,0:T(8,128)(2,1)} %get-tuple-element.18), channel_id=1, source_target_pairs={{0,24},{2,26},{4,28},{6,30},{8,0},{10,2},{12,4},{14,6},{16,8},{18,... | collective-permute-start | bytes 294920 | tf_op jit(solution)/shard_map/ppermute | solution.py:202
  52.2 16.0 %copy-start.1 = (s32[256,1536]{1,0:T(8,128)S(1)}, s32[256,1536]{1,0:T(8,128)}, u32[]{:S(2)}) copy-start(s32[256,1536]{1,0:T(8,128)} %param.9) | copy-start | bytes 4718596
  52.2 11.0 %collective-permute-start.3 = (bf16[4,32,1536]{2,1,0:T(8,128)(2,1)S(1)}, bf16[4,32,1536]{2,1,0:T(8,128)(2,1)S(1)}, u32[]{:S(2)}, u32[]{:S(2)}) collective-permute-start(bf16[4,32,1536]{2,1,0:T(8,128)(2,1)S(1)} %pad_maximum_fusion.1), channel_id=1, source_target_pairs={{0,2},{2,0},{4,6},{6,4},{8,10},{10,8},{12,14},{14,12},{16,18},{18,... | collective-permute-start | bytes 1179656 | tf_op jit(solution)/shard_map/ppermute | solution.py:209
  53.1 14.9 %collective-permute-start.4 = (bf16[4,32,1536]{2,1,0:T(8,128)(2,1)S(1)}, bf16[4,32,1536]{2,1,0:T(8,128)(2,1)S(1)}, u32[]{:S(2)}, u32[]{:S(2)}) collective-permute-start(bf16[4,32,1536]{2,1,0:T(8,128)(2,1)S(1)} %pad_maximum_fusion.1), channel_id=1, source_target_pairs={{0,4},{2,6},{4,0},{6,2},{8,12},{10,14},{12,8},{14,10},{16,20},{18,... | collective-permute-start | bytes 1179656 | tf_op jit(solution)/shard_map/ppermute | solution.py:209
  54.2 13.9 %collective-permute-start.5 = (bf16[4,32,1536]{2,1,0:T(8,128)(2,1)S(1)}, bf16[4,32,1536]{2,1,0:T(8,128)(2,1)S(1)}, u32[]{:S(2)}, u32[]{:S(2)}) collective-permute-start(bf16[4,32,1536]{2,1,0:T(8,128)(2,1)S(1)} %pad_maximum_fusion.1), channel_id=1, source_target_pairs={{0,6},{2,4},{4,2},{6,0},{8,14},{10,12},{12,10},{14,8},{16,22},{18,... | collective-permute-start | bytes 1179656 | tf_op jit(solution)/shard_map/ppermute | solution.py:209
  68.1 1.4 %copy-start = (bf16[16,32,1536]{2,1,0:T(8,128)(2,1)}, bf16[16,32,1536]{2,1,0:T(8,128)(2,1)S(1)}, u32[]{:S(2)}) copy-start(bf16[16,32,1536]{2,1,0:T(8,128)(2,1)S(1)} %constant_dynamic-update-slice_fusion) | copy-start | bytes 4718596
  68.1 8.0 %collective-permute-start.6 = (bf16[16,32,1536]{2,1,0:T(8,128)(2,1)S(1)}, bf16[16,32,1536]{2,1,0:T(8,128)(2,1)}, u32[]{:S(2)}, u32[]{:S(2)}) collective-permute-start(bf16[16,32,1536]{2,1,0:T(8,128)(2,1)S(1)} %constant_dynamic-update-slice_fusion), channel_id=1, source_target_pairs={{0,1},{1,0},{2,3},{3,2},{4,5},{5,4},{6,7},{7,6},{8,9},{9,8},{10,11... | collective-permute-start | bytes 4718600 | tf_op jit(solution)/shard_map/ppermute | solution.py:247
  69.5 26.4 %all-to-all-start.2 = ((bf16[16,16,1536]{2,1,0:T(8,128)(2,1)}), bf16[16,16,1536]{2,1,0:T(8,128)(2,1)}, u32[]{:S(2)}, u32[]{:S(2)}) async-start(bf16[16,16,1536]{2,1,0:T(8,128)(2,1)} %bitcast.6), calls=%async_computation.2 | async-start | bytes 1572864 | tf_op jit(solution)/shard_map/all_to_all | solution.py:220

commit v2 on v1

--- a/solution.py
+++ b/solution.py
@@ -132,19 +132,10 @@
     pair_ref[endpoints:] = jnp.where(chosen, hess, 0.0).astype(bf16)
 
 
-def hist_kernel(blocks, feature_count, order_ref, bins_ref, pairs_ref, gain_ref, sums_ref):
-    block = pl.program_id(0)
-    channels = pairs_ref.shape[1]
-    length = pairs_ref.shape[2]
-
-    @pl.when(block == 0)
-    def _():
-        sums_ref[...] = jnp.zeros_like(sums_ref)
-
+def add_block(codes, pairs, sums_ref, feature_count):
+    length = pairs.shape[1]
     level = lax.broadcasted_iota(jnp.int32, (HALF, length), 0).astype(bf16)
-    pairs = pairs_ref[0]
     nothing = jnp.zeros_like(pairs)
-    codes = bins_ref[0]
     upper = codes >= bf16(HALF)
     low = jnp.where(upper, codes - bf16(HALF), codes)
     high = jnp.where(upper, bf16(1), bf16(0))
@@ -154,28 +145,77 @@
         reach = jnp.where(level >= low[f : f + 1], bf16(1), bf16(0))
         sums_ref[f] += lax.dot_general(left, reach, NT, preferred_element_type=f32)
 
-    @pl.when(block == blocks - 1)
+
+def write_gain(sums_ref, gain_ref, feature_count, channels):
+    quarter = channels // 4
+
+    def part(x):
+        grad = jnp.concatenate([x[0:quarter], x[2 * quarter : 3 * quarter]], axis=0)
+        hess = jnp.concatenate([x[quarter : 2 * quarter], x[3 * quarter :]], axis=0)
+        return grad * grad / (hess + 1.0)
+
+    for f in range(feature_count):
+        lower = sums_ref[f, 0:channels]
+        under = lower[:, HALF - 1 :]
+        uppers = sums_ref[f, channels:] + under
+        whole = uppers[:, HALF - 1 :]
+        whole_part = part(whole)
+        for side, left in enumerate((lower, uppers)):
+            value = part(left) + part(whole - left) - whole_part
+            gain_ref[f : f + 1, side * HALF : (side + 1) * HALF] = jnp.mean(value, axis=0, keepdims=True)
+
+
+def hist_kernel(blocks, feature_count, first, last, *refs):
+    if first:
+        codes_ref, mine_ref, other_ref, *outs = refs
+    else:
+        codes_ref, mine_ref, other_ref, before_ref, *outs = refs
+    sums_ref = outs[-1]
+    block = pl.program_id(0)
+
+    @pl.when(block == 0)
     def _():
-        quarter = channels // 4
-
-        def split(x):
-            grad = jnp.concatenate([x[0:quarter], x[2 * quarter : 3 * quarter]], axis=0)
-            hess = jnp.concatenate([x[quarter : 2 * quarter], x[3 * quarter :]], axis=0)
-            return grad, hess
-
-        def part(x):
-            grad, hess = split(x)
-            return grad * grad / (hess + 1.0)
-
-        for f in range(feature_count):
-            lower = sums_ref[f, 0:channels]
-            under = lower[:, HALF - 1 :]
-            uppers = sums_ref[f, channels:] + under
-            whole = uppers[:, HALF - 1 :]
-            whole_part = part(whole)
-            for side, left in enumerate((lower, uppers)):
-                value = part(left) + part(whole - left) - whole_part
-                gain_ref[f : f + 1, side * HALF : (side + 1) * HALF] = jnp.mean(value, axis=0, keepdims=True)
+        sums_ref[...] = jnp.zeros_like(sums_ref) if first else before_ref[...]
+
+    pairs = jnp.concatenate([mine_ref[0], other_ref[0]], axis=0)
+    add_block(codes_ref[0], pairs, sums_ref, feature_count)
+    if last:
+
+        @pl.when(block == blocks - 1)
+        def _():
+            write_gain(sums_ref, outs[0], feature_count, pairs.shape[0])
+
+
+def histogram(codes, mine, other, before, last):
+    blocks, feature_count, length = codes.shape
+    half = mine.shape[1]
+    sums = (feature_count, 4 * half, HALF)
+    operands = [codes, mine, other]
+    in_specs = [
+        pl.BlockSpec((1, feature_count, length), lambda i: (i, 0, 0)),
+        pl.BlockSpec((1, half, length), lambda i: (i, 0, 0)),
+        pl.BlockSpec((1, half, length), lambda i: (i, 0, 0)),
+    ]
+    whole = pl.BlockSpec(sums, lambda i: (0, 0, 0))
+    if before is not None:
+        operands.append(before)
+        in_specs.append(whole)
+    return pl.pallas_call(
+        functools.partial(hist_kernel, blocks, feature_count, before is None, last),
+        out_shape=shape(feature_count, BINS) if last else shape(*sums),
+        grid=(blocks,),
+        in_specs=in_specs,
+        out_specs=pl.BlockSpec((feature_count, BINS), lambda i: (0, 0)) if last else whole,
+        scratch_shapes=[pltpu.VMEM(sums, f32)] if last else [],
+        input_output_aliases={3: 0} if before is not None and not last else {},
+        name="hist",
+        compiler_params=pltpu.CompilerParams(dimension_semantics=("arbitrary",), vmem_limit_bytes=32 << 20),
+        cost_estimate=pl.CostEstimate(
+            flops=blocks * feature_count * 2 * (4 * half) * HALF * length * 4,
+            bytes_accessed=blocks * (feature_count + 2 * half) * length * 2,
+            transcendentals=0,
+        ),
+    )(*operands)
 
 
 def call(kernel, out_shape, name, **kw):
@@ -190,25 +230,57 @@
 SMEM = pl.BlockSpec(memory_space=pltpu.SMEM)
 
 
-def gather_rows(mine, devices):
+def ring(devices, d):
+    return [(i, (i + 4 * d) % devices) for i in range(devices)]
+
+
+def flip(devices, d):
+    return [(i, i ^ d) for i in range(devices)]
+
+
+def swap(x):
+    return lax.ppermute(x, "feat", [(0, 1), (1, 0)])
+
+
+def pick(x, index, axis):
+    return lax.dynamic_index_in_dim(x, index, axis, False)
+
+
+def send_codes(codes, devices):
+    planes = devices // 4
     place = lax.axis_index("tm")
-    if devices % 4 or devices > 16:
-        return lax.all_gather(mine, "tm"), jnp.arange(devices, dtype=jnp.int32)
+    plane, column = place // 4, place % 4
+    _, mine, length = codes.reshape(devices, -1, codes.shape[1]).shape
+    codes = codes.reshape(planes, 4, mine, length)
+    held = [pick(codes, plane, 0)]
+    for d in range(1, planes):
+        held.append(lax.ppermute(pick(codes, (plane + d) % planes, 0), "tm", ring(devices, d)))
+    own = pick(held[0], column, 0)[None]
+    near = jnp.stack([pick(h, column, 0) for h in held[1:]])
+    far = [
+        lax.ppermute(jnp.stack([pick(h, column ^ d, 0) for h in held]), "tm", flip(devices, d))
+        for d in range(1, 4)
+    ]
+    return own, near, far
+
+
+def spread(codes, pairs, devices):
+    own, near, far = codes
     planes = devices // 4
-    column = [mine]
-    origin = [place]
-    for d in range(1, planes):
-        ring = [(i, (i + 4 * d) % devices) for i in range(devices)]
-        column.append(lax.ppermute(mine, "tm", ring))
-        origin.append((place + devices - 4 * d) % devices)
-    column = jnp.stack(column)
-    origin = jnp.stack(origin)
-    every = [column]
-    order = [origin]
+    sums = histogram(own, pairs[None], swap(pairs)[None], None, False)
+    column = [lax.ppermute(pairs, "tm", ring(devices, d)) for d in range(1, planes)]
+    column = jnp.stack([pairs] + column)
+    other = swap(column)
+    sums = histogram(near, column[1:], other[1:], sums, False)
     for d in range(1, 4):
-        every.append(lax.ppermute(column, "tm", [(i, i ^ d) for i in range(devices)]))
-        order.append(origin ^ d)
-    return jnp.concatenate(every, axis=0), jnp.concatenate(order)
+        there = lax.ppermute(column, "tm", flip(devices, d))
+        sums = histogram(far[d - 1], there, swap(there), sums, d == 3)
+    return sums
+
+
+def spread_any(codes, pairs):
+    rows = lax.all_gather(pairs, "tm")
+    return histogram(codes, rows, swap(rows), None, True)
 
 
 def on_device(devices, margins, events, tie_group, in_node, bins):
@@ -217,7 +289,11 @@
     here = place[None].astype(jnp.int32)
     tie = tie_group[None]
     mine = bins.shape[0] // devices
-    codes = lax.all_to_all(bins.astype(bf16).reshape(devices, mine, length), "tm", 0, 0)
+    codes = bins.astype(bf16)
+    if devices == 16:
+        codes = send_codes(codes, devices)
+    else:
+        codes = lax.all_to_all(codes.reshape(devices, mine, length), "tm", 0, 0)
 
     def exchange(total):
         rows = total.shape[0]
@@ -243,25 +319,7 @@
         in_specs=[SMEM] + [VMEM] * 6, out_specs=(VMEM,) * 3,
     )(here, margins, events, in_node[None], first, second, exchange(total))
 
-    rows, order = gather_rows(pairs, devices)
-    other = lax.ppermute(rows, "feat", [(0, 1), (1, 0)])
-    rows = jnp.concatenate([rows, other], axis=1)
-
-    gain = call(
-        functools.partial(hist_kernel, devices, mine),
-        shape(mine, BINS), "hist",
-        grid_spec=pltpu.PrefetchScalarGridSpec(
-            num_scalar_prefetch=1,
-            grid=(devices,),
-            in_specs=[
-                pl.BlockSpec((1, mine, length), lambda i, order: (order[i], 0, 0)),
-                pl.BlockSpec((1, 4 * endpoints, length), lambda i, order: (i, 0, 0)),
-            ],
-            out_specs=pl.BlockSpec((mine, BINS), lambda i, order: (0, 0)),
-            scratch_shapes=[pltpu.VMEM((mine, 8 * endpoints, HALF), f32)],
-        ),
-        compiler_params=pltpu.CompilerParams(dimension_semantics=("arbitrary",), vmem_limit_bytes=48 << 20),
-    )(order, codes, rows)
+    gain = spread(codes, pairs, devices) if devices == 16 else spread_any(codes, pairs)
     return (grad, hess, gain[None])
 
 

time: 129 us -> 107 us (0.83)
  waiting for transfers between devices: 49.6 us -> 31.8 us
  local copies, waits for them, and re-layouts: 7.33 us -> 5.48 us
  other arithmetic: 4.28 us -> 2.6 us
  Pallas kernels: 40.9 us -> 39.4 us
    all_to_all x1 -> x0, waiting for transfers between devices: 17.8 us -> none  [on_device(): lax.all_to_all(bins.astype(bf16).reshape(devices, mine, length), 'tm', 0, 0)]
    ppermute x7 -> x17, starting transfers between devices: 7.64 us -> 19.1 us  [the longest x3 7.01 us: send_codes(): lax.ppermute(pick(codes, (plane + d) % planes, 0), 'tm', ring(devices, d))]
    all_to_all x1 -> x0, starting transfers between devices: 6.35 us -> none  [on_device(): lax.all_to_all(bins.astype(bf16).reshape(devices, mine, length), 'tm', 0, 0)]
    all_to_all x2, starting transfers between devices: 11.8 us -> 7.47 us  [exchange(): lax.all_to_all(jnp.broadcast_to(total[None], (devices, rows, LANES)), 'tm...]
    concatenate x1 -> x0, other arithmetic: 2.1 us -> none  [on_device(): rows = jnp.concatenate([rows, other], axis=1)]
    pallas_call x1 -> x5, Pallas kernels: 32.7 us -> 31.3 us  [histogram(): pl.pallas_call(functools.partial(hist_kernel, blocks, feature_count, befo...]
    ppermute x7 -> x17, waiting for transfers between devices: 16.2 us -> 17.1 us  [the longest x3 8.4 us: spread(): there = lax.ppermute(column, 'tm', flip(devices, d))]
  transfers between devices with their start and end apart: 10 -> 19, of which waited for: 7 -> 7; matrix products, arithmetic and copies ran while one was open for 4% -> 3% of each run, Pallas kernels for 0% -> 25%
where the time goes in v2:
time: 107 us
  Pallas kernels  39.4 us (37%)
  waiting for transfers between devices  31.8 us (30%)
  starting transfers between devices  26.5 us (25%)
  local copies, waits for them, and re-layouts  5.48 us (5%)
  other arithmetic  2.6 us (2%)
    pallas_call x5, Pallas kernels, histogram(): pl.pallas_call(functools.partial(hist_kernel, blocks, feature_count, befo...  31.3 us
    all_to_all x2, waiting for transfers between devices, exchange(): lax.all_to_all(jnp.broadcast_to(total[None], (devices, rows, LANES)), 'tm...  14.7 us
    ppermute x3, waiting for transfers between devices, spread(): there = lax.ppermute(column, 'tm', flip(devices, d))  8.4 us
    all_to_all x2, starting transfers between devices, exchange(): lax.all_to_all(jnp.broadcast_to(total[None], (devices, rows, LANES)), 'tm...  7.47 us
    ppermute x3, starting transfers between devices, send_codes(): lax.ppermute(pick(codes, (plane + d) % planes, 0), 'tm', ring(devices, d))  7.01 us
    ppermute x3, waiting for transfers between devices, spread(): lax.ppermute(pairs, 'tm', ring(devices, d))  6.6 us
    ppermute x3, starting transfers between devices, send_codes(): lax.ppermute(jnp.stack([pick(h, column ^ d, 0) for h in held]), 'tm', fli...  4.23 us
    ppermute x3, starting transfers between devices, spread(): there = lax.ppermute(column, 'tm', flip(devices, d))  3.69 us
  transfers between devices with their start and end apart: 19, of which 7 were waited for; matrix products, arithmetic and copies ran while one was open for 3% of the time, Pallas kernels for 25%

profile of v2, /device:TPU:0, one launch (start us, length us, event | category | flops | bytes accessed | tf_op | source)
XLA Modules:
  0.0 106.9 jit_solution(16597150856852477245)
XLA Ops:
  0.7 1.5 %convert_element_type.3 = bf16[256,1536]{1,0:T(8,128)(2,1)S(1)} convert(s32[256,1536]{1,0:T(8,128)} %param.9) | non-fusion elementwise | flops 393216 | bytes 2359296 | tf_op jit(solution)/shard_map/convert_element_type | solution.py:292
  2.3 3.1 %collective-permute-start = (bf16[4,16,1536]{2,1,0:T(8,128)(2,1)S(1)}, bf16[4,16,1536]{2,1,0:T(8,128)(2,1)S(1)}, u32[]{:S(2)}, u32[]{:S(2)}) collective-permute-start(bf16[4,16,1536]{2,1,0:T(8,128)(2,1)S(1)} %get-tuple-element.23), channel_id=1, source_target_pairs={{0,8},{2,10},{4,12},{6,14},{8,16},{10,18},{12,20},{14,22},{16,24},... | collective-permute-start | bytes 589832 | tf_op jit(solution)/shard_map/ppermute | solution.py:257
  5.4 2.6 %collective-permute-start.1 = (bf16[4,16,1536]{2,1,0:T(8,128)(2,1)S(1)}, bf16[4,16,1536]{2,1,0:T(8,128)(2,1)S(1)}, u32[]{:S(2)}, u32[]{:S(2)}) collective-permute-start(bf16[4,16,1536]{2,1,0:T(8,128)(2,1)S(1)} %get-tuple-element.25), channel_id=1, source_target_pairs={{0,16},{2,18},{4,20},{6,22},{8,24},{10,26},{12,28},{14,30},{16,0},... | collective-permute-start | bytes 589832 | tf_op jit(solution)/shard_map/ppermute | solution.py:257
  8.0 1.3 %collective-permute-start.2 = (bf16[4,16,1536]{2,1,0:T(8,128)(2,1)S(1)}, bf16[4,16,1536]{2,1,0:T(8,128)(2,1)S(1)}, u32[]{:S(2)}, u32[]{:S(2)}) collective-permute-start(bf16[4,16,1536]{2,1,0:T(8,128)(2,1)S(1)} %get-tuple-element.24), channel_id=1, source_target_pairs={{0,24},{2,26},{4,28},{6,30},{8,0},{10,2},{12,4},{14,6},{16,8},{18,... | collective-permute-start | bytes 589832 | tf_op jit(solution)/shard_map/ppermute | solution.py:257
  9.9 2.8 %risk.1 = (f32[16,1536]{1,0:T(8,128)}, f32[16,128]{1,0:T(8,128)}) custom-call(f32[16,1536]{1,0:T(8,128)} %margins_ref.3, s32[1,1536]{1,0:T(1,128)} %broadcast_in_dim.31.tie_ref), custom_call_target="tpu_custom_call" | custom-call | tf_op jit(solution)/shard_map/risk/pallas_call | solution.py:303
  12.7 1.4 %broadcast_in_dim.32 = f32[16,16,128]{2,1,0:T(8,128)} broadcast(f32[16,128]{1,0:T(8,128)} %get-tuple-element.12), dimensions={1,2} | broadcast | bytes 139264 | tf_op jit(solution)/shard_map/broadcast_in_dim | solution.py:300
  14.1 3.9 %all-to-all-start = ((f32[16,16,128]{2,1,0:T(8,128)}), f32[16,16,128]{2,1,0:T(8,128)S(1)}, u32[]{:S(2)}, u32[]{:S(2)}) async-start(f32[16,16,128]{2,1,0:T(8,128)} %broadcast_in_dim.32), calls=%async_computation | async-start | bytes 262144 | tf_op jit(solution)/shard_map/all_to_all | solution.py:300
  18.7 2.1 %collective-permute-done.1 = bf16[4,16,1536]{2,1,0:T(8,128)(2,1)S(1)} collective-permute-done((bf16[4,16,1536]{2,1,0:T(8,128)(2,1)S(1)}, bf16[4,16,1536]{2,1,0:T(8,128)(2,1)S(1)}, u32[]{:S(2)}, u32[]{:S(2)}) %collective-permute-start.1) | collective-permute-done | bytes 196640 | tf_op jit(solution)/shard_map/ppermute | solution.py:257
  20.9 8.3 %all-to-all-done = f32[16,16,128]{2,1,0:T(8,128)S(1)} async-done(((f32[16,16,128]{2,1,0:T(8,128)}), f32[16,16,128]{2,1,0:T(8,128)S(1)}, u32[]{:S(2)}, u32[]{:S(2)}) %all-to-all-start) | async-done | bytes 131104 | tf_op jit(solution)/shard_map/all_to_all | solution.py:300
  29.9 3.2 %events.1 = (f32[16,1536]{1,0:T(8,128)}, f32[16,1536]{1,0:T(8,128)}, f32[32,128]{1,0:T(8,128)}) custom-call(s32[1]{0:T(128)} %bitcast.place_ref, f32[16,1536]{1,0:T(8,128)} %get-tuple-element.11.local_ref, f32[256,128]{1,0:T(8,128)} %bitcast.30, s32[16,1536]{1,0:T(8,128)} %events_ref.3, s32[1,1536]{1,0:T(1,128)} %broadcast_in_dim.31.tie_ref), custom_call_target="tpu_custom_call" | custom-call | tf_op jit(solution)/shard_map/events/pallas_call | solution.py:307
  33.1 1.4 %broadcast_in_dim.33 = f32[16,32,128]{2,1,0:T(8,128)} broadcast(f32[32,128]{1,0:T(8,128)} %get-tuple-element.15), dimensions={1,2} | broadcast | bytes 278528 | tf_op jit(solution)/shard_map/broadcast_in_dim | solution.py:300
  34.5 3.5 %all-to-all-start.1 = ((f32[16,32,128]{2,1,0:T(8,128)}), f32[16,32,128]{2,1,0:T(8,128)S(1)}, u32[]{:S(2)}, u32[]{:S(2)}) async-start(f32[16,32,128]{2,1,0:T(8,128)} %broadcast_in_dim.33), calls=%async_computation.1 | async-start | bytes 524288 | tf_op jit(solution)/shard_map/all_to_all | solution.py:300
  38.1 1.9 %collective-permute-start.12 = (bf16[4,16,1536]{2,1,0:T(8,128)(2,1)S(1)}, bf16[4,16,1536]{2,1,0:T(8,128)(2,1)S(1)}, u32[]{:S(2)}, u32[]{:S(2)}) collective-permute-start(bf16[4,16,1536]{2,1,0:T(8,128)(2,1)S(1)} %pad_maximum_fusion.4), channel_id=1, source_target_pairs={{0,2},{2,0},{4,6},{6,4},{8,10},{10,8},{12,14},{14,12},{16,18},{18,... | collective-permute-start | bytes 589832 | tf_op jit(solution)/shard_map/ppermute | solution.py:261
  40.0 1.5 %collective-permute-start.9 = (bf16[4,16,1536]{2,1,0:T(8,128)(2,1)S(1)}, bf16[4,16,1536]{2,1,0:T(8,128)(2,1)S(1)}, u32[]{:S(2)}, u32[]{:S(2)}) collective-permute-start(bf16[4,16,1536]{2,1,0:T(8,128)(2,1)S(1)} %pad_maximum_fusion.3), channel_id=1, source_target_pairs={{0,4},{2,6},{4,0},{6,2},{8,12},{10,14},{12,8},{14,10},{16,20},{18,... | collective-permute-start | bytes 589832 | tf_op jit(solution)/shard_map/ppermute | solution.py:261
  41.6 6.4 %all-to-all-done.1 = f32[16,32,128]{2,1,0:T(8,128)S(1)} async-done(((f32[16,32,128]{2,1,0:T(8,128)}), f32[16,32,128]{2,1,0:T(8,128)S(1)}, u32[]{:S(2)}, u32[]{:S(2)}) %all-to-all-start.1) | async-done | bytes 262176 | tf_op jit(solution)/shard_map/all_to_all | solution.py:300
  48.0 0.7 copy-done.1
  48.7 2.1 %grads.1 = (bf16[16,1536]{1,0:T(8,128)(2,1)}, bf16[16,1536]{1,0:T(8,128)(2,1)}, bf16[32,1536]{1,0:T(8,128)(2,1)}) custom-call(s32[1]{0:T(128)} %bitcast.place_ref, f32[16,1536]{1,0:T(8,128)} %margins_ref.3, s32[16,1536]{1,0:T(8,128)} %events_ref.3, s32[1,1536]{1,0:T(1,128)} %broadcast_in_dim.30.node_ref, f32[16,1536]{1,0:T(8,128)} %get-tuple-element.13.first_ref, ...), custom_call_target="tpu_custom_call" | custom-call | tf_op jit(solution)/shard_map/grads/pallas_call | solution.py:312
  51.4 2.9 %collective-permute-start.6 = (bf16[32,1536]{1,0:T(8,128)(2,1)}, bf16[32,1536]{1,0:T(8,128)(2,1)S(1)}, u32[]{:S(2)}, u32[]{:S(2)}) collective-permute-start(bf16[32,1536]{1,0:T(8,128)(2,1)} %get-tuple-element.18), channel_id=1, source_target_pairs={{0,24},{2,26},{4,28},{6,30},{8,0},{10,2},{12,4},{14,6},{16,8},{18,... | collective-permute-start | bytes 294920 | tf_op jit(solution)/shard_map/ppermute | solution.py:271
  54.3 4.3 %collective-permute-done.5 = bf16[32,1536]{1,0:T(8,128)(2,1)S(1)} collective-permute-done((bf16[32,1536]{1,0:T(8,128)(2,1)}, bf16[32,1536]{1,0:T(8,128)(2,1)S(1)}, u32[]{:S(2)}, u32[]{:S(2)}) %collective-permute-start.5) | collective-permute-done | bytes 98336 | tf_op jit(solution)/shard_map/ppermute | solution.py:271
  58.6 2.3 %collective-permute-done.4 = bf16[32,1536]{1,0:T(8,128)(2,1)S(1)} collective-permute-done((bf16[32,1536]{1,0:T(8,128)(2,1)}, bf16[32,1536]{1,0:T(8,128)(2,1)S(1)}, u32[]{:S(2)}, u32[]{:S(2)}) %collective-permute-start.4) | collective-permute-done | bytes 98336 | tf_op jit(solution)/shard_map/ppermute | solution.py:271
  60.9 0.9 pad_maximum_fusion
  62.0 0.7 collective-permute-start.13
  62.7 0.8 collective-permute-start.10
  63.5 1.8 %hist.5.refs_3_ = f32[16,128,128]{2,1,0:T(8,128)S(1)} custom-call(bf16[1,16,1536]{2,1,0:T(8,128)(2,1)S(1)} %get-tuple-element.19.refs_0_, bf16[1,32,1536]{2,1,0:T(8,128)(2,1)S(1)} %bitcast.25, bf16[1,32,1536]{2,1,0:T(8,128)(2,1)S(1)} %bitcast.26), custom_call_target="tpu_custom_call" | custom-call | flops 3221225472 | bytes 245760 | tf_op jit(solution)/shard_map/hist/pallas_call | solution.py:203
  65.3 2.2 %collective-permute-start.7 = (bf16[4,32,1536]{2,1,0:T(8,128)(2,1)S(1)}, bf16[4,32,1536]{2,1,0:T(8,128)(2,1)S(1)}, u32[]{:S(2)}, u32[]{:S(2)}) collective-permute-start(bf16[4,32,1536]{2,1,0:T(8,128)(2,1)S(1)} %pad_maximum_fusion), channel_id=1, source_target_pairs={{0,6},{2,4},{4,2},{6,0},{8,14},{10,12},{12,10},{14,8},{16,22},{18,... | collective-permute-start | bytes 1179656 | tf_op jit(solution)/shard_map/ppermute | solution.py:276
  67.5 6.4 %collective-permute-done.13.refs_1_ = bf16[4,32,1536]{2,1,0:T(8,128)(2,1)S(1)} collective-permute-done((bf16[4,32,1536]{2,1,0:T(8,128)(2,1)S(1)}, bf16[4,32,1536]{2,1,0:T(8,128)(2,1)S(1)}, u32[]{:S(2)}, u32[]{:S(2)}) %collective-permute-start.13) | collective-permute-done | bytes 393248 | tf_op jit(solution)/shard_map/ppermute | solution.py:276
  73.9 5.6 %hist.6.refs_3_ = f32[16,128,128]{2,1,0:T(8,128)S(1)} custom-call(bf16[3,16,1536]{2,1,0:T(8,128)(2,1)S(1)} %pad_maximum_fusion.5.refs_0_, bf16[3,32,1536]{2,1,0:T(8,128)(2,1)S(1)} %pad_maximum_fusion.1.refs_1_, bf16[3,32,1536]{2,1,0:T(8,128)(2,1)S(1)} %slice.6.refs_2_, f32[16,128,128]{2,1,0:T(8,128)S(1)} %hist.5.refs_3_), custom_call_target="tpu_custom_call", output_to_operand_aliasing={{}: (3, {})} | custom-call | flops 9663676416 | bytes 737280 | tf_op jit(solution)/shard_map/hist/pallas_call | solution.py:203
  79.5 0.8 collective-permute-start.3
  80.4 2.0 %collective-permute-done.10.refs_1_ = bf16[4,32,1536]{2,1,0:T(8,128)(2,1)S(1)} collective-permute-done((bf16[4,32,1536]{2,1,0:T(8,128)(2,1)S(1)}, bf16[4,32,1536]{2,1,0:T(8,128)(2,1)S(1)}, u32[]{:S(2)}, u32[]{:S(2)}) %collective-permute-start.10) | collective-permute-done | bytes 393248 | tf_op jit(solution)/shard_map/ppermute | solution.py:276
  82.9 7.4 %hist.7.refs_3_ = f32[16,128,128]{2,1,0:T(8,128)S(1)} custom-call(bf16[4,16,1536]{2,1,0:T(8,128)(2,1)S(1)} %collective-permute-done.12.refs_0_, bf16[4,32,1536]{2,1,0:T(8,128)(2,1)S(1)} %collective-permute-done.13.refs_1_, bf16[4,32,1536]{2,1,0:T(8,128)(2,1)S(1)} %collective-permute-done.14.refs_2_, ...), custom_call_target="tpu_custom_call", output_to_operand_aliasing={{}: (3, {})} | custom-call | flops 12884901888 | bytes 983040 | tf_op jit(solution)/shard_map/hist/pallas_call | solution.py:203
  90.3 7.4 %hist.8.refs_3_ = f32[16,128,128]{2,1,0:T(8,128)S(1)} custom-call(bf16[4,16,1536]{2,1,0:T(8,128)(2,1)S(1)} %collective-permute-done.9.refs_0_, bf16[4,32,1536]{2,1,0:T(8,128)(2,1)S(1)} %collective-permute-done.10.refs_1_, bf16[4,32,1536]{2,1,0:T(8,128)(2,1)S(1)} %collective-permute-done.11.refs_2_, ...), custom_call_target="tpu_custom_call", output_to_operand_aliasing={{}: (3, {})} | custom-call | flops 12884901888 | bytes 983040 | tf_op jit(solution)/shard_map/hist/pallas_call | solution.py:203
  97.8 9.1 %hist.9 = f32[16,256]{1,0:T(8,128)} custom-call(bf16[4,16,1536]{2,1,0:T(8,128)(2,1)S(1)} %collective-permute-done.3.refs_0_, bf16[4,32,1536]{2,1,0:T(8,128)(2,1)S(1)} %collective-permute-done.7.refs_1_, bf16[4,32,1536]{2,1,0:T(8,128)(2,1)S(1)} %collective-permute-done.8.refs_2_, f32[16,128,128]{2,1,0:T(8,128)S(1)} %hist.8.refs_3_), custom_call_target="tpu_custom_call" | custom-call | flops 12884901888 | bytes 983040 | tf_op jit(solution)/shard_map/hist/pallas_call | solution.py:203
  (41 shorter events, 3.4 us)
Async XLA Ops:
  0.7 8.6 %copy-start.3 = (s32[1536]{0:T(1024)S(1)}, s32[1536]{0:T(1024)}, u32[]{:S(2)}) copy-start(s32[1536]{0:T(1024)} %param.7) | copy-start | bytes 18436
  0.7 17.4 %copy-start.4 = (s32[1536]{0:T(1024)S(1)}, s32[1536]{0:T(1024)}, u32[]{:S(2)}) copy-start(s32[1536]{0:T(1024)} %param.8) | copy-start | bytes 18436
  2.3 16.4 %collective-permute-start = (bf16[4,16,1536]{2,1,0:T(8,128)(2,1)S(1)}, bf16[4,16,1536]{2,1,0:T(8,128)(2,1)S(1)}, u32[]{:S(2)}, u32[]{:S(2)}) collective-permute-start(bf16[4,16,1536]{2,1,0:T(8,128)(2,1)S(1)} %get-tuple-element.23), channel_id=1, source_target_pairs={{0,8},{2,10},{4,12},{6,14},{8,16},{10,18},{12,20},{14,22},{16,24},... | collective-permute-start | bytes 589832 | tf_op jit(solution)/shard_map/ppermute | solution.py:257
  5.4 15.5 %collective-permute-start.1 = (bf16[4,16,1536]{2,1,0:T(8,128)(2,1)S(1)}, bf16[4,16,1536]{2,1,0:T(8,128)(2,1)S(1)}, u32[]{:S(2)}, u32[]{:S(2)}) collective-permute-start(bf16[4,16,1536]{2,1,0:T(8,128)(2,1)S(1)} %get-tuple-element.25), channel_id=1, source_target_pairs={{0,16},{2,18},{4,20},{6,22},{8,24},{10,26},{12,28},{14,30},{16,0},... | collective-permute-start | bytes 589832 | tf_op jit(solution)/shard_map/ppermute | solution.py:257
  8.0 12.9 %collective-permute-start.2 = (bf16[4,16,1536]{2,1,0:T(8,128)(2,1)S(1)}, bf16[4,16,1536]{2,1,0:T(8,128)(2,1)S(1)}, u32[]{:S(2)}, u32[]{:S(2)}) collective-permute-start(bf16[4,16,1536]{2,1,0:T(8,128)(2,1)S(1)} %get-tuple-element.24), channel_id=1, source_target_pairs={{0,24},{2,26},{4,28},{6,30},{8,0},{10,2},{12,4},{14,6},{16,8},{18,... | collective-permute-start | bytes 589832 | tf_op jit(solution)/shard_map/ppermute | solution.py:257
  14.1 15.1 %all-to-all-start = ((f32[16,16,128]{2,1,0:T(8,128)}), f32[16,16,128]{2,1,0:T(8,128)S(1)}, u32[]{:S(2)}, u32[]{:S(2)}) async-start(f32[16,16,128]{2,1,0:T(8,128)} %broadcast_in_dim.32), calls=%async_computation | async-start | bytes 262144 | tf_op jit(solution)/shard_map/all_to_all | solution.py:300
  29.2 0.7 copy-start.2
  34.5 13.4 %all-to-all-start.1 = ((f32[16,32,128]{2,1,0:T(8,128)}), f32[16,32,128]{2,1,0:T(8,128)S(1)}, u32[]{:S(2)}, u32[]{:S(2)}) async-start(f32[16,32,128]{2,1,0:T(8,128)} %broadcast_in_dim.33), calls=%async_computation.1 | async-start | bytes 524288 | tf_op jit(solution)/shard_map/all_to_all | solution.py:300
  38.1 41.4 %collective-permute-start.12 = (bf16[4,16,1536]{2,1,0:T(8,128)(2,1)S(1)}, bf16[4,16,1536]{2,1,0:T(8,128)(2,1)S(1)}, u32[]{:S(2)}, u32[]{:S(2)}) collective-permute-start(bf16[4,16,1536]{2,1,0:T(8,128)(2,1)S(1)} %pad_maximum_fusion.4), channel_id=1, source_target_pairs={{0,2},{2,0},{4,6},{6,4},{8,10},{10,8},{12,14},{14,12},{16,18},{18,... | collective-permute-start | bytes 589832 | tf_op jit(solution)/shard_map/ppermute | solution.py:261
  40.0 50.3 %collective-permute-start.9 = (bf16[4,16,1536]{2,1,0:T(8,128)(2,1)S(1)}, bf16[4,16,1536]{2,1,0:T(8,128)(2,1)S(1)}, u32[]{:S(2)}, u32[]{:S(2)}) collective-permute-start(bf16[4,16,1536]{2,1,0:T(8,128)(2,1)S(1)} %pad_maximum_fusion.3), channel_id=1, source_target_pairs={{0,4},{2,6},{4,0},{6,2},{8,12},{10,14},{12,8},{14,10},{16,20},{18,... | collective-permute-start | bytes 589832 | tf_op jit(solution)/shard_map/ppermute | solution.py:261
  48.0 0.7 copy-start.1
  50.7 12.7 %copy-start = (bf16[32,1536]{1,0:T(8,128)(2,1)S(1)}, bf16[32,1536]{1,0:T(8,128)(2,1)}, u32[]{:S(2)}) copy-start(bf16[32,1536]{1,0:T(8,128)(2,1)} %get-tuple-element.18) | copy-start | bytes 294916
  50.7 7.8 %collective-permute-start.5 = (bf16[32,1536]{1,0:T(8,128)(2,1)}, bf16[32,1536]{1,0:T(8,128)(2,1)S(1)}, u32[]{:S(2)}, u32[]{:S(2)}) collective-permute-start(bf16[32,1536]{1,0:T(8,128)(2,1)} %get-tuple-element.18), channel_id=1, source_target_pairs={{0,16},{2,18},{4,20},{6,22},{8,24},{10,26},{12,28},{14,30},{16,0},... | collective-permute-start | bytes 294920 | tf_op jit(solution)/shard_map/ppermute | solution.py:271
  51.4 7.2 %collective-permute-start.6 = (bf16[32,1536]{1,0:T(8,128)(2,1)}, bf16[32,1536]{1,0:T(8,128)(2,1)S(1)}, u32[]{:S(2)}, u32[]{:S(2)}) collective-permute-start(bf16[32,1536]{1,0:T(8,128)(2,1)} %get-tuple-element.18), channel_id=1, source_target_pairs={{0,24},{2,26},{4,28},{6,30},{8,0},{10,2},{12,4},{14,6},{16,8},{18,... | collective-permute-start | bytes 294920 | tf_op jit(solution)/shard_map/ppermute | solution.py:271
  54.3 6.6 %collective-permute-start.4 = (bf16[32,1536]{1,0:T(8,128)(2,1)}, bf16[32,1536]{1,0:T(8,128)(2,1)S(1)}, u32[]{:S(2)}, u32[]{:S(2)}) collective-permute-start(bf16[32,1536]{1,0:T(8,128)(2,1)} %get-tuple-element.18), channel_id=1, source_target_pairs={{0,8},{2,10},{4,12},{6,14},{8,16},{10,18},{12,20},{14,22},{16,24},... | collective-permute-start | bytes 294920 | tf_op jit(solution)/shard_map/ppermute | solution.py:271
  58.6 4.1 %collective-permute-start.16 = (bf16[32,1536]{1,0:T(8,128)(2,1)}, bf16[32,1536]{1,0:T(8,128)(2,1)S(1)}, u32[]{:S(2)}, u32[]{:S(2)}) collective-permute-start(bf16[32,1536]{1,0:T(8,128)(2,1)} %get-tuple-element.18), channel_id=1, source_target_pairs={{0,1},{1,0},{2,3},{3,2},{4,5},{5,4},{6,7},{7,6},{8,9},{9,8},{10,11... | collective-permute-start | bytes 294920 | tf_op jit(solution)/shard_map/ppermute | solution.py:242
  61.9 3.4 %collective-permute-start.15 = (bf16[4,32,1536]{2,1,0:T(8,128)(2,1)S(1)}, bf16[4,32,1536]{2,1,0:T(8,128)(2,1)S(1)}, u32[]{:S(2)}, u32[]{:S(2)}) collective-permute-start(bf16[4,32,1536]{2,1,0:T(8,128)(2,1)S(1)} %pad_maximum_fusion), channel_id=1, source_target_pairs={{0,1},{1,0},{2,3},{3,2},{4,5},{5,4},{6,7},{7,6},{8,9},{9,8},{10,11... | collective-permute-start | bytes 1179656 | tf_op jit(solution)/shard_map/ppermute | solution.py:242
  62.0 12.0 %collective-permute-start.13 = (bf16[4,32,1536]{2,1,0:T(8,128)(2,1)S(1)}, bf16[4,32,1536]{2,1,0:T(8,128)(2,1)S(1)}, u32[]{:S(2)}, u32[]{:S(2)}) collective-permute-start(bf16[4,32,1536]{2,1,0:T(8,128)(2,1)S(1)} %pad_maximum_fusion), channel_id=1, source_target_pairs={{0,2},{2,0},{4,6},{6,4},{8,10},{10,8},{12,14},{14,12},{16,18},{18,... | collective-permute-start | bytes 1179656 | tf_op jit(solution)/shard_map/ppermute | solution.py:276
  62.7 19.7 %collective-permute-start.10 = (bf16[4,32,1536]{2,1,0:T(8,128)(2,1)S(1)}, bf16[4,32,1536]{2,1,0:T(8,128)(2,1)S(1)}, u32[]{:S(2)}, u32[]{:S(2)}) collective-permute-start(bf16[4,32,1536]{2,1,0:T(8,128)(2,1)S(1)} %pad_maximum_fusion), channel_id=1, source_target_pairs={{0,4},{2,6},{4,0},{6,2},{8,12},{10,14},{12,8},{14,10},{16,20},{18,... | collective-permute-start | bytes 1179656 | tf_op jit(solution)/shard_map/ppermute | solution.py:276
  65.3 17.1 %collective-permute-start.7 = (bf16[4,32,1536]{2,1,0:T(8,128)(2,1)S(1)}, bf16[4,32,1536]{2,1,0:T(8,128)(2,1)S(1)}, u32[]{:S(2)}, u32[]{:S(2)}) collective-permute-start(bf16[4,32,1536]{2,1,0:T(8,128)(2,1)S(1)} %pad_maximum_fusion), channel_id=1, source_target_pairs={{0,6},{2,4},{4,2},{6,0},{8,14},{10,12},{12,10},{14,8},{16,22},{18,... | collective-permute-start | bytes 1179656 | tf_op jit(solution)/shard_map/ppermute | solution.py:276
  73.9 9.0 %collective-permute-start.14 = (bf16[4,32,1536]{2,1,0:T(8,128)(2,1)S(1)}, bf16[4,32,1536]{2,1,0:T(8,128)(2,1)S(1)}, u32[]{:S(2)}, u32[]{:S(2)}) collective-permute-start(bf16[4,32,1536]{2,1,0:T(8,128)(2,1)S(1)} %collective-permute-done.13.refs_1_), channel_id=1, source_target_pairs={{0,1},{1,0},{2,3},{3,2},{4,5},{5,4},{6,7},{7,6},{8,9},{9,8},{10,11... | collective-permute-start | bytes 1179656 | tf_op jit(solution)/shard_map/ppermute | solution.py:242
  79.5 18.2 %collective-permute-start.3 = (bf16[4,16,1536]{2,1,0:T(8,128)(2,1)S(1)}, bf16[4,16,1536]{2,1,0:T(8,128)(2,1)S(1)}, u32[]{:S(2)}, u32[]{:S(2)}) collective-permute-start(bf16[4,16,1536]{2,1,0:T(8,128)(2,1)S(1)} %pad_maximum_fusion.2), channel_id=1, source_target_pairs={{0,6},{2,4},{4,2},{6,0},{8,14},{10,12},{12,10},{14,8},{16,22},{18,... | collective-permute-start | bytes 589832 | tf_op jit(solution)/shard_map/ppermute | solution.py:261
  82.4 7.9 %collective-permute-start.11 = (bf16[4,32,1536]{2,1,0:T(8,128)(2,1)S(1)}, bf16[4,32,1536]{2,1,0:T(8,128)(2,1)S(1)}, u32[]{:S(2)}, u32[]{:S(2)}) collective-permute-start(bf16[4,32,1536]{2,1,0:T(8,128)(2,1)S(1)} %collective-permute-done.10.refs_1_), channel_id=1, source_target_pairs={{0,1},{1,0},{2,3},{3,2},{4,5},{5,4},{6,7},{7,6},{8,9},{9,8},{10,11... | collective-permute-start | bytes 1179656 | tf_op jit(solution)/shard_map/ppermute | solution.py:242
  82.4 15.4 %collective-permute-start.8 = (bf16[4,32,1536]{2,1,0:T(8,128)(2,1)S(1)}, bf16[4,32,1536]{2,1,0:T(8,128)(2,1)S(1)}, u32[]{:S(2)}, u32[]{:S(2)}) collective-permute-start(bf16[4,32,1536]{2,1,0:T(8,128)(2,1)S(1)} %collective-permute-done.7.refs_1_), channel_id=1, source_target_pairs={{0,1},{1,0},{2,3},{3,2},{4,5},{5,4},{6,7},{7,6},{8,9},{9,8},{10,11... | collective-permute-start | bytes 1179656 | tf_op jit(solution)/shard_map/ppermute | solution.py:242

commit v3 on v2

--- a/solution.py
+++ b/solution.py
@@ -46,7 +46,23 @@
     return peak + jnp.log(1.0 + jnp.exp(-jnp.abs(a - b)))
 
 
-def risk_kernel(margins_ref, tie_ref, local_ref, total_ref):
+def share(total, total_ref):
+    wide = jnp.broadcast_to(total, total_ref.shape[1:])
+    for k in range(total_ref.shape[0]):
+        total_ref[k] = wide
+
+
+def share_row(total, total_ref):
+    row = jnp.sum(jnp.where(diagonal((total.shape[0], LANES)), total, 0.0), axis=0, keepdims=True)
+    for k in range(total_ref.shape[0]):
+        total_ref[k] = row
+
+
+def diagonal(like):
+    return lax.broadcasted_iota(jnp.int32, like, 0) == lax.broadcasted_iota(jnp.int32, like, 1)
+
+
+def risk_kernel(margins_ref, risk_ref, total_ref):
     peak = margins_ref[...]
     length = peak.shape[1]
     mass = jnp.ones_like(peak)
@@ -58,30 +74,46 @@
         mass = jnp.where(gap >= 0, mass + far_mass * shrink, mass * shrink + far_mass)
         peak = jnp.maximum(peak, far_peak)
     risk = peak + jnp.log(mass)
-    total_ref[...] = jnp.broadcast_to(risk[:, 0:1], (risk.shape[0], LANES))
-    tie = jnp.broadcast_to(tie_ref[...], risk.shape)
+    share(risk[:, 0:1], total_ref)
+    risk_ref[...] = risk
+
+
+def tie_rows(tie_ref, like):
+    return jnp.broadcast_to(tie_ref[...][None], like.shape)
+
+
+def open_kernel(risk_ref, tie_ref, local_ref):
+    risk = risk_ref[...]
+    tie = tie_rows(tie_ref, risk)
     lane = lax.broadcasted_iota(jnp.int32, risk.shape, 1)
     opens = (lane == 0) | (tie != pltpu.roll(tie, 1, 1))
     filled = jnp.where(opens, risk, -log_floor)
-    for step in steps(length):
+    for step in steps(risk.shape[1]):
         filled = jnp.minimum(filled, behind(filled, step, -log_floor))
     local_ref[...] = filled
 
 
-def carried(place, parts, later, endpoints):
-    count = parts.shape[0] // endpoints
-    held = [parts[k * endpoints : (k + 1) * endpoints] for k in range(count)]
-    held = [jnp.where((place < k) if later else (place > k), h, log_floor) for k, h in enumerate(held)]
+def carried_later(place, parts_ref):
+    held = [jnp.where(place < k, parts_ref[k], log_floor) for k in range(parts_ref.shape[0])]
     peak = functools.reduce(jnp.maximum, held)
     mass = functools.reduce(jnp.add, [jnp.exp(h - peak) for h in held])
-    return jnp.where(peak > 0.5 * log_floor, peak + jnp.log(mass), log_floor)
-
-
-def event_kernel(place_ref, local_ref, parts_ref, events_ref, tie_ref, first_ref, second_ref, total_ref):
+    return jnp.where(peak > 0.5 * log_floor, peak + jnp.log(mass), log_floor)[:, 0:1]
+
+
+def carried_earlier(place, parts_ref, count):
+    parts = jnp.concatenate([parts_ref[k] for k in range(parts_ref.shape[0])], axis=0)
+    device = lax.broadcasted_iota(jnp.int32, parts.shape, 0)
+    held = jnp.where(device < place, parts, log_floor)
+    peak = jnp.max(held, axis=0, keepdims=True)
+    mass = jnp.sum(jnp.exp(held - peak), axis=0, keepdims=True)
+    row = jnp.where(peak > 0.5 * log_floor, peak + jnp.log(mass), log_floor)
+    return jnp.sum(jnp.where(diagonal((count, LANES)), row, 0.0), axis=1, keepdims=True)
+
+
+def event_kernel(place_ref, local_ref, parts_ref, events_ref, first_ref, second_ref, total_ref):
     local = local_ref[...]
     endpoints, length = local.shape
-    carry = carried(place_ref[0], parts_ref[...], True, endpoints)
-    risk = log_sum(local, carry[:, 0:1])
+    risk = log_sum(local, carried_later(place_ref[0], parts_ref))
     happened = events_ref[...] == 1
     peak = jnp.where(happened, -risk, log_floor)
     first = happened.astype(f32)
@@ -101,33 +133,40 @@
     first_log = jnp.where(some, peak + jnp.log(first), log_floor)
     second_log = jnp.where(some, 2.0 * peak + jnp.log(second), log_floor)
     end = length - 1
-    total_ref[0:endpoints] = jnp.broadcast_to(first_log[:, end:], (endpoints, LANES))
-    total_ref[endpoints:] = jnp.broadcast_to(second_log[:, end:], (endpoints, LANES))
-    tie = jnp.broadcast_to(tie_ref[...], local.shape)
-    lane = lax.broadcasted_iota(jnp.int32, local.shape, 1)
-    closes = (lane == end) | (tie != pltpu.roll(tie, length - 1, 1))
-    first_fill = jnp.where(closes, first_log, -log_floor)
-    second_fill = jnp.where(closes, second_log, -log_floor)
+    share_row(jnp.concatenate([first_log[:, end:], second_log[:, end:]], axis=0), total_ref)
+    first_ref[...] = first_log
+    second_ref[...] = second_log
+
+
+def close_kernel(first_ref, second_ref, tie_ref, first_out, second_out):
+    first = first_ref[...]
+    second = second_ref[...]
+    tie = tie_rows(tie_ref, first)
+    length = first.shape[1]
+    lane = lax.broadcasted_iota(jnp.int32, first.shape, 1)
+    closes = (lane == length - 1) | (tie != pltpu.roll(tie, length - 1, 1))
+    first = jnp.where(closes, first, -log_floor)
+    second = jnp.where(closes, second, -log_floor)
     for step in steps(length):
-        first_fill = jnp.minimum(first_fill, ahead(first_fill, step, -log_floor))
-        second_fill = jnp.minimum(second_fill, ahead(second_fill, step, -log_floor))
-    first_ref[...] = first_fill
-    second_ref[...] = second_fill
+        first = jnp.minimum(first, ahead(first, step, -log_floor))
+        second = jnp.minimum(second, ahead(second, step, -log_floor))
+    first_out[...] = first
+    second_out[...] = second
 
 
 def grad_kernel(place_ref, margins_ref, events_ref, node_ref, first_ref, second_ref, parts_ref, grad_ref, hess_ref, pair_ref):
     margins = margins_ref[...]
     endpoints = margins.shape[0]
-    carry = carried(place_ref[0], parts_ref[...], False, 2 * endpoints)
-    first_log = log_sum(first_ref[...], carry[0:endpoints, 0:1])
-    second_log = log_sum(second_ref[...], carry[endpoints:, 0:1])
+    carry = carried_earlier(place_ref[0], parts_ref, 2 * endpoints)
+    first_log = log_sum(first_ref[...], carry[0:endpoints])
+    second_log = log_sum(second_ref[...], carry[endpoints:])
     first = jnp.exp(margins + first_log)
     second = jnp.exp(2.0 * margins + second_log)
     grad = first - (events_ref[...] == 1).astype(f32)
     hess = first - second
     grad_ref[...] = grad.astype(bf16)
     hess_ref[...] = hess.astype(bf16)
-    chosen = jnp.broadcast_to(node_ref[...], margins.shape) == 1
+    chosen = tie_rows(node_ref, margins) == 1
     pair_ref[0:endpoints] = jnp.where(chosen, grad, 0.0).astype(bf16)
     pair_ref[endpoints:] = jnp.where(chosen, hess, 0.0).astype(bf16)
 
@@ -209,7 +248,7 @@
         scratch_shapes=[pltpu.VMEM(sums, f32)] if last else [],
         input_output_aliases={3: 0} if before is not None and not last else {},
         name="hist",
-        compiler_params=pltpu.CompilerParams(dimension_semantics=("arbitrary",), vmem_limit_bytes=32 << 20),
+        compiler_params=pltpu.CompilerParams(dimension_semantics=("arbitrary",), vmem_limit_bytes=20 << 20),
         cost_estimate=pl.CostEstimate(
             flops=blocks * feature_count * 2 * (4 * half) * HALF * length * 4,
             bytes_accessed=blocks * (feature_count + 2 * half) * length * 2,
@@ -218,8 +257,16 @@
     )(*operands)
 
 
-def call(kernel, out_shape, name, **kw):
-    return pl.pallas_call(kernel, out_shape=out_shape, name=name, **kw)
+def call(kernel, out_shape, name, *operands, place=False):
+    single = isinstance(out_shape, jax.ShapeDtypeStruct)
+    return pl.pallas_call(
+        kernel,
+        out_shape=out_shape,
+        in_specs=([SMEM] if place else []) + [VMEM] * (len(operands) - place),
+        out_specs=VMEM if single else (VMEM,) * len(out_shape),
+        name=name,
+        compiler_params=pltpu.CompilerParams(vmem_limit_bytes=12 << 20),
+    )(*operands)
 
 
 def shape(*dims, dtype=f32):
@@ -246,35 +293,43 @@
     return lax.dynamic_index_in_dim(x, index, axis, False)
 
 
-def send_codes(codes, devices):
+def send_planes(codes, devices):
     planes = devices // 4
-    place = lax.axis_index("tm")
-    plane, column = place // 4, place % 4
-    _, mine, length = codes.reshape(devices, -1, codes.shape[1]).shape
-    codes = codes.reshape(planes, 4, mine, length)
+    plane = lax.axis_index("tm") // 4
+    codes = codes.reshape(planes, 4, -1, codes.shape[1])
     held = [pick(codes, plane, 0)]
     for d in range(1, planes):
         held.append(lax.ppermute(pick(codes, (plane + d) % planes, 0), "tm", ring(devices, d)))
-    own = pick(held[0], column, 0)[None]
-    near = jnp.stack([pick(h, column, 0) for h in held[1:]])
+    return held
+
+
+def spread(held, pairs, devices):
+    planes = devices // 4
+    here = lax.axis_index("tm") % 4
+    column = [lax.ppermute(pairs, "tm", ring(devices, d)) for d in range(1, planes)]
+    sums = histogram(pick(held[0], here, 0)[None], pairs[None], swap(pairs)[None], None, False)
+    held, sums = lax.optimization_barrier((held, sums))
+    near = jnp.stack([pick(h, here, 0) for h in held[1:]])
     far = [
-        lax.ppermute(jnp.stack([pick(h, column ^ d, 0) for h in held]), "tm", flip(devices, d))
+        lax.ppermute(jnp.stack([pick(h, here ^ d, 0) for h in held]), "tm", flip(devices, d))
         for d in range(1, 4)
     ]
-    return own, near, far
-
-
-def spread(codes, pairs, devices):
-    own, near, far = codes
-    planes = devices // 4
-    sums = histogram(own, pairs[None], swap(pairs)[None], None, False)
-    column = [lax.ppermute(pairs, "tm", ring(devices, d)) for d in range(1, planes)]
+    far, *column, sums = lax.optimization_barrier((far, *column, sums))
     column = jnp.stack([pairs] + column)
     other = swap(column)
-    sums = histogram(near, column[1:], other[1:], sums, False)
+    there = [lax.ppermute(column, "tm", flip(devices, d)) for d in range(1, 4)]
+    cut = planes - 2
+    sums = histogram(near[:cut], column[1 : cut + 1], other[1 : cut + 1], sums, False)
+    there[0], sums = lax.optimization_barrier((there[0], sums))
+    back = swap(there[0])
+    sums = histogram(near[cut:], column[cut + 1 :], other[cut + 1 :], sums, False)
     for d in range(1, 4):
-        there = lax.ppermute(column, "tm", flip(devices, d))
-        sums = histogram(far[d - 1], there, swap(there), sums, d == 3)
+        mine = there[d - 1]
+        now = back
+        if d < 3:
+            there[d], sums = lax.optimization_barrier((there[d], sums))
+            back = swap(there[d])
+        sums = histogram(far[d - 1], mine, now, sums, d == 3)
     return sums
 
 
@@ -285,41 +340,36 @@
 
 def on_device(devices, margins, events, tie_group, in_node, bins):
     endpoints, length = margins.shape
-    place = lax.axis_index("tm")
-    here = place[None].astype(jnp.int32)
-    tie = tie_group[None]
+    here = lax.axis_index("tm")[None].astype(jnp.int32)
     mine = bins.shape[0] // devices
+    rows = shape(endpoints, length)
+    narrow = shape(endpoints, length, dtype=bf16)
+
+    def exchange(total):
+        return lax.all_to_all(total, "tm", 0, 0)
+
+    risk, total = call(risk_kernel, (rows, shape(devices, endpoints, LANES)), "risk", margins)
+    parts = exchange(total)
+    local = call(open_kernel, rows, "opens", risk, tie_group)
+    bins, local = lax.optimization_barrier((bins, local))
     codes = bins.astype(bf16)
-    if devices == 16:
-        codes = send_codes(codes, devices)
+    blocked = devices == 16
+    if blocked:
+        codes = send_planes(codes, devices)
     else:
         codes = lax.all_to_all(codes.reshape(devices, mine, length), "tm", 0, 0)
-
-    def exchange(total):
-        rows = total.shape[0]
-        sent = lax.all_to_all(jnp.broadcast_to(total[None], (devices, rows, LANES)), "tm", 0, 0)
-        return sent.reshape(devices * rows, LANES)
-
-    local, total = call(
-        risk_kernel, (shape(endpoints, length), shape(endpoints, LANES)), "risk",
-        in_specs=[VMEM] * 2, out_specs=(VMEM,) * 2,
-    )(margins, tie)
     first, second, total = call(
-        event_kernel,
-        (shape(endpoints, length), shape(endpoints, length), shape(2 * endpoints, LANES)), "events",
-        in_specs=[SMEM] + [VMEM] * 4, out_specs=(VMEM,) * 3,
-    )(here, local, exchange(total), events, tie)
+        event_kernel, (rows, rows, shape(devices, 1, LANES)), "events",
+        here, local, parts, events, place=True,
+    )
+    parts = exchange(total)
+    first, second = call(close_kernel, (rows, rows), "closes", first, second, tie_group)
+    codes, parts = lax.optimization_barrier((codes, parts))
     grad, hess, pairs = call(
-        grad_kernel,
-        (
-            shape(endpoints, length, dtype=bf16),
-            shape(endpoints, length, dtype=bf16),
-            shape(2 * endpoints, length, dtype=bf16),
-        ), "grads",
-        in_specs=[SMEM] + [VMEM] * 6, out_specs=(VMEM,) * 3,
-    )(here, margins, events, in_node[None], first, second, exchange(total))
-
-    gain = spread(codes, pairs, devices) if devices == 16 else spread_any(codes, pairs)
+        grad_kernel, (narrow, narrow, shape(2 * endpoints, length, dtype=bf16)), "grads",
+        here, margins, events, in_node, first, second, parts, place=True,
+    )
+    gain = spread(codes, pairs, devices) if blocked else spread_any(codes, pairs)
     return (grad, hess, gain[None])
 
 

time: 107 us -> 94.1 us (0.88)
  waiting for transfers between devices: 31.8 us -> 24.3 us
  local copies, waits for them, and re-layouts: 5.48 us -> 1.77 us
  Pallas kernels: 39.4 us -> 36.7 us
  starting transfers between devices: 26.5 us -> 28.2 us
    all_to_all x2, waiting for transfers between devices: 14.7 us -> 6.1 us  [exchange(): return lax.all_to_all(total, 'tm', 0, 0)]
    all_to_all x2, starting transfers between devices: 7.47 us -> 12.1 us  [exchange(): return lax.all_to_all(total, 'tm', 0, 0)]
    broadcast_in_dim x4 -> x0, local copies, waits for them, and re-layouts: 3.98 us -> none  [the longest x2 2.79 us: exchange(): jnp.broadcast_to(total[None], (devices, rows, LANES))]
    pallas_call x3 -> x5, Pallas kernels: 8.1 us -> 5.33 us  [call(): pl.pallas_call(kernel, out_shape=out_shape, in_specs=([SMEM] if place els...]
    ppermute x9, starting transfers between devices: 14.9 us -> 12.3 us  [the longest x3 5.72 us: send_planes(): lax.ppermute(pick(codes, (plane + d) % planes, 0), 'tm', ring(devices, d))]
    ppermute x9, waiting for transfers between devices: 10.5 us -> 12.7 us  [the longest x3 7.67 us: spread(): there = [lax.ppermute(column, 'tm', flip(devices, d)) for d in range(1, 4)]]
    ppermute x3, waiting for transfers between devices: 6.6 us -> 4.75 us  [spread(): lax.ppermute(pairs, 'tm', ring(devices, d))]
    pallas_call x5 -> x6, Pallas kernels: 31.3 us -> 31.4 us  [histogram(): pl.pallas_call(functools.partial(hist_kernel, blocks, feature_count, befo...]
  transfers between devices with their start and end apart: 19 -> 19, of which waited for: 7 -> 7; matrix products, arithmetic and copies ran while one was open for 3% -> 2% of each run, Pallas kernels for 25% -> 27%
where the time goes in v3:
time: 94.1 us; the launch traced here: 93.7 us
  Pallas kernels  36.7 us (39%)
  starting transfers between devices  28.2 us (30%)
  waiting for transfers between devices  24.3 us (26%)
  local copies, waits for them, and re-layouts  1.77 us (2%)
  other arithmetic  1.71 us (2%)
  between operations  1.01 us (1%)
    pallas_call x6, Pallas kernels, histogram(): pl.pallas_call(functools.partial(hist_kernel, blocks, feature_count, befo...  31.4 us
    all_to_all x2, starting transfers between devices, exchange(): return lax.all_to_all(total, 'tm', 0, 0)  12.1 us
    ppermute x3, waiting for transfers between devices, spread(): there = [lax.ppermute(column, 'tm', flip(devices, d)) for d in range(1, 4)]  7.67 us
    all_to_all x2, waiting for transfers between devices, exchange(): return lax.all_to_all(total, 'tm', 0, 0)  6.1 us
    ppermute x3, starting transfers between devices, send_planes(): lax.ppermute(pick(codes, (plane + d) % planes, 0), 'tm', ring(devices, d))  5.72 us
    pallas_call x5, Pallas kernels, call(): pl.pallas_call(kernel, out_shape=out_shape, in_specs=([SMEM] if place els...  5.33 us
    ppermute x3, waiting for transfers between devices, send_planes(): lax.ppermute(pick(codes, (plane + d) % planes, 0), 'tm', ring(devices, d))  4.88 us
    ppermute x3, waiting for transfers between devices, spread(): lax.ppermute(pairs, 'tm', ring(devices, d))  4.75 us
  transfers between devices with their start and end apart: 19, of which 7 were waited for; matrix products, arithmetic and copies ran while one was open for 2% of the time, Pallas kernels for 27%

profile of v3, /device:TPU:0, one launch (start us, length us, event | category | flops | bytes accessed | tf_op | source)
XLA Modules:
  0.0 93.7 jit_solution(14210860162464445961)
XLA Ops:
  0.6 0.9 copy-done
  1.5 1.4 %risk.1 = (f32[16,1536]{1,0:T(8,128)S(1)}, f32[16,16,128]{2,1,0:T(8,128)}) custom-call(f32[16,1536]{1,0:T(8,128)S(1)} %copy-done), custom_call_target="tpu_custom_call" | custom-call | tf_op jit(solution)/shard_map/risk/pallas_call | solution.py:262
  3.0 8.3 %all-to-all-start = ((f32[16,16,128]{2,1,0:T(8,128)}), f32[16,16,128]{2,1,0:T(8,128)S(1)}, u32[]{:S(2)}, u32[]{:S(2)}) async-start(f32[16,16,128]{2,1,0:T(8,128)} %get-tuple-element.40), calls=%async_computation | async-start | bytes 262144 | tf_op jit(solution)/shard_map/all_to_all | solution.py:349
  11.4 0.7 copy-done.3
  12.1 0.7 opens.1.local_ref
  12.7 1.5 %convert_element_type.3 = bf16[256,1536]{1,0:T(8,128)(2,1)S(1)} convert(s32[256,1536]{1,0:T(8,128)} %param.9) | non-fusion elementwise | flops 393216 | bytes 2359296 | tf_op jit(solution)/shard_map/convert_element_type | solution.py:355
  14.4 1.9 %collective-permute-start = (bf16[4,16,1536]{2,1,0:T(8,128)(2,1)S(1)}, bf16[4,16,1536]{2,1,0:T(8,128)(2,1)S(1)}, u32[]{:S(2)}, u32[]{:S(2)}) collective-permute-start(bf16[4,16,1536]{2,1,0:T(8,128)(2,1)S(1)} %get-tuple-element.75), channel_id=1, source_target_pairs={{0,8},{2,10},{4,12},{6,14},{8,16},{10,18},{12,20},{14,22},{16,24},... | collective-permute-start | bytes 589832 | tf_op jit(solution)/shard_map/ppermute | solution.py:302
  16.3 2.4 %collective-permute-start.1 = (bf16[4,16,1536]{2,1,0:T(8,128)(2,1)S(1)}, bf16[4,16,1536]{2,1,0:T(8,128)(2,1)S(1)}, u32[]{:S(2)}, u32[]{:S(2)}) collective-permute-start(bf16[4,16,1536]{2,1,0:T(8,128)(2,1)S(1)} %get-tuple-element.74), channel_id=1, source_target_pairs={{0,16},{2,18},{4,20},{6,22},{8,24},{10,26},{12,28},{14,30},{16,0},... | collective-permute-start | bytes 589832 | tf_op jit(solution)/shard_map/ppermute | solution.py:302
  18.7 1.5 %collective-permute-start.2 = (bf16[4,16,1536]{2,1,0:T(8,128)(2,1)S(1)}, bf16[4,16,1536]{2,1,0:T(8,128)(2,1)S(1)}, u32[]{:S(2)}, u32[]{:S(2)}) collective-permute-start(bf16[4,16,1536]{2,1,0:T(8,128)(2,1)S(1)} %get-tuple-element.73), channel_id=1, source_target_pairs={{0,24},{2,26},{4,28},{6,30},{8,0},{10,2},{12,4},{14,6},{16,8},{18,... | collective-permute-start | bytes 589832 | tf_op jit(solution)/shard_map/ppermute | solution.py:302
  20.1 1.7 %events.1 = (f32[16,1536]{1,0:T(8,128)S(1)}, f32[16,1536]{1,0:T(8,128)S(1)}, f32[16,1,128]{2,1,0:T(1,128)}) custom-call(s32[1]{0:T(128)} %bitcast.place_ref, f32[16,1536]{1,0:T(8,128)S(1)} %opens.1.local_ref, f32[16,16,128]{2,1,0:T(8,128)S(1)} %all-to-all-done.parts_ref, s32[16,1536]{1,0:T(8,128)S(1)} %copy-done.2), custom_call_target="tpu_custom_call" | custom-call | tf_op jit(solution)/shard_map/events/pallas_call | solution.py:262
  21.9 3.7 %all-to-all-start.1 = ((f32[16,1,128]{2,1,0:T(1,128)}), f32[16,1,128]{2,1,0:T(1,128)S(1)}, u32[]{:S(2)}, u32[]{:S(2)}) async-start(f32[16,1,128]{2,1,0:T(1,128)} %get-tuple-element.46), calls=%async_computation.1 | async-start | bytes 16384 | tf_op jit(solution)/shard_map/all_to_all | solution.py:349
  25.7 0.6 closes.1
  26.3 4.9 %collective-permute-done.1 = bf16[4,16,1536]{2,1,0:T(8,128)(2,1)S(1)} collective-permute-done((bf16[4,16,1536]{2,1,0:T(8,128)(2,1)S(1)}, bf16[4,16,1536]{2,1,0:T(8,128)(2,1)S(1)}, u32[]{:S(2)}, u32[]{:S(2)}) %collective-permute-start.1) | collective-permute-done | bytes 196640 | tf_op jit(solution)/shard_map/ppermute | solution.py:302
  31.2 6.1 %all-to-all-done.1.parts_ref = f32[16,1,128]{2,1,0:T(1,128)S(1)} async-done(((f32[16,1,128]{2,1,0:T(1,128)}), f32[16,1,128]{2,1,0:T(1,128)S(1)}, u32[]{:S(2)}, u32[]{:S(2)}) %all-to-all-start.1) | async-done | bytes 8224 | tf_op jit(solution)/shard_map/all_to_all | solution.py:349
  37.3 0.9 grads.1
  38.8 0.7 collective-permute-done.3
  39.5 1.8 %hist.6.refs_3_ = f32[16,128,128]{2,1,0:T(8,128)S(1)} custom-call(bf16[1,16,1536]{2,1,0:T(8,128)(2,1)S(1)} %constant_dynamic-slice_fusion.15.refs_0_, bf16[1,32,1536]{2,1,0:T(8,128)(2,1)S(1)} %bitcast.16, bf16[1,32,1536]{2,1,0:T(8,128)(2,1)S(1)} %bitcast.20), custom_call_target="tpu_custom_call" | custom-call | flops 3221225472 | bytes 245760 | tf_op jit(solution)/shard_map/hist/pallas_call | solution.py:242
  41.4 0.6 collective-permute-start.6
  42.1 1.5 %collective-permute-start.5 = (bf16[4,16,1536]{2,1,0:T(8,128)(2,1)S(1)}, bf16[4,16,1536]{2,1,0:T(8,128)(2,1)S(1)}, u32[]{:S(2)}, u32[]{:S(2)}) collective-permute-start(bf16[4,16,1536]{2,1,0:T(8,128)(2,1)S(1)} %pad_maximum_fusion.2), channel_id=1, source_target_pairs={{0,4},{2,6},{4,0},{6,2},{8,12},{10,14},{12,8},{14,10},{16,20},{18,... | collective-permute-start | bytes 589832 | tf_op jit(solution)/shard_map/ppermute | solution.py:314
  43.6 1.5 %collective-permute-start.4 = (bf16[4,16,1536]{2,1,0:T(8,128)(2,1)S(1)}, bf16[4,16,1536]{2,1,0:T(8,128)(2,1)S(1)}, u32[]{:S(2)}, u32[]{:S(2)}) collective-permute-start(bf16[4,16,1536]{2,1,0:T(8,128)(2,1)S(1)} %pad_maximum_fusion.1), channel_id=1, source_target_pairs={{0,2},{2,0},{4,6},{6,4},{8,10},{10,8},{12,14},{14,12},{16,18},{18,... | collective-permute-start | bytes 589832 | tf_op jit(solution)/shard_map/ppermute | solution.py:314
  45.2 0.7 collective-permute-start.8
  45.9 2.2 %collective-permute-start.9 = (bf16[32,1536]{1,0:T(8,128)(2,1)S(1)}, bf16[32,1536]{1,0:T(8,128)(2,1)S(1)}, u32[]{:S(2)}, u32[]{:S(2)}) collective-permute-start(bf16[32,1536]{1,0:T(8,128)(2,1)S(1)} %get-tuple-element.54), channel_id=1, source_target_pairs={{0,24},{2,26},{4,28},{6,30},{8,0},{10,2},{12,4},{14,6},{16,8},{18,... | collective-permute-start | bytes 294920 | tf_op jit(solution)/shard_map/ppermute | solution.py:309
  48.1 4.7 %collective-permute-done.8 = bf16[32,1536]{1,0:T(8,128)(2,1)S(1)} collective-permute-done((bf16[32,1536]{1,0:T(8,128)(2,1)S(1)}, bf16[32,1536]{1,0:T(8,128)(2,1)S(1)}, u32[]{:S(2)}, u32[]{:S(2)}) %collective-permute-start.8) | collective-permute-done | bytes 98336 | tf_op jit(solution)/shard_map/ppermute | solution.py:309
  53.2 1.1 %collective-permute-start.11 = (bf16[4,32,1536]{2,1,0:T(8,128)(2,1)S(1)}, bf16[4,32,1536]{2,1,0:T(8,128)(2,1)S(1)}, u32[]{:S(2)}, u32[]{:S(2)}) collective-permute-start(bf16[4,32,1536]{2,1,0:T(8,128)(2,1)S(1)} %pad_maximum_fusion), channel_id=1, source_target_pairs={{0,2},{2,0},{4,6},{6,4},{8,10},{10,8},{12,14},{14,12},{16,18},{18,... | collective-permute-start | bytes 1179656 | tf_op jit(solution)/shard_map/ppermute | solution.py:320
  55.0 3.8 %hist.7.refs_3_ = f32[16,128,128]{2,1,0:T(8,128)S(1)} custom-call(bf16[2,16,1536]{2,1,0:T(8,128)(2,1)S(1)} %pad_maximum_fusion.5.refs_0_, bf16[2,32,1536]{2,1,0:T(8,128)(2,1)S(1)} %pad_maximum_fusion.4.refs_1_, bf16[2,32,1536]{2,1,0:T(8,128)(2,1)S(1)} %slice.10.refs_2_, f32[16,128,128]{2,1,0:T(8,128)S(1)} %hist.6.refs_3_), custom_call_target="tpu_custom_call", output_to_operand_aliasing={{}: (3, {})} | custom-call | flops 6442450944 | bytes 491520 | tf_op jit(solution)/shard_map/hist/pallas_call | solution.py:242
  58.8 6.0 %collective-permute-done.11.refs_1_ = bf16[4,32,1536]{2,1,0:T(8,128)(2,1)S(1)} collective-permute-done((bf16[4,32,1536]{2,1,0:T(8,128)(2,1)S(1)}, bf16[4,32,1536]{2,1,0:T(8,128)(2,1)S(1)}, u32[]{:S(2)}, u32[]{:S(2)}) %collective-permute-start.11) | collective-permute-done | bytes 393248 | tf_op jit(solution)/shard_map/ppermute | solution.py:320
  64.8 1.1 %collective-permute-start.10 = (bf16[4,32,1536]{2,1,0:T(8,128)(2,1)S(1)}, bf16[4,32,1536]{2,1,0:T(8,128)(2,1)S(1)}, u32[]{:S(2)}, u32[]{:S(2)}) collective-permute-start(bf16[4,32,1536]{2,1,0:T(8,128)(2,1)S(1)} %pad_maximum_fusion), channel_id=1, source_target_pairs={{0,6},{2,4},{4,2},{6,0},{8,14},{10,12},{12,10},{14,8},{16,22},{18,... | collective-permute-start | bytes 1179656 | tf_op jit(solution)/shard_map/ppermute | solution.py:320
  65.9 1.9 %hist.8.refs_3_ = f32[16,128,128]{2,1,0:T(8,128)S(1)} custom-call(bf16[1,16,1536]{2,1,0:T(8,128)(2,1)S(1)} %get-tuple-element.77.refs_0_, bf16[1,32,1536]{2,1,0:T(8,128)(2,1)S(1)} %bitcast.19, bf16[1,32,1536]{2,1,0:T(8,128)(2,1)S(1)} %slice.11.refs_2_, f32[16,128,128]{2,1,0:T(8,128)S(1)} %hist.7.refs_3_), custom_call_target="tpu_custom_call", output_to_operand_aliasing={{}: (3, {})} | custom-call | flops 3221225472 | bytes 245760 | tf_op jit(solution)/shard_map/hist/pallas_call | solution.py:242
  68.1 7.4 %hist.9.refs_3_ = f32[16,128,128]{2,1,0:T(8,128)S(1)} custom-call(bf16[4,16,1536]{2,1,0:T(8,128)(2,1)S(1)} %collective-permute-done.4.refs_0_, bf16[4,32,1536]{2,1,0:T(8,128)(2,1)S(1)} %collective-permute-done.11.refs_1_, bf16[4,32,1536]{2,1,0:T(8,128)(2,1)S(1)} %collective-permute-done.13.refs_2_, ...), custom_call_target="tpu_custom_call", output_to_operand_aliasing={{}: (3, {})} | custom-call | flops 12884901888 | bytes 983040 | tf_op jit(solution)/shard_map/hist/pallas_call | solution.py:242
  75.5 1.7 %collective-permute-done.10.refs_1_ = bf16[4,32,1536]{2,1,0:T(8,128)(2,1)S(1)} collective-permute-done((bf16[4,32,1536]{2,1,0:T(8,128)(2,1)S(1)}, bf16[4,32,1536]{2,1,0:T(8,128)(2,1)S(1)}, u32[]{:S(2)}, u32[]{:S(2)}) %collective-permute-start.10) | collective-permute-done | bytes 393248 | tf_op jit(solution)/shard_map/ppermute | solution.py:320
  77.2 7.4 %hist.10.refs_3_ = f32[16,128,128]{2,1,0:T(8,128)S(1)} custom-call(bf16[4,16,1536]{2,1,0:T(8,128)(2,1)S(1)} %collective-permute-done.5.refs_0_, bf16[4,32,1536]{2,1,0:T(8,128)(2,1)S(1)} %collective-permute-done.14.refs_1_, bf16[4,32,1536]{2,1,0:T(8,128)(2,1)S(1)} %collective-permute-done.16.refs_2_, ...), custom_call_target="tpu_custom_call", output_to_operand_aliasing={{}: (3, {})} | custom-call | flops 12884901888 | bytes 983040 | tf_op jit(solution)/shard_map/hist/pallas_call | solution.py:242
  84.6 9.1 %hist.11 = f32[16,256]{1,0:T(8,128)} custom-call(bf16[4,16,1536]{2,1,0:T(8,128)(2,1)S(1)} %collective-permute-done.6.refs_0_, bf16[4,32,1536]{2,1,0:T(8,128)(2,1)S(1)} %collective-permute-done.10.refs_1_, bf16[4,32,1536]{2,1,0:T(8,128)(2,1)S(1)} %collective-permute-done.15.refs_2_, f32[16,128,128]{2,1,0:T(8,128)S(1)} %hist.10.refs_3_), custom_call_target="tpu_custom_call" | custom-call | flops 12884901888 | bytes 983040 | tf_op jit(solution)/shard_map/hist/pallas_call | solution.py:242
  (42 shorter events, 2.1 us)
Async XLA Ops:
  0.6 0.9 copy-start
  3.0 17.2 %all-to-all-start = ((f32[16,16,128]{2,1,0:T(8,128)}), f32[16,16,128]{2,1,0:T(8,128)S(1)}, u32[]{:S(2)}, u32[]{:S(2)}) async-start(f32[16,16,128]{2,1,0:T(8,128)} %get-tuple-element.40), calls=%async_computation | async-start | bytes 262144 | tf_op jit(solution)/shard_map/all_to_all | solution.py:349
  11.4 0.7 copy-start.3
  12.7 7.4 %copy-start.2 = (s32[16,1536]{1,0:T(8,128)S(1)}, s32[16,1536]{1,0:T(8,128)}, u32[]{:S(2)}) copy-start(s32[16,1536]{1,0:T(8,128)} %events_ref.3) | copy-start | bytes 294916
  14.3 11.4 %copy-start.4 = (s32[1536]{0:T(1024)S(1)}, s32[1536]{0:T(1024)}, u32[]{:S(2)}) copy-start(s32[1536]{0:T(1024)} %tie_ref.3) | copy-start | bytes 18436
  14.3 23.0 %copy-start.1 = (f32[16,1536]{1,0:T(8,128)S(1)}, f32[16,1536]{1,0:T(8,128)}, u32[]{:S(2)}) copy-start(f32[16,1536]{1,0:T(8,128)} %margins_ref.3) | copy-start | bytes 294916
  14.3 23.0 %copy-start.5 = (s32[1536]{0:T(1024)S(1)}, s32[1536]{0:T(1024)}, u32[]{:S(2)}) copy-start(s32[1536]{0:T(1024)} %node_ref.1) | copy-start | bytes 18436
  14.4 11.9 %collective-permute-start = (bf16[4,16,1536]{2,1,0:T(8,128)(2,1)S(1)}, bf16[4,16,1536]{2,1,0:T(8,128)(2,1)S(1)}, u32[]{:S(2)}, u32[]{:S(2)}) collective-permute-start(bf16[4,16,1536]{2,1,0:T(8,128)(2,1)S(1)} %get-tuple-element.75), channel_id=1, source_target_pairs={{0,8},{2,10},{4,12},{6,14},{8,16},{10,18},{12,20},{14,22},{16,24},... | collective-permute-start | bytes 589832 | tf_op jit(solution)/shard_map/ppermute | solution.py:302
  16.3 14.9 %collective-permute-start.1 = (bf16[4,16,1536]{2,1,0:T(8,128)(2,1)S(1)}, bf16[4,16,1536]{2,1,0:T(8,128)(2,1)S(1)}, u32[]{:S(2)}, u32[]{:S(2)}) collective-permute-start(bf16[4,16,1536]{2,1,0:T(8,128)(2,1)S(1)} %get-tuple-element.74), channel_id=1, source_target_pairs={{0,16},{2,18},{4,20},{6,22},{8,24},{10,26},{12,28},{14,30},{16,0},... | collective-permute-start | bytes 589832 | tf_op jit(solution)/shard_map/ppermute | solution.py:302
  18.7 12.5 %collective-permute-start.2 = (bf16[4,16,1536]{2,1,0:T(8,128)(2,1)S(1)}, bf16[4,16,1536]{2,1,0:T(8,128)(2,1)S(1)}, u32[]{:S(2)}, u32[]{:S(2)}) collective-permute-start(bf16[4,16,1536]{2,1,0:T(8,128)(2,1)S(1)} %get-tuple-element.73), channel_id=1, source_target_pairs={{0,24},{2,26},{4,28},{6,30},{8,0},{10,2},{12,4},{14,6},{16,8},{18,... | collective-permute-start | bytes 589832 | tf_op jit(solution)/shard_map/ppermute | solution.py:302
  21.9 15.4 %all-to-all-start.1 = ((f32[16,1,128]{2,1,0:T(1,128)}), f32[16,1,128]{2,1,0:T(1,128)S(1)}, u32[]{:S(2)}, u32[]{:S(2)}) async-start(f32[16,1,128]{2,1,0:T(1,128)} %get-tuple-element.46), calls=%async_computation.1 | async-start | bytes 16384 | tf_op jit(solution)/shard_map/all_to_all | solution.py:349
  38.2 1.3 %collective-permute-start.3 = (bf16[32,1536]{1,0:T(8,128)(2,1)S(1)}, bf16[32,1536]{1,0:T(8,128)(2,1)S(1)}, u32[]{:S(2)}, u32[]{:S(2)}) collective-permute-start(bf16[32,1536]{1,0:T(8,128)(2,1)S(1)} %get-tuple-element.54), channel_id=1, source_target_pairs={{0,1},{1,0},{2,3},{3,2},{4,5},{5,4},{6,7},{7,6},{8,9},{9,8},{10,11... | collective-permute-start | bytes 294920 | tf_op jit(solution)/shard_map/ppermute | solution.py:289
  38.2 7.7 %collective-permute-start.7 = (bf16[32,1536]{1,0:T(8,128)(2,1)S(1)}, bf16[32,1536]{1,0:T(8,128)(2,1)S(1)}, u32[]{:S(2)}, u32[]{:S(2)}) collective-permute-start(bf16[32,1536]{1,0:T(8,128)(2,1)S(1)} %get-tuple-element.54), channel_id=1, source_target_pairs={{0,8},{2,10},{4,12},{6,14},{8,16},{10,18},{12,20},{14,22},{16,24},... | collective-permute-start | bytes 294920 | tf_op jit(solution)/shard_map/ppermute | solution.py:309
  41.4 11.4 %collective-permute-start.6 = (bf16[4,16,1536]{2,1,0:T(8,128)(2,1)S(1)}, bf16[4,16,1536]{2,1,0:T(8,128)(2,1)S(1)}, u32[]{:S(2)}, u32[]{:S(2)}) collective-permute-start(bf16[4,16,1536]{2,1,0:T(8,128)(2,1)S(1)} %pad_maximum_fusion.3), channel_id=1, source_target_pairs={{0,6},{2,4},{4,2},{6,0},{8,14},{10,12},{12,10},{14,8},{16,22},{18,... | collective-permute-start | bytes 589832 | tf_op jit(solution)/shard_map/ppermute | solution.py:314
  42.1 11.0 %collective-permute-start.5 = (bf16[4,16,1536]{2,1,0:T(8,128)(2,1)S(1)}, bf16[4,16,1536]{2,1,0:T(8,128)(2,1)S(1)}, u32[]{:S(2)}, u32[]{:S(2)}) collective-permute-start(bf16[4,16,1536]{2,1,0:T(8,128)(2,1)S(1)} %pad_maximum_fusion.2), channel_id=1, source_target_pairs={{0,4},{2,6},{4,0},{6,2},{8,12},{10,14},{12,8},{14,10},{16,20},{18,... | collective-permute-start | bytes 589832 | tf_op jit(solution)/shard_map/ppermute | solution.py:314
  43.6 9.4 %collective-permute-start.4 = (bf16[4,16,1536]{2,1,0:T(8,128)(2,1)S(1)}, bf16[4,16,1536]{2,1,0:T(8,128)(2,1)S(1)}, u32[]{:S(2)}, u32[]{:S(2)}) collective-permute-start(bf16[4,16,1536]{2,1,0:T(8,128)(2,1)S(1)} %pad_maximum_fusion.1), channel_id=1, source_target_pairs={{0,2},{2,0},{4,6},{6,4},{8,10},{10,8},{12,14},{14,12},{16,18},{18,... | collective-permute-start | bytes 589832 | tf_op jit(solution)/shard_map/ppermute | solution.py:314
  45.2 7.7 %collective-permute-start.8 = (bf16[32,1536]{1,0:T(8,128)(2,1)S(1)}, bf16[32,1536]{1,0:T(8,128)(2,1)S(1)}, u32[]{:S(2)}, u32[]{:S(2)}) collective-permute-start(bf16[32,1536]{1,0:T(8,128)(2,1)S(1)} %get-tuple-element.54), channel_id=1, source_target_pairs={{0,16},{2,18},{4,20},{6,22},{8,24},{10,26},{12,28},{14,30},{16,0},... | collective-permute-start | bytes 294920 | tf_op jit(solution)/shard_map/ppermute | solution.py:309
  45.9 6.9 %collective-permute-start.9 = (bf16[32,1536]{1,0:T(8,128)(2,1)S(1)}, bf16[32,1536]{1,0:T(8,128)(2,1)S(1)}, u32[]{:S(2)}, u32[]{:S(2)}) collective-permute-start(bf16[32,1536]{1,0:T(8,128)(2,1)S(1)} %get-tuple-element.54), channel_id=1, source_target_pairs={{0,24},{2,26},{4,28},{6,30},{8,0},{10,2},{12,4},{14,6},{16,8},{18,... | collective-permute-start | bytes 294920 | tf_op jit(solution)/shard_map/ppermute | solution.py:309
  53.1 1.9 %collective-permute-start.12 = (bf16[4,32,1536]{2,1,0:T(8,128)(2,1)S(1)}, bf16[4,32,1536]{2,1,0:T(8,128)(2,1)S(1)}, u32[]{:S(2)}, u32[]{:S(2)}) collective-permute-start(bf16[4,32,1536]{2,1,0:T(8,128)(2,1)S(1)} %pad_maximum_fusion), channel_id=1, source_target_pairs={{0,1},{1,0},{2,3},{3,2},{4,5},{5,4},{6,7},{7,6},{8,9},{9,8},{10,11... | collective-permute-start | bytes 1179656 | tf_op jit(solution)/shard_map/ppermute | solution.py:289
  53.2 11.6 %collective-permute-start.11 = (bf16[4,32,1536]{2,1,0:T(8,128)(2,1)S(1)}, bf16[4,32,1536]{2,1,0:T(8,128)(2,1)S(1)}, u32[]{:S(2)}, u32[]{:S(2)}) collective-permute-start(bf16[4,32,1536]{2,1,0:T(8,128)(2,1)S(1)} %pad_maximum_fusion), channel_id=1, source_target_pairs={{0,2},{2,0},{4,6},{6,4},{8,10},{10,8},{12,14},{14,12},{16,18},{18,... | collective-permute-start | bytes 1179656 | tf_op jit(solution)/shard_map/ppermute | solution.py:320
  54.3 13.4 %collective-permute-start.14 = (bf16[4,32,1536]{2,1,0:T(8,128)(2,1)S(1)}, bf16[4,32,1536]{2,1,0:T(8,128)(2,1)S(1)}, u32[]{:S(2)}, u32[]{:S(2)}) collective-permute-start(bf16[4,32,1536]{2,1,0:T(8,128)(2,1)S(1)} %pad_maximum_fusion), channel_id=1, source_target_pairs={{0,4},{2,6},{4,0},{6,2},{8,12},{10,14},{12,8},{14,10},{16,20},{18,... | collective-permute-start | bytes 1179656 | tf_op jit(solution)/shard_map/ppermute | solution.py:320
  64.8 3.3 %collective-permute-start.13 = (bf16[4,32,1536]{2,1,0:T(8,128)(2,1)S(1)}, bf16[4,32,1536]{2,1,0:T(8,128)(2,1)S(1)}, u32[]{:S(2)}, u32[]{:S(2)}) collective-permute-start(bf16[4,32,1536]{2,1,0:T(8,128)(2,1)S(1)} %collective-permute-done.11.refs_1_), channel_id=1, source_target_pairs={{0,1},{1,0},{2,3},{3,2},{4,5},{5,4},{6,7},{7,6},{8,9},{9,8},{10,11... | collective-permute-start | bytes 1179656 | tf_op jit(solution)/shard_map/ppermute | solution.py:289
  64.8 12.4 %collective-permute-start.10 = (bf16[4,32,1536]{2,1,0:T(8,128)(2,1)S(1)}, bf16[4,32,1536]{2,1,0:T(8,128)(2,1)S(1)}, u32[]{:S(2)}, u32[]{:S(2)}) collective-permute-start(bf16[4,32,1536]{2,1,0:T(8,128)(2,1)S(1)} %pad_maximum_fusion), channel_id=1, source_target_pairs={{0,6},{2,4},{4,2},{6,0},{8,14},{10,12},{12,10},{14,8},{16,22},{18,... | collective-permute-start | bytes 1179656 | tf_op jit(solution)/shard_map/ppermute | solution.py:320
  67.8 9.4 %collective-permute-start.16 = (bf16[4,32,1536]{2,1,0:T(8,128)(2,1)S(1)}, bf16[4,32,1536]{2,1,0:T(8,128)(2,1)S(1)}, u32[]{:S(2)}, u32[]{:S(2)}) collective-permute-start(bf16[4,32,1536]{2,1,0:T(8,128)(2,1)S(1)} %collective-permute-done.14.refs_1_), channel_id=1, source_target_pairs={{0,1},{1,0},{2,3},{3,2},{4,5},{5,4},{6,7},{7,6},{8,9},{9,8},{10,11... | collective-permute-start | bytes 1179656 | tf_op jit(solution)/shard_map/ppermute | solution.py:289
  77.2 7.4 %collective-permute-start.15 = (bf16[4,32,1536]{2,1,0:T(8,128)(2,1)S(1)}, bf16[4,32,1536]{2,1,0:T(8,128)(2,1)S(1)}, u32[]{:S(2)}, u32[]{:S(2)}) collective-permute-start(bf16[4,32,1536]{2,1,0:T(8,128)(2,1)S(1)} %collective-permute-done.10.refs_1_), channel_id=1, source_target_pairs={{0,1},{1,0},{2,3},{3,2},{4,5},{5,4},{6,7},{7,6},{8,9},{9,8},{10,11... | collective-permute-start | bytes 1179656 | tf_op jit(solution)/shard_map/ppermute | solution.py:289

commit v4 on v3

--- a/solution.py
+++ b/solution.py
@@ -171,7 +171,7 @@
     pair_ref[endpoints:] = jnp.where(chosen, hess, 0.0).astype(bf16)
 
 
-def add_block(codes, pairs, sums_ref, feature_count):
+def add_block(codes, pairs, sums_ref, feature_count, finish=None):
     length = pairs.shape[1]
     level = lax.broadcasted_iota(jnp.int32, (HALF, length), 0).astype(bf16)
     nothing = jnp.zeros_like(pairs)
@@ -182,10 +182,15 @@
         up = jnp.broadcast_to(high[f : f + 1], pairs.shape) == bf16(1)
         left = jnp.concatenate([jnp.where(up, nothing, pairs), jnp.where(up, pairs, nothing)], axis=0)
         reach = jnp.where(level >= low[f : f + 1], bf16(1), bf16(0))
-        sums_ref[f] += lax.dot_general(left, reach, NT, preferred_element_type=f32)
-
-
-def write_gain(sums_ref, gain_ref, feature_count, channels):
+        sums = sums_ref[f] + lax.dot_general(left, reach, NT, preferred_element_type=f32)
+        if finish is None:
+            sums_ref[f] = sums
+        else:
+            finish(f, sums)
+
+
+def write_gain(gain_ref, f, sums):
+    channels = sums.shape[0] // 2
     quarter = channels // 4
 
     def part(x):
@@ -193,15 +198,13 @@
         hess = jnp.concatenate([x[quarter : 2 * quarter], x[3 * quarter :]], axis=0)
         return grad * grad / (hess + 1.0)
 
-    for f in range(feature_count):
-        lower = sums_ref[f, 0:channels]
-        under = lower[:, HALF - 1 :]
-        uppers = sums_ref[f, channels:] + under
-        whole = uppers[:, HALF - 1 :]
-        whole_part = part(whole)
-        for side, left in enumerate((lower, uppers)):
-            value = part(left) + part(whole - left) - whole_part
-            gain_ref[f : f + 1, side * HALF : (side + 1) * HALF] = jnp.mean(value, axis=0, keepdims=True)
+    lower = sums[0:channels]
+    uppers = sums[channels:] + lower[:, HALF - 1 :]
+    whole = uppers[:, HALF - 1 :]
+    whole_part = part(whole)
+    for side, left in enumerate((lower, uppers)):
+        value = part(left) + part(whole - left) - whole_part
+        gain_ref[f : f + 1, side * HALF : (side + 1) * HALF] = jnp.mean(value, axis=0, keepdims=True)
 
 
 def hist_kernel(blocks, feature_count, first, last, *refs):
@@ -217,12 +220,17 @@
         sums_ref[...] = jnp.zeros_like(sums_ref) if first else before_ref[...]
 
     pairs = jnp.concatenate([mine_ref[0], other_ref[0]], axis=0)
-    add_block(codes_ref[0], pairs, sums_ref, feature_count)
-    if last:
-
-        @pl.when(block == blocks - 1)
-        def _():
-            write_gain(sums_ref, outs[0], feature_count, pairs.shape[0])
+    if not last:
+        add_block(codes_ref[0], pairs, sums_ref, feature_count)
+        return
+
+    @pl.when(block < blocks - 1)
+    def _():
+        add_block(codes_ref[0], pairs, sums_ref, feature_count)
+
+    @pl.when(block == blocks - 1)
+    def _():
+        add_block(codes_ref[0], pairs, sums_ref, feature_count, functools.partial(write_gain, outs[0]))
 
 
 def histogram(codes, mine, other, before, last):
@@ -303,33 +311,32 @@
     return held
 
 
-def spread(held, pairs, devices):
+def spread(held, plane, pairs, devices):
     planes = devices // 4
     here = lax.axis_index("tm") % 4
     column = [lax.ppermute(pairs, "tm", ring(devices, d)) for d in range(1, planes)]
-    sums = histogram(pick(held[0], here, 0)[None], pairs[None], swap(pairs)[None], None, False)
-    held, sums = lax.optimization_barrier((held, sums))
+    beside = [lax.ppermute(pairs, "tm", flip(devices, d)) for d in range(1, 3)]
+    own = pick(held[0], here, 0)
     near = jnp.stack([pick(h, here, 0) for h in held[1:]])
     far = [
-        lax.ppermute(jnp.stack([pick(h, here ^ d, 0) for h in held]), "tm", flip(devices, d))
+        lax.ppermute(jnp.stack([pick(h, here ^ d, 0) for h in (held if d == 3 else held[1:])]), "tm", flip(devices, d))
         for d in range(1, 4)
     ]
-    far, *column, sums = lax.optimization_barrier((far, *column, sums))
-    column = jnp.stack([pairs] + column)
+    *column, pairs = lax.optimization_barrier((*column, pairs))
+    column_sent = jnp.stack(column)
+    there = [lax.ppermute(column_sent, "tm", flip(devices, d)) for d in range(1, 3)]
+    there.append(lax.ppermute(jnp.stack([pairs] + column), "tm", flip(devices, 3)))
+    column = column_sent
     other = swap(column)
-    there = [lax.ppermute(column, "tm", flip(devices, d)) for d in range(1, 4)]
+    beside = jnp.stack([pairs] + beside)
+    sums = histogram(jnp.stack([own] + plane), beside, swap(beside), None, False)
     cut = planes - 2
-    sums = histogram(near[:cut], column[1 : cut + 1], other[1 : cut + 1], sums, False)
+    sums = histogram(near[:cut], column[:cut], other[:cut], sums, False)
     there[0], sums = lax.optimization_barrier((there[0], sums))
-    back = swap(there[0])
-    sums = histogram(near[cut:], column[cut + 1 :], other[cut + 1 :], sums, False)
+    back = [swap(x) for x in there]
+    sums = histogram(near[cut:], column[cut:], other[cut:], sums, False)
     for d in range(1, 4):
-        mine = there[d - 1]
-        now = back
-        if d < 3:
-            there[d], sums = lax.optimization_barrier((there[d], sums))
-            back = swap(there[d])
-        sums = histogram(far[d - 1], mine, now, sums, d == 3)
+        sums = histogram(far[d - 1], there[d - 1], back[d - 1], sums, d == 3)
     return sums
 
 
@@ -363,13 +370,19 @@
         here, local, parts, events, place=True,
     )
     parts = exchange(total)
+    if blocked:
+        column = lax.axis_index("tm") % 4
+        aside, second = lax.optimization_barrier((codes[0], second))
+        plane = [lax.ppermute(pick(aside, column ^ d, 0), "tm", flip(devices, d)) for d in range(1, 3)]
     first, second = call(close_kernel, (rows, rows), "closes", first, second, tie_group)
     codes, parts = lax.optimization_barrier((codes, parts))
     grad, hess, pairs = call(
         grad_kernel, (narrow, narrow, shape(2 * endpoints, length, dtype=bf16)), "grads",
         here, margins, events, in_node, first, second, parts, place=True,
     )
-    gain = spread(codes, pairs, devices) if blocked else spread_any(codes, pairs)
+    if blocked:
+        plane, pairs = lax.optimization_barrier((plane, pairs))
+    gain = spread(codes, plane, pairs, devices) if blocked else spread_any(codes, pairs)
     return (grad, hess, gain[None])
 
 

time: 94.1 us -> 89.8 us (0.954)
  waiting for transfers between devices: 24.3 us -> 14.9 us
  starting transfers between devices: 28.2 us -> 33.8 us
    ppermute x6 -> x10, waiting for transfers between devices: 7.86 us -> 1.7 us  [the longest x2 1.68 us: spread(): lax.ppermute(column_sent, 'tm', flip(devices, d))]
    ppermute x6 -> x10, starting transfers between devices: 6.55 us -> 10.8 us  [the longest x2 3.44 us: on_device(): lax.ppermute(pick(aside, column ^ d, 0), 'tm', flip(devices, d))]
    ppermute x3, waiting for transfers between devices: 4.88 us -> 1.32 us  [send_planes(): lax.ppermute(pick(codes, (plane + d) % planes, 0), 'tm', ring(devices, d))]
  transfers between devices with their start and end apart: 19 -> 23, of which waited for: 7 -> 6; matrix products, arithmetic and copies ran while one was open for 2% -> 2% of each run, Pallas kernels for 27% -> 29%
where the time goes in v4:
time: 89.8 us; the launch traced here: 89.4 us
  Pallas kernels  36.1 us (40%)
  starting transfers between devices  33.8 us (38%)
  waiting for transfers between devices  14.9 us (17%)
  other arithmetic  1.79 us (2%)
  local copies, waits for them, and re-layouts  1.77 us (2%)
  between operations  1.06 us (1%)
    pallas_call x6, Pallas kernels, histogram(): pl.pallas_call(functools.partial(hist_kernel, blocks, feature_count, befo...  30.8 us
    all_to_all x2, starting transfers between devices, exchange(): return lax.all_to_all(total, 'tm', 0, 0)  12.2 us
    all_to_all x2, waiting for transfers between devices, exchange(): return lax.all_to_all(total, 'tm', 0, 0)  6.1 us
    ppermute x3, starting transfers between devices, send_planes(): lax.ppermute(pick(codes, (plane + d) % planes, 0), 'tm', ring(devices, d))  5.72 us
    pallas_call x5, Pallas kernels, call(): pl.pallas_call(kernel, out_shape=out_shape, in_specs=([SMEM] if place els...  5.32 us
    ppermute x3, waiting for transfers between devices, spread(): lax.ppermute(pairs, 'tm', ring(devices, d))  5.04 us
    ppermute x3, starting transfers between devices, spread(): lax.ppermute(pairs, 'tm', ring(devices, d))  3.87 us
    ppermute x2, starting transfers between devices, on_device(): lax.ppermute(pick(aside, column ^ d, 0), 'tm', flip(devices, d))  3.44 us
  transfers between devices with their start and end apart: 23, of which 6 were waited for; matrix products, arithmetic and copies ran while one was open for 2% of the time, Pallas kernels for 29%

profile of v4, /device:TPU:0, one launch (start us, length us, event | category | flops | bytes accessed | tf_op | source)
XLA Modules:
  0.0 89.4 jit_solution(15836346315670080848)
XLA Ops:
  0.6 0.9 copy-done
  1.5 1.4 %risk.1 = (f32[16,1536]{1,0:T(8,128)S(1)}, f32[16,16,128]{2,1,0:T(8,128)}) custom-call(f32[16,1536]{1,0:T(8,128)S(1)} %copy-done), custom_call_target="tpu_custom_call" | custom-call | tf_op jit(solution)/shard_map/risk/pallas_call | solution.py:270
  3.0 8.3 %all-to-all-start = ((f32[16,16,128]{2,1,0:T(8,128)}), f32[16,16,128]{2,1,0:T(8,128)S(1)}, u32[]{:S(2)}, u32[]{:S(2)}) async-start(f32[16,16,128]{2,1,0:T(8,128)} %get-tuple-element.33), calls=%async_computation | async-start | bytes 262144 | tf_op jit(solution)/shard_map/all_to_all | solution.py:356
  11.4 0.7 copy-done.3
  12.1 0.7 opens.1.local_ref
  12.7 1.5 %convert_element_type.3 = bf16[256,1536]{1,0:T(8,128)(2,1)S(1)} convert(s32[256,1536]{1,0:T(8,128)} %param.9) | non-fusion elementwise | flops 393216 | bytes 2359296 | tf_op jit(solution)/shard_map/convert_element_type | solution.py:362
  14.4 1.9 %collective-permute-start = (bf16[4,16,1536]{2,1,0:T(8,128)(2,1)S(1)}, bf16[4,16,1536]{2,1,0:T(8,128)(2,1)S(1)}, u32[]{:S(2)}, u32[]{:S(2)}) collective-permute-start(bf16[4,16,1536]{2,1,0:T(8,128)(2,1)S(1)} %get-tuple-element.61), channel_id=1, source_target_pairs={{0,8},{2,10},{4,12},{6,14},{8,16},{10,18},{12,20},{14,22},{16,24},... | collective-permute-start | bytes 589832 | tf_op jit(solution)/shard_map/ppermute | solution.py:310
  16.3 2.4 %collective-permute-start.1 = (bf16[4,16,1536]{2,1,0:T(8,128)(2,1)S(1)}, bf16[4,16,1536]{2,1,0:T(8,128)(2,1)S(1)}, u32[]{:S(2)}, u32[]{:S(2)}) collective-permute-start(bf16[4,16,1536]{2,1,0:T(8,128)(2,1)S(1)} %get-tuple-element.60), channel_id=1, source_target_pairs={{0,16},{2,18},{4,20},{6,22},{8,24},{10,26},{12,28},{14,30},{16,0},... | collective-permute-start | bytes 589832 | tf_op jit(solution)/shard_map/ppermute | solution.py:310
  18.6 1.5 %collective-permute-start.2 = (bf16[4,16,1536]{2,1,0:T(8,128)(2,1)S(1)}, bf16[4,16,1536]{2,1,0:T(8,128)(2,1)S(1)}, u32[]{:S(2)}, u32[]{:S(2)}) collective-permute-start(bf16[4,16,1536]{2,1,0:T(8,128)(2,1)S(1)} %get-tuple-element.59), channel_id=1, source_target_pairs={{0,24},{2,26},{4,28},{6,30},{8,0},{10,2},{12,4},{14,6},{16,8},{18,... | collective-permute-start | bytes 589832 | tf_op jit(solution)/shard_map/ppermute | solution.py:310
  20.1 1.7 %events.1 = (f32[16,1536]{1,0:T(8,128)S(1)}, f32[16,1536]{1,0:T(8,128)S(1)}, f32[16,1,128]{2,1,0:T(1,128)}) custom-call(s32[1]{0:T(128)} %bitcast.place_ref, f32[16,1536]{1,0:T(8,128)S(1)} %opens.1.local_ref, f32[16,16,128]{2,1,0:T(8,128)S(1)} %all-to-all-done.parts_ref, s32[16,1536]{1,0:T(8,128)S(1)} %copy-done.2), custom_call_target="tpu_custom_call" | custom-call | tf_op jit(solution)/shard_map/events/pallas_call | solution.py:270
  21.8 3.9 %all-to-all-start.1 = ((f32[16,1,128]{2,1,0:T(1,128)}), f32[16,1,128]{2,1,0:T(1,128)S(1)}, u32[]{:S(2)}, u32[]{:S(2)}) async-start(f32[16,1,128]{2,1,0:T(1,128)} %get-tuple-element.40), calls=%async_computation.1 | async-start | bytes 16384 | tf_op jit(solution)/shard_map/all_to_all | solution.py:356
  25.7 2.0 %collective-permute-start.4 = (bf16[16,1536]{1,0:T(8,128)(2,1)S(1)}, bf16[16,1536]{1,0:T(8,128)(2,1)S(1)}, u32[]{:S(2)}, u32[]{:S(2)}) collective-permute-start(bf16[16,1536]{1,0:T(8,128)(2,1)S(1)} %get-tuple-element.78), channel_id=1, source_target_pairs={{0,2},{2,0},{4,6},{6,4},{8,10},{10,8},{12,14},{14,12},{16,18},{18,... | collective-permute-start | bytes 147464 | tf_op jit(solution)/shard_map/ppermute | solution.py:376
  27.7 1.5 %collective-permute-start.5 = (bf16[16,1536]{1,0:T(8,128)(2,1)S(1)}, bf16[16,1536]{1,0:T(8,128)(2,1)S(1)}, u32[]{:S(2)}, u32[]{:S(2)}) collective-permute-start(bf16[16,1536]{1,0:T(8,128)(2,1)S(1)} %get-tuple-element.77), channel_id=1, source_target_pairs={{0,4},{2,6},{4,0},{6,2},{8,12},{10,14},{12,8},{14,10},{16,20},{18,... | collective-permute-start | bytes 147464 | tf_op jit(solution)/shard_map/ppermute | solution.py:376
  29.2 0.6 closes.1
  29.8 1.3 %collective-permute-done.1 = bf16[4,16,1536]{2,1,0:T(8,128)(2,1)S(1)} collective-permute-done((bf16[4,16,1536]{2,1,0:T(8,128)(2,1)S(1)}, bf16[4,16,1536]{2,1,0:T(8,128)(2,1)S(1)}, u32[]{:S(2)}, u32[]{:S(2)}) %collective-permute-start.1) | collective-permute-done | bytes 196640 | tf_op jit(solution)/shard_map/ppermute | solution.py:310
  31.2 6.1 %all-to-all-done.1.parts_ref = f32[16,1,128]{2,1,0:T(1,128)S(1)} async-done(((f32[16,1,128]{2,1,0:T(1,128)}), f32[16,1,128]{2,1,0:T(1,128)S(1)}, u32[]{:S(2)}, u32[]{:S(2)}) %all-to-all-start.1) | async-done | bytes 8224 | tf_op jit(solution)/shard_map/all_to_all | solution.py:356
  37.5 0.9 grads.1
  39.0 1.5 %collective-permute-start.7 = (bf16[32,1536]{1,0:T(8,128)(2,1)S(1)}, bf16[32,1536]{1,0:T(8,128)(2,1)S(1)}, u32[]{:S(2)}, u32[]{:S(2)}) collective-permute-start(bf16[32,1536]{1,0:T(8,128)(2,1)S(1)} %get-tuple-element.51), channel_id=1, source_target_pairs={{0,16},{2,18},{4,20},{6,22},{8,24},{10,26},{12,28},{14,30},{16,0},... | collective-permute-start | bytes 294920 | tf_op jit(solution)/shard_map/ppermute | solution.py:317
  40.4 1.8 %collective-permute-start.8 = (bf16[32,1536]{1,0:T(8,128)(2,1)S(1)}, bf16[32,1536]{1,0:T(8,128)(2,1)S(1)}, u32[]{:S(2)}, u32[]{:S(2)}) collective-permute-start(bf16[32,1536]{1,0:T(8,128)(2,1)S(1)} %get-tuple-element.51), channel_id=1, source_target_pairs={{0,24},{2,26},{4,28},{6,30},{8,0},{10,2},{12,4},{14,6},{16,8},{18,... | collective-permute-start | bytes 294920 | tf_op jit(solution)/shard_map/ppermute | solution.py:317
  43.4 2.5 %collective-permute-done.6 = bf16[32,1536]{1,0:T(8,128)(2,1)S(1)} collective-permute-done((bf16[32,1536]{1,0:T(8,128)(2,1)S(1)}, bf16[32,1536]{1,0:T(8,128)(2,1)S(1)}, u32[]{:S(2)}, u32[]{:S(2)}) %collective-permute-start.6) | collective-permute-done | bytes 98336 | tf_op jit(solution)/shard_map/ppermute | solution.py:317
  46.5 2.5 %collective-permute-done.7 = bf16[32,1536]{1,0:T(8,128)(2,1)S(1)} collective-permute-done((bf16[32,1536]{1,0:T(8,128)(2,1)S(1)}, bf16[32,1536]{1,0:T(8,128)(2,1)S(1)}, u32[]{:S(2)}, u32[]{:S(2)}) %collective-permute-start.7) | collective-permute-done | bytes 98336 | tf_op jit(solution)/shard_map/ppermute | solution.py:317
  51.0 0.7 collective-permute-done.16
  51.7 1.5 %collective-permute-start.12 = (bf16[3,32,1536]{2,1,0:T(8,128)(2,1)S(1)}, bf16[3,32,1536]{2,1,0:T(8,128)(2,1)S(1)}, u32[]{:S(2)}, u32[]{:S(2)}) collective-permute-start(bf16[3,32,1536]{2,1,0:T(8,128)(2,1)S(1)} %pad_maximum_fusion.1), channel_id=1, source_target_pairs={{0,4},{2,6},{4,0},{6,2},{8,12},{10,14},{12,8},{14,10},{16,20},{18,... | collective-permute-start | bytes 884744 | tf_op jit(solution)/shard_map/ppermute | solution.py:327
  53.2 0.9 %collective-permute-start.9 = (bf16[4,32,1536]{2,1,0:T(8,128)(2,1)S(1)}, bf16[4,32,1536]{2,1,0:T(8,128)(2,1)S(1)}, u32[]{:S(2)}, u32[]{:S(2)}) collective-permute-start(bf16[4,32,1536]{2,1,0:T(8,128)(2,1)S(1)} %pad_maximum_fusion), channel_id=1, source_target_pairs={{0,6},{2,4},{4,2},{6,0},{8,14},{10,12},{12,10},{14,8},{16,22},{18,... | collective-permute-start | bytes 1179656 | tf_op jit(solution)/shard_map/ppermute | solution.py:328
  54.1 5.5 %hist.6.refs_3_ = f32[16,128,128]{2,1,0:T(8,128)S(1)} custom-call(bf16[3,16,1536]{2,1,0:T(8,128)(2,1)S(1)} %pad_maximum_fusion.7.refs_0_, bf16[3,32,1536]{2,1,0:T(8,128)(2,1)S(1)} %pad_maximum_fusion.2.refs_1_, bf16[3,32,1536]{2,1,0:T(8,128)(2,1)S(1)} %collective-permute-done.19.refs_2_), custom_call_target="tpu_custom_call" | custom-call | flops 9663676416 | bytes 737280 | tf_op jit(solution)/shard_map/hist/pallas_call | solution.py:250
  59.6 3.8 %hist.7.refs_3_ = f32[16,128,128]{2,1,0:T(8,128)S(1)} custom-call(bf16[2,16,1536]{2,1,0:T(8,128)(2,1)S(1)} %pad_maximum_fusion.8.refs_0_, bf16[2,32,1536]{2,1,0:T(8,128)(2,1)S(1)} %pad_maximum_fusion.4.refs_1_, bf16[2,32,1536]{2,1,0:T(8,128)(2,1)S(1)} %slice.10.refs_2_, f32[16,128,128]{2,1,0:T(8,128)S(1)} %hist.6.refs_3_), custom_call_target="tpu_custom_call", output_to_operand_aliasing={{}: (3, {})} | custom-call | flops 6442450944 | bytes 491520 | tf_op jit(solution)/shard_map/hist/pallas_call | solution.py:250
  63.5 1.9 %hist.8.refs_3_ = f32[16,128,128]{2,1,0:T(8,128)S(1)} custom-call(bf16[1,16,1536]{2,1,0:T(8,128)(2,1)S(1)} %get-tuple-element.63.refs_0_, bf16[1,32,1536]{2,1,0:T(8,128)(2,1)S(1)} %bitcast.25, bf16[1,32,1536]{2,1,0:T(8,128)(2,1)S(1)} %slice.11.refs_2_, f32[16,128,128]{2,1,0:T(8,128)S(1)} %hist.7.refs_3_), custom_call_target="tpu_custom_call", output_to_operand_aliasing={{}: (3, {})} | custom-call | flops 3221225472 | bytes 245760 | tf_op jit(solution)/shard_map/hist/pallas_call | solution.py:250
  65.4 2.1 %collective-permute-start.3 = (bf16[4,16,1536]{2,1,0:T(8,128)(2,1)S(1)}, bf16[4,16,1536]{2,1,0:T(8,128)(2,1)S(1)}, u32[]{:S(2)}, u32[]{:S(2)}) collective-permute-start(bf16[4,16,1536]{2,1,0:T(8,128)(2,1)S(1)} %pad_maximum_fusion.3), channel_id=1, source_target_pairs={{0,6},{2,4},{4,2},{6,0},{8,14},{10,12},{12,10},{14,8},{16,22},{18,... | collective-permute-start | bytes 589832 | tf_op jit(solution)/shard_map/ppermute | solution.py:322
  67.5 1.7 %collective-permute-done.12.refs_1_ = bf16[3,32,1536]{2,1,0:T(8,128)(2,1)S(1)} collective-permute-done((bf16[3,32,1536]{2,1,0:T(8,128)(2,1)S(1)}, bf16[3,32,1536]{2,1,0:T(8,128)(2,1)S(1)}, u32[]{:S(2)}, u32[]{:S(2)}) %collective-permute-start.12) | collective-permute-done | bytes 294944 | tf_op jit(solution)/shard_map/ppermute | solution.py:327
  69.7 5.6 %hist.9.refs_3_ = f32[16,128,128]{2,1,0:T(8,128)S(1)} custom-call(bf16[3,16,1536]{2,1,0:T(8,128)(2,1)S(1)} %collective-permute-done.14.refs_0_, bf16[3,32,1536]{2,1,0:T(8,128)(2,1)S(1)} %collective-permute-done.15.refs_1_, bf16[3,32,1536]{2,1,0:T(8,128)(2,1)S(1)} %collective-permute-done.20.refs_2_, ...), custom_call_target="tpu_custom_call", output_to_operand_aliasing={{}: (3, {})} | custom-call | flops 9663676416 | bytes 737280 | tf_op jit(solution)/shard_map/hist/pallas_call | solution.py:250
  75.3 5.6 %hist.10.refs_3_ = f32[16,128,128]{2,1,0:T(8,128)S(1)} custom-call(bf16[3,16,1536]{2,1,0:T(8,128)(2,1)S(1)} %collective-permute-done.11.refs_0_, bf16[3,32,1536]{2,1,0:T(8,128)(2,1)S(1)} %collective-permute-done.12.refs_1_, bf16[3,32,1536]{2,1,0:T(8,128)(2,1)S(1)} %collective-permute-done.13.refs_2_, ...), custom_call_target="tpu_custom_call", output_to_operand_aliasing={{}: (3, {})} | custom-call | flops 9663676416 | bytes 737280 | tf_op jit(solution)/shard_map/hist/pallas_call | solution.py:250
  81.0 8.4 %hist.11 = f32[16,256]{1,0:T(8,128)} custom-call(bf16[4,16,1536]{2,1,0:T(8,128)(2,1)S(1)} %collective-permute-done.3.refs_0_, bf16[4,32,1536]{2,1,0:T(8,128)(2,1)S(1)} %collective-permute-done.9.refs_1_, bf16[4,32,1536]{2,1,0:T(8,128)(2,1)S(1)} %collective-permute-done.10.refs_2_, f32[16,128,128]{2,1,0:T(8,128)S(1)} %hist.10.refs_3_), custom_call_target="tpu_custom_call" | custom-call | flops 12884901888 | bytes 983040 | tf_op jit(solution)/shard_map/hist/pallas_call | solution.py:250
  (54 shorter events, 5.2 us)
Async XLA Ops:
  0.6 0.9 %copy-start = (f32[16,1536]{1,0:T(8,128)S(1)}, f32[16,1536]{1,0:T(8,128)}, u32[]{:S(2)}) copy-start(f32[16,1536]{1,0:T(8,128)} %margins_ref.3) | copy-start | bytes 294916
  3.0 17.1 %all-to-all-start = ((f32[16,16,128]{2,1,0:T(8,128)}), f32[16,16,128]{2,1,0:T(8,128)S(1)}, u32[]{:S(2)}, u32[]{:S(2)}) async-start(f32[16,16,128]{2,1,0:T(8,128)} %get-tuple-element.33), calls=%async_computation | async-start | bytes 262144 | tf_op jit(solution)/shard_map/all_to_all | solution.py:356
  11.4 0.7 copy-start.3
  12.7 7.4 %copy-start.2 = (s32[16,1536]{1,0:T(8,128)S(1)}, s32[16,1536]{1,0:T(8,128)}, u32[]{:S(2)}) copy-start(s32[16,1536]{1,0:T(8,128)} %events_ref.3) | copy-start | bytes 294916
  14.3 14.9 %copy-start.4 = (s32[1536]{0:T(1024)S(1)}, s32[1536]{0:T(1024)}, u32[]{:S(2)}) copy-start(s32[1536]{0:T(1024)} %tie_ref.3) | copy-start | bytes 18436
  14.4 15.5 %collective-permute-start = (bf16[4,16,1536]{2,1,0:T(8,128)(2,1)S(1)}, bf16[4,16,1536]{2,1,0:T(8,128)(2,1)S(1)}, u32[]{:S(2)}, u32[]{:S(2)}) collective-permute-start(bf16[4,16,1536]{2,1,0:T(8,128)(2,1)S(1)} %get-tuple-element.61), channel_id=1, source_target_pairs={{0,8},{2,10},{4,12},{6,14},{8,16},{10,18},{12,20},{14,22},{16,24},... | collective-permute-start | bytes 589832 | tf_op jit(solution)/shard_map/ppermute | solution.py:310
  16.3 14.9 %collective-permute-start.1 = (bf16[4,16,1536]{2,1,0:T(8,128)(2,1)S(1)}, bf16[4,16,1536]{2,1,0:T(8,128)(2,1)S(1)}, u32[]{:S(2)}, u32[]{:S(2)}) collective-permute-start(bf16[4,16,1536]{2,1,0:T(8,128)(2,1)S(1)} %get-tuple-element.60), channel_id=1, source_target_pairs={{0,16},{2,18},{4,20},{6,22},{8,24},{10,26},{12,28},{14,30},{16,0},... | collective-permute-start | bytes 589832 | tf_op jit(solution)/shard_map/ppermute | solution.py:310
  18.6 12.5 %collective-permute-start.2 = (bf16[4,16,1536]{2,1,0:T(8,128)(2,1)S(1)}, bf16[4,16,1536]{2,1,0:T(8,128)(2,1)S(1)}, u32[]{:S(2)}, u32[]{:S(2)}) collective-permute-start(bf16[4,16,1536]{2,1,0:T(8,128)(2,1)S(1)} %get-tuple-element.59), channel_id=1, source_target_pairs={{0,24},{2,26},{4,28},{6,30},{8,0},{10,2},{12,4},{14,6},{16,8},{18,... | collective-permute-start | bytes 589832 | tf_op jit(solution)/shard_map/ppermute | solution.py:310
  21.8 15.6 %copy-start.1 = (f32[16,1536]{1,0:T(8,128)S(1)}, f32[16,1536]{1,0:T(8,128)}, u32[]{:S(2)}) copy-start(f32[16,1536]{1,0:T(8,128)} %margins_ref.3) | copy-start | bytes 294916
  21.8 15.6 %copy-start.5 = (s32[1536]{0:T(1024)S(1)}, s32[1536]{0:T(1024)}, u32[]{:S(2)}) copy-start(s32[1536]{0:T(1024)} %node_ref.1) | copy-start | bytes 18436
  21.8 15.4 %all-to-all-start.1 = ((f32[16,1,128]{2,1,0:T(1,128)}), f32[16,1,128]{2,1,0:T(1,128)S(1)}, u32[]{:S(2)}, u32[]{:S(2)}) async-start(f32[16,1,128]{2,1,0:T(1,128)} %get-tuple-element.40), calls=%async_computation.1 | async-start | bytes 16384 | tf_op jit(solution)/shard_map/all_to_all | solution.py:356
  25.7 12.6 %collective-permute-start.4 = (bf16[16,1536]{1,0:T(8,128)(2,1)S(1)}, bf16[16,1536]{1,0:T(8,128)(2,1)S(1)}, u32[]{:S(2)}, u32[]{:S(2)}) collective-permute-start(bf16[16,1536]{1,0:T(8,128)(2,1)S(1)} %get-tuple-element.78), channel_id=1, source_target_pairs={{0,2},{2,0},{4,6},{6,4},{8,10},{10,8},{12,14},{14,12},{16,18},{18,... | collective-permute-start | bytes 147464 | tf_op jit(solution)/shard_map/ppermute | solution.py:376
  27.7 10.6 %collective-permute-start.5 = (bf16[16,1536]{1,0:T(8,128)(2,1)S(1)}, bf16[16,1536]{1,0:T(8,128)(2,1)S(1)}, u32[]{:S(2)}, u32[]{:S(2)}) collective-permute-start(bf16[16,1536]{1,0:T(8,128)(2,1)S(1)} %get-tuple-element.77), channel_id=1, source_target_pairs={{0,4},{2,6},{4,0},{6,2},{8,12},{10,14},{12,8},{14,10},{16,20},{18,... | collective-permute-start | bytes 147464 | tf_op jit(solution)/shard_map/ppermute | solution.py:376
  38.4 7.6 %collective-permute-start.6 = (bf16[32,1536]{1,0:T(8,128)(2,1)S(1)}, bf16[32,1536]{1,0:T(8,128)(2,1)S(1)}, u32[]{:S(2)}, u32[]{:S(2)}) collective-permute-start(bf16[32,1536]{1,0:T(8,128)(2,1)S(1)} %get-tuple-element.51), channel_id=1, source_target_pairs={{0,8},{2,10},{4,12},{6,14},{8,16},{10,18},{12,20},{14,22},{16,24},... | collective-permute-start | bytes 294920 | tf_op jit(solution)/shard_map/ppermute | solution.py:317
  39.0 10.0 %collective-permute-start.7 = (bf16[32,1536]{1,0:T(8,128)(2,1)S(1)}, bf16[32,1536]{1,0:T(8,128)(2,1)S(1)}, u32[]{:S(2)}, u32[]{:S(2)}) collective-permute-start(bf16[32,1536]{1,0:T(8,128)(2,1)S(1)} %get-tuple-element.51), channel_id=1, source_target_pairs={{0,16},{2,18},{4,20},{6,22},{8,24},{10,26},{12,28},{14,30},{16,0},... | collective-permute-start | bytes 294920 | tf_op jit(solution)/shard_map/ppermute | solution.py:317
  40.4 9.1 %collective-permute-start.8 = (bf16[32,1536]{1,0:T(8,128)(2,1)S(1)}, bf16[32,1536]{1,0:T(8,128)(2,1)S(1)}, u32[]{:S(2)}, u32[]{:S(2)}) collective-permute-start(bf16[32,1536]{1,0:T(8,128)(2,1)S(1)} %get-tuple-element.51), channel_id=1, source_target_pairs={{0,24},{2,26},{4,28},{6,30},{8,0},{10,2},{12,4},{14,6},{16,8},{18,... | collective-permute-start | bytes 294920 | tf_op jit(solution)/shard_map/ppermute | solution.py:317
  42.2 7.3 %collective-permute-start.17 = (bf16[32,1536]{1,0:T(8,128)(2,1)S(1)}, bf16[32,1536]{1,0:T(8,128)(2,1)S(1)}, u32[]{:S(2)}, u32[]{:S(2)}) collective-permute-start(bf16[32,1536]{1,0:T(8,128)(2,1)S(1)} %get-tuple-element.51), channel_id=1, source_target_pairs={{0,2},{2,0},{4,6},{6,4},{8,10},{10,8},{12,14},{14,12},{16,18},{18,... | collective-permute-start | bytes 294920 | tf_op jit(solution)/shard_map/ppermute | solution.py:318
  42.8 6.8 %collective-permute-start.18 = (bf16[32,1536]{1,0:T(8,128)(2,1)S(1)}, bf16[32,1536]{1,0:T(8,128)(2,1)S(1)}, u32[]{:S(2)}, u32[]{:S(2)}) collective-permute-start(bf16[32,1536]{1,0:T(8,128)(2,1)S(1)} %get-tuple-element.51), channel_id=1, source_target_pairs={{0,4},{2,6},{4,0},{6,2},{8,12},{10,14},{12,8},{14,10},{16,20},{18,... | collective-permute-start | bytes 294920 | tf_op jit(solution)/shard_map/ppermute | solution.py:318
  45.9 19.5 %collective-permute-start.14 = (bf16[3,16,1536]{2,1,0:T(8,128)(2,1)S(1)}, bf16[3,16,1536]{2,1,0:T(8,128)(2,1)S(1)}, u32[]{:S(2)}, u32[]{:S(2)}) collective-permute-start(bf16[3,16,1536]{2,1,0:T(8,128)(2,1)S(1)} %pad_maximum_fusion.6), channel_id=1, source_target_pairs={{0,2},{2,0},{4,6},{6,4},{8,10},{10,8},{12,14},{14,12},{16,18},{18,... | collective-permute-start | bytes 442376 | tf_op jit(solution)/shard_map/ppermute | solution.py:322
  49.0 26.3 %collective-permute-start.11 = (bf16[3,16,1536]{2,1,0:T(8,128)(2,1)S(1)}, bf16[3,16,1536]{2,1,0:T(8,128)(2,1)S(1)}, u32[]{:S(2)}, u32[]{:S(2)}) collective-permute-start(bf16[3,16,1536]{2,1,0:T(8,128)(2,1)S(1)} %pad_maximum_fusion.5), channel_id=1, source_target_pairs={{0,4},{2,6},{4,0},{6,2},{8,12},{10,14},{12,8},{14,10},{16,20},{18,... | collective-permute-start | bytes 442376 | tf_op jit(solution)/shard_map/ppermute | solution.py:322
  49.6 3.5 %collective-permute-start.19 = (bf16[3,32,1536]{2,1,0:T(8,128)(2,1)S(1)}, bf16[3,32,1536]{2,1,0:T(8,128)(2,1)S(1)}, u32[]{:S(2)}, u32[]{:S(2)}) collective-permute-start(bf16[3,32,1536]{2,1,0:T(8,128)(2,1)S(1)} %pad_maximum_fusion.2.refs_1_), channel_id=1, source_target_pairs={{0,1},{1,0},{2,3},{3,2},{4,5},{5,4},{6,7},{7,6},{8,9},{9,8},{10,11... | collective-permute-start | bytes 884744 | tf_op jit(solution)/shard_map/ppermute | solution.py:297
  49.7 1.9 %collective-permute-start.16 = (bf16[3,32,1536]{2,1,0:T(8,128)(2,1)S(1)}, bf16[3,32,1536]{2,1,0:T(8,128)(2,1)S(1)}, u32[]{:S(2)}, u32[]{:S(2)}) collective-permute-start(bf16[3,32,1536]{2,1,0:T(8,128)(2,1)S(1)} %pad_maximum_fusion.1), channel_id=1, source_target_pairs={{0,1},{1,0},{2,3},{3,2},{4,5},{5,4},{6,7},{7,6},{8,9},{9,8},{10,11... | collective-permute-start | bytes 884744 | tf_op jit(solution)/shard_map/ppermute | solution.py:297
  50.3 13.1 %collective-permute-start.15 = (bf16[3,32,1536]{2,1,0:T(8,128)(2,1)S(1)}, bf16[3,32,1536]{2,1,0:T(8,128)(2,1)S(1)}, u32[]{:S(2)}, u32[]{:S(2)}) collective-permute-start(bf16[3,32,1536]{2,1,0:T(8,128)(2,1)S(1)} %pad_maximum_fusion.1), channel_id=1, source_target_pairs={{0,2},{2,0},{4,6},{6,4},{8,10},{10,8},{12,14},{14,12},{16,18},{18,... | collective-permute-start | bytes 884744 | tf_op jit(solution)/shard_map/ppermute | solution.py:327
  51.7 17.5 %collective-permute-start.12 = (bf16[3,32,1536]{2,1,0:T(8,128)(2,1)S(1)}, bf16[3,32,1536]{2,1,0:T(8,128)(2,1)S(1)}, u32[]{:S(2)}, u32[]{:S(2)}) collective-permute-start(bf16[3,32,1536]{2,1,0:T(8,128)(2,1)S(1)} %pad_maximum_fusion.1), channel_id=1, source_target_pairs={{0,4},{2,6},{4,0},{6,2},{8,12},{10,14},{12,8},{14,10},{16,20},{18,... | collective-permute-start | bytes 884744 | tf_op jit(solution)/shard_map/ppermute | solution.py:327
  53.2 16.1 %collective-permute-start.9 = (bf16[4,32,1536]{2,1,0:T(8,128)(2,1)S(1)}, bf16[4,32,1536]{2,1,0:T(8,128)(2,1)S(1)}, u32[]{:S(2)}, u32[]{:S(2)}) collective-permute-start(bf16[4,32,1536]{2,1,0:T(8,128)(2,1)S(1)} %pad_maximum_fusion), channel_id=1, source_target_pairs={{0,6},{2,4},{4,2},{6,0},{8,14},{10,12},{12,10},{14,8},{16,22},{18,... | collective-permute-start | bytes 1179656 | tf_op jit(solution)/shard_map/ppermute | solution.py:328
  63.4 6.3 %collective-permute-start.20 = (bf16[3,32,1536]{2,1,0:T(8,128)(2,1)S(1)}, bf16[3,32,1536]{2,1,0:T(8,128)(2,1)S(1)}, u32[]{:S(2)}, u32[]{:S(2)}) collective-permute-start(bf16[3,32,1536]{2,1,0:T(8,128)(2,1)S(1)} %collective-permute-done.15.refs_1_), channel_id=1, source_target_pairs={{0,1},{1,0},{2,3},{3,2},{4,5},{5,4},{6,7},{7,6},{8,9},{9,8},{10,11... | collective-permute-start | bytes 884744 | tf_op jit(solution)/shard_map/ppermute | solution.py:297
  65.4 15.6 %collective-permute-start.3 = (bf16[4,16,1536]{2,1,0:T(8,128)(2,1)S(1)}, bf16[4,16,1536]{2,1,0:T(8,128)(2,1)S(1)}, u32[]{:S(2)}, u32[]{:S(2)}) collective-permute-start(bf16[4,16,1536]{2,1,0:T(8,128)(2,1)S(1)} %pad_maximum_fusion.3), channel_id=1, source_target_pairs={{0,6},{2,4},{4,2},{6,0},{8,14},{10,12},{12,10},{14,8},{16,22},{18,... | collective-permute-start | bytes 589832 | tf_op jit(solution)/shard_map/ppermute | solution.py:322
  69.2 6.1 %collective-permute-start.13 = (bf16[3,32,1536]{2,1,0:T(8,128)(2,1)S(1)}, bf16[3,32,1536]{2,1,0:T(8,128)(2,1)S(1)}, u32[]{:S(2)}, u32[]{:S(2)}) collective-permute-start(bf16[3,32,1536]{2,1,0:T(8,128)(2,1)S(1)} %collective-permute-done.12.refs_1_), channel_id=1, source_target_pairs={{0,1},{1,0},{2,3},{3,2},{4,5},{5,4},{6,7},{7,6},{8,9},{9,8},{10,11... | collective-permute-start | bytes 884744 | tf_op jit(solution)/shard_map/ppermute | solution.py:297
  69.2 11.8 %collective-permute-start.10 = (bf16[4,32,1536]{2,1,0:T(8,128)(2,1)S(1)}, bf16[4,32,1536]{2,1,0:T(8,128)(2,1)S(1)}, u32[]{:S(2)}, u32[]{:S(2)}) collective-permute-start(bf16[4,32,1536]{2,1,0:T(8,128)(2,1)S(1)} %collective-permute-done.9.refs_1_), channel_id=1, source_target_pairs={{0,1},{1,0},{2,3},{3,2},{4,5},{5,4},{6,7},{7,6},{8,9},{9,8},{10,11... | collective-permute-start | bytes 1179656 | tf_op jit(solution)/shard_map/ppermute | solution.py:297

commit v5 on v4

--- a/solution.py
+++ b/solution.py
@@ -207,50 +207,59 @@
         gain_ref[f : f + 1, side * HALF : (side + 1) * HALF] = jnp.mean(value, axis=0, keepdims=True)
 
 
-def hist_kernel(blocks, feature_count, first, last, *refs):
+def hist_kernel(steps, feature_count, first, last, *refs):
     if first:
         codes_ref, mine_ref, other_ref, *outs = refs
     else:
         codes_ref, mine_ref, other_ref, before_ref, *outs = refs
     sums_ref = outs[-1]
-    block = pl.program_id(0)
-
-    @pl.when(block == 0)
+    step = pl.program_id(0)
+    blocks = codes_ref.shape[0]
+
+    @pl.when(step == 0)
     def _():
         sums_ref[...] = jnp.zeros_like(sums_ref) if first else before_ref[...]
 
-    pairs = jnp.concatenate([mine_ref[0], other_ref[0]], axis=0)
+    codes = jnp.concatenate([codes_ref[k] for k in range(blocks)], axis=1)
+    mine = jnp.concatenate([mine_ref[k] for k in range(blocks)], axis=1)
+    other = jnp.concatenate([other_ref[k] for k in range(blocks)], axis=1)
+    pairs = jnp.concatenate([mine, other], axis=0)
     if not last:
-        add_block(codes_ref[0], pairs, sums_ref, feature_count)
+        add_block(codes, pairs, sums_ref, feature_count)
         return
-
-    @pl.when(block < blocks - 1)
+    finish = functools.partial(write_gain, outs[0])
+    if steps == 1:
+        add_block(codes, pairs, sums_ref, feature_count, finish)
+        return
+
+    @pl.when(step < steps - 1)
     def _():
-        add_block(codes_ref[0], pairs, sums_ref, feature_count)
-
-    @pl.when(block == blocks - 1)
+        add_block(codes, pairs, sums_ref, feature_count)
+
+    @pl.when(step == steps - 1)
     def _():
-        add_block(codes_ref[0], pairs, sums_ref, feature_count, functools.partial(write_gain, outs[0]))
+        add_block(codes, pairs, sums_ref, feature_count, finish)
 
 
 def histogram(codes, mine, other, before, last):
     blocks, feature_count, length = codes.shape
     half = mine.shape[1]
+    joined = next(n for n in (3, 2, 1) if blocks % n == 0)
     sums = (feature_count, 4 * half, HALF)
     operands = [codes, mine, other]
     in_specs = [
-        pl.BlockSpec((1, feature_count, length), lambda i: (i, 0, 0)),
-        pl.BlockSpec((1, half, length), lambda i: (i, 0, 0)),
-        pl.BlockSpec((1, half, length), lambda i: (i, 0, 0)),
+        pl.BlockSpec((joined, feature_count, length), lambda i: (i, 0, 0)),
+        pl.BlockSpec((joined, half, length), lambda i: (i, 0, 0)),
+        pl.BlockSpec((joined, half, length), lambda i: (i, 0, 0)),
     ]
     whole = pl.BlockSpec(sums, lambda i: (0, 0, 0))
     if before is not None:
         operands.append(before)
         in_specs.append(whole)
     return pl.pallas_call(
-        functools.partial(hist_kernel, blocks, feature_count, before is None, last),
+        functools.partial(hist_kernel, blocks // joined, feature_count, before is None, last),
         out_shape=shape(feature_count, BINS) if last else shape(*sums),
-        grid=(blocks,),
+        grid=(blocks // joined,),
         in_specs=in_specs,
         out_specs=pl.BlockSpec((feature_count, BINS), lambda i: (0, 0)) if last else whole,
         scratch_shapes=[pltpu.VMEM(sums, f32)] if last else [],
@@ -315,18 +324,16 @@
     planes = devices // 4
     here = lax.axis_index("tm") % 4
     column = [lax.ppermute(pairs, "tm", ring(devices, d)) for d in range(1, planes)]
-    beside = [lax.ppermute(pairs, "tm", flip(devices, d)) for d in range(1, 3)]
+    beside = [lax.ppermute(pairs, "tm", flip(devices, d)) for d in range(1, 4)]
     own = pick(held[0], here, 0)
     near = jnp.stack([pick(h, here, 0) for h in held[1:]])
     far = [
-        lax.ppermute(jnp.stack([pick(h, here ^ d, 0) for h in (held if d == 3 else held[1:])]), "tm", flip(devices, d))
+        lax.ppermute(jnp.stack([pick(h, here ^ d, 0) for h in held[1:]]), "tm", flip(devices, d))
         for d in range(1, 4)
     ]
     *column, pairs = lax.optimization_barrier((*column, pairs))
-    column_sent = jnp.stack(column)
-    there = [lax.ppermute(column_sent, "tm", flip(devices, d)) for d in range(1, 3)]
-    there.append(lax.ppermute(jnp.stack([pairs] + column), "tm", flip(devices, 3)))
-    column = column_sent
+    column = jnp.stack(column)
+    there = [lax.ppermute(column, "tm", flip(devices, d)) for d in range(1, 4)]
     other = swap(column)
     beside = jnp.stack([pairs] + beside)
     sums = histogram(jnp.stack([own] + plane), beside, swap(beside), None, False)
@@ -373,7 +380,7 @@
     if blocked:
         column = lax.axis_index("tm") % 4
         aside, second = lax.optimization_barrier((codes[0], second))
-        plane = [lax.ppermute(pick(aside, column ^ d, 0), "tm", flip(devices, d)) for d in range(1, 3)]
+        plane = [lax.ppermute(pick(aside, column ^ d, 0), "tm", flip(devices, d)) for d in range(1, 4)]
     first, second = call(close_kernel, (rows, rows), "closes", first, second, tie_group)
     codes, parts = lax.optimization_barrier((codes, parts))
     grad, hess, pairs = call(

time: 89.8 us -> 88.2 us (0.982)
  Pallas kernels: 36.1 us -> 34.4 us
    pallas_call x6, Pallas kernels: 30.8 us -> 29.1 us  [histogram(): pl.pallas_call(functools.partial(hist_kernel, blocks // joined, feature_c...]
    ppermute x3, waiting for transfers between devices: 5.04 us -> 3.92 us  [spread(): lax.ppermute(pairs, 'tm', ring(devices, d))]
    ppermute x8 -> x9, waiting for transfers between devices: 1.7 us -> 2.42 us  [the longest x3 2.4 us: spread(): beside = [lax.ppermute(pairs, 'tm', flip(devices, d)) for d in range(1, 4)]]
    ppermute x2 -> x3, starting transfers between devices: 3.44 us -> 3.62 us  [on_device(): lax.ppermute(pick(aside, column ^ d, 0), 'tm', flip(devices, d))]
    ppermute x8 -> x9, starting transfers between devices: 7.38 us -> 7.3 us  [the longest x3 2.69 us: spread(): beside = [lax.ppermute(pairs, 'tm', flip(devices, d)) for d in range(1, 4)]]
  transfers between devices with their start and end apart: 23 -> 25, of which waited for: 6 -> 6; matrix products, arithmetic and copies ran while one was open for 2% -> 2% of each run, Pallas kernels for 29% -> 31%
where the time goes in v5:
time: 88.2 us; the launch traced here: 87.9 us
  Pallas kernels  34.4 us (39%)
  starting transfers between devices  33.9 us (38%)
  waiting for transfers between devices  15 us (17%)
  local copies, waits for them, and re-layouts  1.77 us (2%)
  other arithmetic  1.75 us (2%)
  between operations  1.05 us (1%)
    pallas_call x6, Pallas kernels, histogram(): pl.pallas_call(functools.partial(hist_kernel, blocks // joined, feature_c...  29.1 us
    all_to_all x2, starting transfers between devices, exchange(): return lax.all_to_all(total, 'tm', 0, 0)  12.1 us
    all_to_all x2, waiting for transfers between devices, exchange(): return lax.all_to_all(total, 'tm', 0, 0)  6.1 us
    ppermute x3, starting transfers between devices, send_planes(): lax.ppermute(pick(codes, (plane + d) % planes, 0), 'tm', ring(devices, d))  5.72 us
    pallas_call x5, Pallas kernels, call(): pl.pallas_call(kernel, out_shape=out_shape, in_specs=([SMEM] if place els...  5.33 us
    ppermute x3, starting transfers between devices, spread(): lax.ppermute(pairs, 'tm', ring(devices, d))  4.01 us
    ppermute x3, waiting for transfers between devices, spread(): lax.ppermute(pairs, 'tm', ring(devices, d))  3.92 us
    ppermute x3, starting transfers between devices, on_device(): lax.ppermute(pick(aside, column ^ d, 0), 'tm', flip(devices, d))  3.62 us
  transfers between devices with their start and end apart: 25, of which 6 were waited for; matrix products, arithmetic and copies ran while one was open for 2% of the time, Pallas kernels for 31%

profile of v5, /device:TPU:0, one launch (start us, length us, event | category | flops | bytes accessed | tf_op | source)
XLA Modules:
  0.0 87.9 jit_solution(1043155557950970504)
XLA Ops:
  0.6 0.9 %copy-done = f32[16,1536]{1,0:T(8,128)S(1)} copy-done((f32[16,1536]{1,0:T(8,128)S(1)}, f32[16,1536]{1,0:T(8,128)}, u32[]{:S(2)}) %copy-start) | copy-done | bytes 98328
  1.5 1.4 %risk.1 = (f32[16,1536]{1,0:T(8,128)S(1)}, f32[16,16,128]{2,1,0:T(8,128)}) custom-call(f32[16,1536]{1,0:T(8,128)S(1)} %copy-done), custom_call_target="tpu_custom_call" | custom-call | tf_op jit(solution)/shard_map/risk/pallas_call | solution.py:279
  3.0 8.3 %all-to-all-start = ((f32[16,16,128]{2,1,0:T(8,128)}), f32[16,16,128]{2,1,0:T(8,128)S(1)}, u32[]{:S(2)}, u32[]{:S(2)}) async-start(f32[16,16,128]{2,1,0:T(8,128)} %get-tuple-element.34), calls=%async_computation | async-start | bytes 262144 | tf_op jit(solution)/shard_map/all_to_all | solution.py:363
  11.4 0.7 copy-done.3
  12.1 0.7 opens.1.local_ref
  12.7 1.5 %convert_element_type.3 = bf16[256,1536]{1,0:T(8,128)(2,1)S(1)} convert(s32[256,1536]{1,0:T(8,128)} %param.9) | non-fusion elementwise | flops 393216 | bytes 2359296 | tf_op jit(solution)/shard_map/convert_element_type | solution.py:369
  14.4 1.9 %collective-permute-start = (bf16[4,16,1536]{2,1,0:T(8,128)(2,1)S(1)}, bf16[4,16,1536]{2,1,0:T(8,128)(2,1)S(1)}, u32[]{:S(2)}, u32[]{:S(2)}) collective-permute-start(bf16[4,16,1536]{2,1,0:T(8,128)(2,1)S(1)} %get-tuple-element.63), channel_id=1, source_target_pairs={{0,8},{2,10},{4,12},{6,14},{8,16},{10,18},{12,20},{14,22},{16,24},... | collective-permute-start | bytes 589832 | tf_op jit(solution)/shard_map/ppermute | solution.py:319
  16.3 2.4 %collective-permute-start.1 = (bf16[4,16,1536]{2,1,0:T(8,128)(2,1)S(1)}, bf16[4,16,1536]{2,1,0:T(8,128)(2,1)S(1)}, u32[]{:S(2)}, u32[]{:S(2)}) collective-permute-start(bf16[4,16,1536]{2,1,0:T(8,128)(2,1)S(1)} %get-tuple-element.62), channel_id=1, source_target_pairs={{0,16},{2,18},{4,20},{6,22},{8,24},{10,26},{12,28},{14,30},{16,0},... | collective-permute-start | bytes 589832 | tf_op jit(solution)/shard_map/ppermute | solution.py:319
  18.7 1.5 %collective-permute-start.2 = (bf16[4,16,1536]{2,1,0:T(8,128)(2,1)S(1)}, bf16[4,16,1536]{2,1,0:T(8,128)(2,1)S(1)}, u32[]{:S(2)}, u32[]{:S(2)}) collective-permute-start(bf16[4,16,1536]{2,1,0:T(8,128)(2,1)S(1)} %get-tuple-element.61), channel_id=1, source_target_pairs={{0,24},{2,26},{4,28},{6,30},{8,0},{10,2},{12,4},{14,6},{16,8},{18,... | collective-permute-start | bytes 589832 | tf_op jit(solution)/shard_map/ppermute | solution.py:319
  20.1 1.7 %events.1 = (f32[16,1536]{1,0:T(8,128)S(1)}, f32[16,1536]{1,0:T(8,128)S(1)}, f32[16,1,128]{2,1,0:T(1,128)}) custom-call(s32[1]{0:T(128)} %bitcast.place_ref, f32[16,1536]{1,0:T(8,128)S(1)} %opens.1.local_ref, f32[16,16,128]{2,1,0:T(8,128)S(1)} %all-to-all-done.parts_ref, s32[16,1536]{1,0:T(8,128)S(1)} %copy-done.2), custom_call_target="tpu_custom_call" | custom-call | tf_op jit(solution)/shard_map/events/pallas_call | solution.py:279
  21.9 3.7 %all-to-all-start.1 = ((f32[16,1,128]{2,1,0:T(1,128)}), f32[16,1,128]{2,1,0:T(1,128)S(1)}, u32[]{:S(2)}, u32[]{:S(2)}) async-start(f32[16,1,128]{2,1,0:T(1,128)} %get-tuple-element.41), calls=%async_computation.1 | async-start | bytes 16384 | tf_op jit(solution)/shard_map/all_to_all | solution.py:363
  25.6 2.0 %collective-permute-start.4 = (bf16[16,1536]{1,0:T(8,128)(2,1)S(1)}, bf16[16,1536]{1,0:T(8,128)(2,1)S(1)}, u32[]{:S(2)}, u32[]{:S(2)}) collective-permute-start(bf16[16,1536]{1,0:T(8,128)(2,1)S(1)} %get-tuple-element.79), channel_id=1, source_target_pairs={{0,2},{2,0},{4,6},{6,4},{8,10},{10,8},{12,14},{14,12},{16,18},{18,... | collective-permute-start | bytes 147464 | tf_op jit(solution)/shard_map/ppermute | solution.py:383
  27.6 1.5 %collective-permute-start.5 = (bf16[16,1536]{1,0:T(8,128)(2,1)S(1)}, bf16[16,1536]{1,0:T(8,128)(2,1)S(1)}, u32[]{:S(2)}, u32[]{:S(2)}) collective-permute-start(bf16[16,1536]{1,0:T(8,128)(2,1)S(1)} %get-tuple-element.78), channel_id=1, source_target_pairs={{0,4},{2,6},{4,0},{6,2},{8,12},{10,14},{12,8},{14,10},{16,20},{18,... | collective-permute-start | bytes 147464 | tf_op jit(solution)/shard_map/ppermute | solution.py:383
  29.9 1.3 %collective-permute-done.1 = bf16[4,16,1536]{2,1,0:T(8,128)(2,1)S(1)} collective-permute-done((bf16[4,16,1536]{2,1,0:T(8,128)(2,1)S(1)}, bf16[4,16,1536]{2,1,0:T(8,128)(2,1)S(1)}, u32[]{:S(2)}, u32[]{:S(2)}) %collective-permute-start.1) | collective-permute-done | bytes 196640 | tf_op jit(solution)/shard_map/ppermute | solution.py:319
  31.2 6.1 %all-to-all-done.1.parts_ref = f32[16,1,128]{2,1,0:T(1,128)S(1)} async-done(((f32[16,1,128]{2,1,0:T(1,128)}), f32[16,1,128]{2,1,0:T(1,128)S(1)}, u32[]{:S(2)}, u32[]{:S(2)}) %all-to-all-start.1) | async-done | bytes 8224 | tf_op jit(solution)/shard_map/all_to_all | solution.py:363
  37.5 0.9 grads.1
  39.0 1.5 %collective-permute-start.8 = (bf16[32,1536]{1,0:T(8,128)(2,1)S(1)}, bf16[32,1536]{1,0:T(8,128)(2,1)S(1)}, u32[]{:S(2)}, u32[]{:S(2)}) collective-permute-start(bf16[32,1536]{1,0:T(8,128)(2,1)S(1)} %get-tuple-element.58), channel_id=1, source_target_pairs={{0,16},{2,18},{4,20},{6,22},{8,24},{10,26},{12,28},{14,30},{16,0},... | collective-permute-start | bytes 294920 | tf_op jit(solution)/shard_map/ppermute | solution.py:326
  40.5 1.9 %collective-permute-start.9 = (bf16[32,1536]{1,0:T(8,128)(2,1)S(1)}, bf16[32,1536]{1,0:T(8,128)(2,1)S(1)}, u32[]{:S(2)}, u32[]{:S(2)}) collective-permute-start(bf16[32,1536]{1,0:T(8,128)(2,1)S(1)} %get-tuple-element.58), channel_id=1, source_target_pairs={{0,24},{2,26},{4,28},{6,30},{8,0},{10,2},{12,4},{14,6},{16,8},{18,... | collective-permute-start | bytes 294920 | tf_op jit(solution)/shard_map/ppermute | solution.py:326
  42.4 0.7 collective-permute-start.18
  43.0 1.5 %collective-permute-start.19 = (bf16[32,1536]{1,0:T(8,128)(2,1)S(1)}, bf16[32,1536]{1,0:T(8,128)(2,1)S(1)}, u32[]{:S(2)}, u32[]{:S(2)}) collective-permute-start(bf16[32,1536]{1,0:T(8,128)(2,1)S(1)} %get-tuple-element.58), channel_id=1, source_target_pairs={{0,4},{2,6},{4,0},{6,2},{8,12},{10,14},{12,8},{14,10},{16,20},{18,... | collective-permute-start | bytes 294920 | tf_op jit(solution)/shard_map/ppermute | solution.py:327
  44.5 1.4 %collective-permute-done.7 = bf16[32,1536]{1,0:T(8,128)(2,1)S(1)} collective-permute-done((bf16[32,1536]{1,0:T(8,128)(2,1)S(1)}, bf16[32,1536]{1,0:T(8,128)(2,1)S(1)}, u32[]{:S(2)}, u32[]{:S(2)}) %collective-permute-start.7) | collective-permute-done | bytes 98336 | tf_op jit(solution)/shard_map/ppermute | solution.py:326
  46.5 2.5 %collective-permute-done.8 = bf16[32,1536]{1,0:T(8,128)(2,1)S(1)} collective-permute-done((bf16[32,1536]{1,0:T(8,128)(2,1)S(1)}, bf16[32,1536]{1,0:T(8,128)(2,1)S(1)}, u32[]{:S(2)}, u32[]{:S(2)}) %collective-permute-start.8) | collective-permute-done | bytes 98336 | tf_op jit(solution)/shard_map/ppermute | solution.py:326
  50.1 2.4 %collective-permute-done.20 = bf16[32,1536]{1,0:T(8,128)(2,1)S(1)} collective-permute-done((bf16[32,1536]{1,0:T(8,128)(2,1)S(1)}, bf16[32,1536]{1,0:T(8,128)(2,1)S(1)}, u32[]{:S(2)}, u32[]{:S(2)}) %collective-permute-start.20) | collective-permute-done | bytes 98336 | tf_op jit(solution)/shard_map/ppermute | solution.py:327
  53.5 1.2 %collective-permute-done.17 = bf16[3,32,1536]{2,1,0:T(8,128)(2,1)S(1)} collective-permute-done((bf16[3,32,1536]{2,1,0:T(8,128)(2,1)S(1)}, bf16[3,32,1536]{2,1,0:T(8,128)(2,1)S(1)}, u32[]{:S(2)}, u32[]{:S(2)}) %collective-permute-start.17) | collective-permute-done | bytes 294944 | tf_op jit(solution)/shard_map/ppermute | solution.py:306
  55.0 2.0 %collective-permute-start.10 = (bf16[3,32,1536]{2,1,0:T(8,128)(2,1)S(1)}, bf16[3,32,1536]{2,1,0:T(8,128)(2,1)S(1)}, u32[]{:S(2)}, u32[]{:S(2)}) collective-permute-start(bf16[3,32,1536]{2,1,0:T(8,128)(2,1)S(1)} %pad_maximum_fusion.1), channel_id=1, source_target_pairs={{0,6},{2,4},{4,2},{6,0},{8,14},{10,12},{12,10},{14,8},{16,22},{18,... | collective-permute-start | bytes 884744 | tf_op jit(solution)/shard_map/ppermute | solution.py:336
  57.0 7.2 %hist.6.refs_3_ = f32[16,128,128]{2,1,0:T(8,128)S(1)} custom-call(bf16[4,16,1536]{2,1,0:T(8,128)(2,1)S(1)} %pad_maximum_fusion.3.refs_0_, bf16[4,32,1536]{2,1,0:T(8,128)(2,1)S(1)} %pad_maximum_fusion.refs_1_, bf16[4,32,1536]{2,1,0:T(8,128)(2,1)S(1)} %collective-permute-done.21.refs_2_), custom_call_target="tpu_custom_call" | custom-call | flops 12884901888 | bytes 983040 | tf_op jit(solution)/shard_map/hist/pallas_call | solution.py:259
  64.2 3.6 %hist.7.refs_3_ = f32[16,128,128]{2,1,0:T(8,128)S(1)} custom-call(bf16[2,16,1536]{2,1,0:T(8,128)(2,1)S(1)} %pad_maximum_fusion.7.refs_0_, bf16[2,32,1536]{2,1,0:T(8,128)(2,1)S(1)} %pad_maximum_fusion.2.refs_1_, bf16[2,32,1536]{2,1,0:T(8,128)(2,1)S(1)} %slice.10.refs_2_, f32[16,128,128]{2,1,0:T(8,128)S(1)} %hist.6.refs_3_), custom_call_target="tpu_custom_call", output_to_operand_aliasing={{}: (3, {})} | custom-call | flops 6442450944 | bytes 491520 | tf_op jit(solution)/shard_map/hist/pallas_call | solution.py:259
  67.9 1.9 %hist.8.refs_3_ = f32[16,128,128]{2,1,0:T(8,128)S(1)} custom-call(bf16[1,16,1536]{2,1,0:T(8,128)(2,1)S(1)} %get-tuple-element.65.refs_0_, bf16[1,32,1536]{2,1,0:T(8,128)(2,1)S(1)} %bitcast.28, bf16[1,32,1536]{2,1,0:T(8,128)(2,1)S(1)} %slice.11.refs_2_, f32[16,128,128]{2,1,0:T(8,128)S(1)} %hist.7.refs_3_), custom_call_target="tpu_custom_call", output_to_operand_aliasing={{}: (3, {})} | custom-call | flops 3221225472 | bytes 245760 | tf_op jit(solution)/shard_map/hist/pallas_call | solution.py:259
  69.7 1.0 %collective-permute-start.3 = (bf16[3,16,1536]{2,1,0:T(8,128)(2,1)S(1)}, bf16[3,16,1536]{2,1,0:T(8,128)(2,1)S(1)}, u32[]{:S(2)}, u32[]{:S(2)}) collective-permute-start(bf16[3,16,1536]{2,1,0:T(8,128)(2,1)S(1)} %pad_maximum_fusion.4), channel_id=1, source_target_pairs={{0,6},{2,4},{4,2},{6,0},{8,14},{10,12},{12,10},{14,8},{16,22},{18,... | collective-permute-start | bytes 442376 | tf_op jit(solution)/shard_map/ppermute | solution.py:331
  71.3 5.2 %hist.9.refs_3_ = f32[16,128,128]{2,1,0:T(8,128)S(1)} custom-call(bf16[3,16,1536]{2,1,0:T(8,128)(2,1)S(1)} %collective-permute-done.15.refs_0_, bf16[3,32,1536]{2,1,0:T(8,128)(2,1)S(1)} %collective-permute-done.16.refs_1_, bf16[3,32,1536]{2,1,0:T(8,128)(2,1)S(1)} %collective-permute-done.22.refs_2_, ...), custom_call_target="tpu_custom_call", output_to_operand_aliasing={{}: (3, {})} | custom-call | flops 9663676416 | bytes 737280 | tf_op jit(solution)/shard_map/hist/pallas_call | solution.py:259
  76.5 5.4 %hist.10.refs_3_ = f32[16,128,128]{2,1,0:T(8,128)S(1)} custom-call(bf16[3,16,1536]{2,1,0:T(8,128)(2,1)S(1)} %collective-permute-done.12.refs_0_, bf16[3,32,1536]{2,1,0:T(8,128)(2,1)S(1)} %collective-permute-done.13.refs_1_, bf16[3,32,1536]{2,1,0:T(8,128)(2,1)S(1)} %collective-permute-done.14.refs_2_, ...), custom_call_target="tpu_custom_call", output_to_operand_aliasing={{}: (3, {})} | custom-call | flops 9663676416 | bytes 737280 | tf_op jit(solution)/shard_map/hist/pallas_call | solution.py:259
  82.0 5.9 %hist.11 = f32[16,256]{1,0:T(8,128)} custom-call(bf16[3,16,1536]{2,1,0:T(8,128)(2,1)S(1)} %collective-permute-done.3.refs_0_, bf16[3,32,1536]{2,1,0:T(8,128)(2,1)S(1)} %collective-permute-done.10.refs_1_, bf16[3,32,1536]{2,1,0:T(8,128)(2,1)S(1)} %collective-permute-done.11.refs_2_, f32[16,128,128]{2,1,0:T(8,128)S(1)} %hist.10.refs_3_), custom_call_target="tpu_custom_call" | custom-call | flops 9663676416 | bytes 737280 | tf_op jit(solution)/shard_map/hist/pallas_call | solution.py:259
  (57 shorter events, 5.2 us)
Async XLA Ops:
  0.6 0.9 %copy-start = (f32[16,1536]{1,0:T(8,128)S(1)}, f32[16,1536]{1,0:T(8,128)}, u32[]{:S(2)}) copy-start(f32[16,1536]{1,0:T(8,128)} %margins_ref.3) | copy-start | bytes 294916
  3.0 17.2 %all-to-all-start = ((f32[16,16,128]{2,1,0:T(8,128)}), f32[16,16,128]{2,1,0:T(8,128)S(1)}, u32[]{:S(2)}, u32[]{:S(2)}) async-start(f32[16,16,128]{2,1,0:T(8,128)} %get-tuple-element.34), calls=%async_computation | async-start | bytes 262144 | tf_op jit(solution)/shard_map/all_to_all | solution.py:363
  11.4 0.7 copy-start.3
  12.7 7.4 %copy-start.2 = (s32[16,1536]{1,0:T(8,128)S(1)}, s32[16,1536]{1,0:T(8,128)}, u32[]{:S(2)}) copy-start(s32[16,1536]{1,0:T(8,128)} %events_ref.3) | copy-start | bytes 294916
  14.3 14.8 %copy-start.4 = (s32[1536]{0:T(1024)S(1)}, s32[1536]{0:T(1024)}, u32[]{:S(2)}) copy-start(s32[1536]{0:T(1024)} %tie_ref.3) | copy-start | bytes 18436
  14.4 23.1 %copy-start.1 = (f32[16,1536]{1,0:T(8,128)S(1)}, f32[16,1536]{1,0:T(8,128)}, u32[]{:S(2)}) copy-start(f32[16,1536]{1,0:T(8,128)} %margins_ref.3) | copy-start | bytes 294916
  14.4 23.1 %copy-start.5 = (s32[1536]{0:T(1024)S(1)}, s32[1536]{0:T(1024)}, u32[]{:S(2)}) copy-start(s32[1536]{0:T(1024)} %node_ref.1) | copy-start | bytes 18436
  14.4 15.3 %collective-permute-start = (bf16[4,16,1536]{2,1,0:T(8,128)(2,1)S(1)}, bf16[4,16,1536]{2,1,0:T(8,128)(2,1)S(1)}, u32[]{:S(2)}, u32[]{:S(2)}) collective-permute-start(bf16[4,16,1536]{2,1,0:T(8,128)(2,1)S(1)} %get-tuple-element.63), channel_id=1, source_target_pairs={{0,8},{2,10},{4,12},{6,14},{8,16},{10,18},{12,20},{14,22},{16,24},... | collective-permute-start | bytes 589832 | tf_op jit(solution)/shard_map/ppermute | solution.py:319
  16.3 14.9 %collective-permute-start.1 = (bf16[4,16,1536]{2,1,0:T(8,128)(2,1)S(1)}, bf16[4,16,1536]{2,1,0:T(8,128)(2,1)S(1)}, u32[]{:S(2)}, u32[]{:S(2)}) collective-permute-start(bf16[4,16,1536]{2,1,0:T(8,128)(2,1)S(1)} %get-tuple-element.62), channel_id=1, source_target_pairs={{0,16},{2,18},{4,20},{6,22},{8,24},{10,26},{12,28},{14,30},{16,0},... | collective-permute-start | bytes 589832 | tf_op jit(solution)/shard_map/ppermute | solution.py:319
  18.7 12.5 %collective-permute-start.2 = (bf16[4,16,1536]{2,1,0:T(8,128)(2,1)S(1)}, bf16[4,16,1536]{2,1,0:T(8,128)(2,1)S(1)}, u32[]{:S(2)}, u32[]{:S(2)}) collective-permute-start(bf16[4,16,1536]{2,1,0:T(8,128)(2,1)S(1)} %get-tuple-element.61), channel_id=1, source_target_pairs={{0,24},{2,26},{4,28},{6,30},{8,0},{10,2},{12,4},{14,6},{16,8},{18,... | collective-permute-start | bytes 589832 | tf_op jit(solution)/shard_map/ppermute | solution.py:319
  21.9 15.4 %all-to-all-start.1 = ((f32[16,1,128]{2,1,0:T(1,128)}), f32[16,1,128]{2,1,0:T(1,128)S(1)}, u32[]{:S(2)}, u32[]{:S(2)}) async-start(f32[16,1,128]{2,1,0:T(1,128)} %get-tuple-element.41), calls=%async_computation.1 | async-start | bytes 16384 | tf_op jit(solution)/shard_map/all_to_all | solution.py:363
  25.6 12.7 %collective-permute-start.4 = (bf16[16,1536]{1,0:T(8,128)(2,1)S(1)}, bf16[16,1536]{1,0:T(8,128)(2,1)S(1)}, u32[]{:S(2)}, u32[]{:S(2)}) collective-permute-start(bf16[16,1536]{1,0:T(8,128)(2,1)S(1)} %get-tuple-element.79), channel_id=1, source_target_pairs={{0,2},{2,0},{4,6},{6,4},{8,10},{10,8},{12,14},{14,12},{16,18},{18,... | collective-permute-start | bytes 147464 | tf_op jit(solution)/shard_map/ppermute | solution.py:383
  27.6 10.7 %collective-permute-start.5 = (bf16[16,1536]{1,0:T(8,128)(2,1)S(1)}, bf16[16,1536]{1,0:T(8,128)(2,1)S(1)}, u32[]{:S(2)}, u32[]{:S(2)}) collective-permute-start(bf16[16,1536]{1,0:T(8,128)(2,1)S(1)} %get-tuple-element.78), channel_id=1, source_target_pairs={{0,4},{2,6},{4,0},{6,2},{8,12},{10,14},{12,8},{14,10},{16,20},{18,... | collective-permute-start | bytes 147464 | tf_op jit(solution)/shard_map/ppermute | solution.py:383
  29.8 8.6 %collective-permute-start.6 = (bf16[16,1536]{1,0:T(8,128)(2,1)S(1)}, bf16[16,1536]{1,0:T(8,128)(2,1)S(1)}, u32[]{:S(2)}, u32[]{:S(2)}) collective-permute-start(bf16[16,1536]{1,0:T(8,128)(2,1)S(1)} %get-tuple-element.77), channel_id=1, source_target_pairs={{0,6},{2,4},{4,2},{6,0},{8,14},{10,12},{12,10},{14,8},{16,22},{18,... | collective-permute-start | bytes 147464 | tf_op jit(solution)/shard_map/ppermute | solution.py:383
  38.4 7.6 %collective-permute-start.7 = (bf16[32,1536]{1,0:T(8,128)(2,1)S(1)}, bf16[32,1536]{1,0:T(8,128)(2,1)S(1)}, u32[]{:S(2)}, u32[]{:S(2)}) collective-permute-start(bf16[32,1536]{1,0:T(8,128)(2,1)S(1)} %get-tuple-element.58), channel_id=1, source_target_pairs={{0,8},{2,10},{4,12},{6,14},{8,16},{10,18},{12,20},{14,22},{16,24},... | collective-permute-start | bytes 294920 | tf_op jit(solution)/shard_map/ppermute | solution.py:326
  39.0 10.0 %collective-permute-start.8 = (bf16[32,1536]{1,0:T(8,128)(2,1)S(1)}, bf16[32,1536]{1,0:T(8,128)(2,1)S(1)}, u32[]{:S(2)}, u32[]{:S(2)}) collective-permute-start(bf16[32,1536]{1,0:T(8,128)(2,1)S(1)} %get-tuple-element.58), channel_id=1, source_target_pairs={{0,16},{2,18},{4,20},{6,22},{8,24},{10,26},{12,28},{14,30},{16,0},... | collective-permute-start | bytes 294920 | tf_op jit(solution)/shard_map/ppermute | solution.py:326
  40.5 9.0 %collective-permute-start.9 = (bf16[32,1536]{1,0:T(8,128)(2,1)S(1)}, bf16[32,1536]{1,0:T(8,128)(2,1)S(1)}, u32[]{:S(2)}, u32[]{:S(2)}) collective-permute-start(bf16[32,1536]{1,0:T(8,128)(2,1)S(1)} %get-tuple-element.58), channel_id=1, source_target_pairs={{0,24},{2,26},{4,28},{6,30},{8,0},{10,2},{12,4},{14,6},{16,8},{18,... | collective-permute-start | bytes 294920 | tf_op jit(solution)/shard_map/ppermute | solution.py:326
  42.4 7.7 %collective-permute-start.18 = (bf16[32,1536]{1,0:T(8,128)(2,1)S(1)}, bf16[32,1536]{1,0:T(8,128)(2,1)S(1)}, u32[]{:S(2)}, u32[]{:S(2)}) collective-permute-start(bf16[32,1536]{1,0:T(8,128)(2,1)S(1)} %get-tuple-element.58), channel_id=1, source_target_pairs={{0,2},{2,0},{4,6},{6,4},{8,10},{10,8},{12,14},{14,12},{16,18},{18,... | collective-permute-start | bytes 294920 | tf_op jit(solution)/shard_map/ppermute | solution.py:327
  43.0 7.1 %collective-permute-start.19 = (bf16[32,1536]{1,0:T(8,128)(2,1)S(1)}, bf16[32,1536]{1,0:T(8,128)(2,1)S(1)}, u32[]{:S(2)}, u32[]{:S(2)}) collective-permute-start(bf16[32,1536]{1,0:T(8,128)(2,1)S(1)} %get-tuple-element.58), channel_id=1, source_target_pairs={{0,4},{2,6},{4,0},{6,2},{8,12},{10,14},{12,8},{14,10},{16,20},{18,... | collective-permute-start | bytes 294920 | tf_op jit(solution)/shard_map/ppermute | solution.py:327
  45.9 6.6 %collective-permute-start.20 = (bf16[32,1536]{1,0:T(8,128)(2,1)S(1)}, bf16[32,1536]{1,0:T(8,128)(2,1)S(1)}, u32[]{:S(2)}, u32[]{:S(2)}) collective-permute-start(bf16[32,1536]{1,0:T(8,128)(2,1)S(1)} %get-tuple-element.58), channel_id=1, source_target_pairs={{0,6},{2,4},{4,2},{6,0},{8,14},{10,12},{12,10},{14,8},{16,22},{18,... | collective-permute-start | bytes 294920 | tf_op jit(solution)/shard_map/ppermute | solution.py:327
  49.0 20.8 %collective-permute-start.15 = (bf16[3,16,1536]{2,1,0:T(8,128)(2,1)S(1)}, bf16[3,16,1536]{2,1,0:T(8,128)(2,1)S(1)}, u32[]{:S(2)}, u32[]{:S(2)}) collective-permute-start(bf16[3,16,1536]{2,1,0:T(8,128)(2,1)S(1)} %pad_maximum_fusion.6), channel_id=1, source_target_pairs={{0,2},{2,0},{4,6},{6,4},{8,10},{10,8},{12,14},{14,12},{16,18},{18,... | collective-permute-start | bytes 442376 | tf_op jit(solution)/shard_map/ppermute | solution.py:331
  49.5 27.0 %collective-permute-start.12 = (bf16[3,16,1536]{2,1,0:T(8,128)(2,1)S(1)}, bf16[3,16,1536]{2,1,0:T(8,128)(2,1)S(1)}, u32[]{:S(2)}, u32[]{:S(2)}) collective-permute-start(bf16[3,16,1536]{2,1,0:T(8,128)(2,1)S(1)} %pad_maximum_fusion.5), channel_id=1, source_target_pairs={{0,4},{2,6},{4,0},{6,2},{8,12},{10,14},{12,8},{14,10},{16,20},{18,... | collective-permute-start | bytes 442376 | tf_op jit(solution)/shard_map/ppermute | solution.py:331
  52.6 2.5 %collective-permute-start.21 = (bf16[4,32,1536]{2,1,0:T(8,128)(2,1)S(1)}, bf16[4,32,1536]{2,1,0:T(8,128)(2,1)S(1)}, u32[]{:S(2)}, u32[]{:S(2)}) collective-permute-start(bf16[4,32,1536]{2,1,0:T(8,128)(2,1)S(1)} %pad_maximum_fusion.refs_1_), channel_id=1, source_target_pairs={{0,1},{1,0},{2,3},{3,2},{4,5},{5,4},{6,7},{7,6},{8,9},{9,8},{10,11... | collective-permute-start | bytes 1179656 | tf_op jit(solution)/shard_map/ppermute | solution.py:306
  52.7 2.1 %collective-permute-start.17 = (bf16[3,32,1536]{2,1,0:T(8,128)(2,1)S(1)}, bf16[3,32,1536]{2,1,0:T(8,128)(2,1)S(1)}, u32[]{:S(2)}, u32[]{:S(2)}) collective-permute-start(bf16[3,32,1536]{2,1,0:T(8,128)(2,1)S(1)} %pad_maximum_fusion.1), channel_id=1, source_target_pairs={{0,1},{1,0},{2,3},{3,2},{4,5},{5,4},{6,7},{7,6},{8,9},{9,8},{10,11... | collective-permute-start | bytes 884744 | tf_op jit(solution)/shard_map/ppermute | solution.py:306
  53.3 14.5 %collective-permute-start.16 = (bf16[3,32,1536]{2,1,0:T(8,128)(2,1)S(1)}, bf16[3,32,1536]{2,1,0:T(8,128)(2,1)S(1)}, u32[]{:S(2)}, u32[]{:S(2)}) collective-permute-start(bf16[3,32,1536]{2,1,0:T(8,128)(2,1)S(1)} %pad_maximum_fusion.1), channel_id=1, source_target_pairs={{0,2},{2,0},{4,6},{6,4},{8,10},{10,8},{12,14},{14,12},{16,18},{18,... | collective-permute-start | bytes 884744 | tf_op jit(solution)/shard_map/ppermute | solution.py:336
  54.8 16.0 %collective-permute-start.13 = (bf16[3,32,1536]{2,1,0:T(8,128)(2,1)S(1)}, bf16[3,32,1536]{2,1,0:T(8,128)(2,1)S(1)}, u32[]{:S(2)}, u32[]{:S(2)}) collective-permute-start(bf16[3,32,1536]{2,1,0:T(8,128)(2,1)S(1)} %pad_maximum_fusion.1), channel_id=1, source_target_pairs={{0,4},{2,6},{4,0},{6,2},{8,12},{10,14},{12,8},{14,10},{16,20},{18,... | collective-permute-start | bytes 884744 | tf_op jit(solution)/shard_map/ppermute | solution.py:336
  55.0 16.0 %collective-permute-start.10 = (bf16[3,32,1536]{2,1,0:T(8,128)(2,1)S(1)}, bf16[3,32,1536]{2,1,0:T(8,128)(2,1)S(1)}, u32[]{:S(2)}, u32[]{:S(2)}) collective-permute-start(bf16[3,32,1536]{2,1,0:T(8,128)(2,1)S(1)} %pad_maximum_fusion.1), channel_id=1, source_target_pairs={{0,6},{2,4},{4,2},{6,0},{8,14},{10,12},{12,10},{14,8},{16,22},{18,... | collective-permute-start | bytes 884744 | tf_op jit(solution)/shard_map/ppermute | solution.py:336
  67.8 3.5 %collective-permute-start.22 = (bf16[3,32,1536]{2,1,0:T(8,128)(2,1)S(1)}, bf16[3,32,1536]{2,1,0:T(8,128)(2,1)S(1)}, u32[]{:S(2)}, u32[]{:S(2)}) collective-permute-start(bf16[3,32,1536]{2,1,0:T(8,128)(2,1)S(1)} %collective-permute-done.16.refs_1_), channel_id=1, source_target_pairs={{0,1},{1,0},{2,3},{3,2},{4,5},{5,4},{6,7},{7,6},{8,9},{9,8},{10,11... | collective-permute-start | bytes 884744 | tf_op jit(solution)/shard_map/ppermute | solution.py:306
  69.7 12.2 %collective-permute-start.3 = (bf16[3,16,1536]{2,1,0:T(8,128)(2,1)S(1)}, bf16[3,16,1536]{2,1,0:T(8,128)(2,1)S(1)}, u32[]{:S(2)}, u32[]{:S(2)}) collective-permute-start(bf16[3,16,1536]{2,1,0:T(8,128)(2,1)S(1)} %pad_maximum_fusion.4), channel_id=1, source_target_pairs={{0,6},{2,4},{4,2},{6,0},{8,14},{10,12},{12,10},{14,8},{16,22},{18,... | collective-permute-start | bytes 442376 | tf_op jit(solution)/shard_map/ppermute | solution.py:331
  70.8 5.7 %collective-permute-start.14 = (bf16[3,32,1536]{2,1,0:T(8,128)(2,1)S(1)}, bf16[3,32,1536]{2,1,0:T(8,128)(2,1)S(1)}, u32[]{:S(2)}, u32[]{:S(2)}) collective-permute-start(bf16[3,32,1536]{2,1,0:T(8,128)(2,1)S(1)} %collective-permute-done.13.refs_1_), channel_id=1, source_target_pairs={{0,1},{1,0},{2,3},{3,2},{4,5},{5,4},{6,7},{7,6},{8,9},{9,8},{10,11... | collective-permute-start | bytes 884744 | tf_op jit(solution)/shard_map/ppermute | solution.py:306
  71.0 11.0 %collective-permute-start.11 = (bf16[3,32,1536]{2,1,0:T(8,128)(2,1)S(1)}, bf16[3,32,1536]{2,1,0:T(8,128)(2,1)S(1)}, u32[]{:S(2)}, u32[]{:S(2)}) collective-permute-start(bf16[3,32,1536]{2,1,0:T(8,128)(2,1)S(1)} %collective-permute-done.10.refs_1_), channel_id=1, source_target_pairs={{0,1},{1,0},{2,3},{3,2},{4,5},{5,4},{6,7},{7,6},{8,9},{9,8},{10,11... | collective-permute-start | bytes 884744 | tf_op jit(solution)/shard_map/ppermute | solution.py:306

commit v6 on v5

--- a/solution.py
+++ b/solution.py
@@ -331,7 +331,7 @@
         lax.ppermute(jnp.stack([pick(h, here ^ d, 0) for h in held[1:]]), "tm", flip(devices, d))
         for d in range(1, 4)
     ]
-    *column, pairs = lax.optimization_barrier((*column, pairs))
+    column, beside, pairs = lax.optimization_barrier((column, beside, pairs))
     column = jnp.stack(column)
     there = [lax.ppermute(column, "tm", flip(devices, d)) for d in range(1, 4)]
     other = swap(column)

time: 88.2 us -> 87.8 us (level)
  waiting for transfers between devices: 15 us -> 11.9 us
  starting transfers between devices: 33.9 us -> 36.6 us
    ppermute x3, waiting for transfers between devices: 2.4 us -> 0.01 us  [spread(): beside = [lax.ppermute(pairs, 'tm', flip(devices, d)) for d in range(1, 4)]]
    ppermute x3, starting transfers between devices: 2.16 us -> 3.65 us  [spread(): lax.ppermute(jnp.stack([pick(h, here ^ d, 0) for h in held[1:]]), 'tm', f...]
    ppermute x3, starting transfers between devices: 2.69 us -> 3.62 us  [spread(): beside = [lax.ppermute(pairs, 'tm', flip(devices, d)) for d in range(1, 4)]]
  transfers between devices with their start and end apart: 25 -> 25, of which waited for: 6 -> 5; matrix products, arithmetic and copies ran while one was open for 2% -> 2% of each run, Pallas kernels for 31% -> 31%
where the time goes in v6:
time: 87.8 us; the launch traced here: 87.5 us
  starting transfers between devices  36.6 us (42%)
  Pallas kernels  34.4 us (39%)
  waiting for transfers between devices  11.9 us (14%)
  local copies, waits for them, and re-layouts  1.77 us (2%)
  other arithmetic  1.75 us (2%)
  between operations  1.05 us (1%)
    pallas_call x6, Pallas kernels, histogram(): pl.pallas_call(functools.partial(hist_kernel, blocks // joined, feature_c...  29.1 us
    all_to_all x2, starting transfers between devices, exchange(): return lax.all_to_all(total, 'tm', 0, 0)  12.1 us
    all_to_all x2, waiting for transfers between devices, exchange(): return lax.all_to_all(total, 'tm', 0, 0)  6.1 us
    ppermute x3, starting transfers between devices, send_planes(): lax.ppermute(pick(codes, (plane + d) % planes, 0), 'tm', ring(devices, d))  5.72 us
    pallas_call x5, Pallas kernels, call(): pl.pallas_call(kernel, out_shape=out_shape, in_specs=([SMEM] if place els...  5.33 us
    ppermute x3, starting transfers between devices, spread(): lax.ppermute(pairs, 'tm', ring(devices, d))  3.83 us
    ppermute x3, waiting for transfers between devices, spread(): lax.ppermute(pairs, 'tm', ring(devices, d))  3.67 us
    ppermute x3, starting transfers between devices, spread(): lax.ppermute(jnp.stack([pick(h, here ^ d, 0) for h in held[1:]]), 'tm', f...  3.65 us
  transfers between devices with their start and end apart: 25, of which 5 were waited for; matrix products, arithmetic and copies ran while one was open for 2% of the time, Pallas kernels for 31%

profile of v6, /device:TPU:0, one launch (start us, length us, event | category | flops | bytes accessed | tf_op | source)
XLA Modules:
  0.0 87.5 jit_solution(18189248386195834501)
XLA Ops:
  0.6 0.9 %copy-done = f32[16,1536]{1,0:T(8,128)S(1)} copy-done((f32[16,1536]{1,0:T(8,128)S(1)}, f32[16,1536]{1,0:T(8,128)}, u32[]{:S(2)}) %copy-start) | copy-done | bytes 98328
  1.5 1.4 %risk.1 = (f32[16,1536]{1,0:T(8,128)S(1)}, f32[16,16,128]{2,1,0:T(8,128)}) custom-call(f32[16,1536]{1,0:T(8,128)S(1)} %copy-done), custom_call_target="tpu_custom_call" | custom-call | tf_op jit(solution)/shard_map/risk/pallas_call | solution.py:279
  3.0 8.3 %all-to-all-start = ((f32[16,16,128]{2,1,0:T(8,128)}), f32[16,16,128]{2,1,0:T(8,128)S(1)}, u32[]{:S(2)}, u32[]{:S(2)}) async-start(f32[16,16,128]{2,1,0:T(8,128)} %get-tuple-element.37), calls=%async_computation | async-start | bytes 262144 | tf_op jit(solution)/shard_map/all_to_all | solution.py:363
  11.4 0.7 copy-done.3
  12.1 0.7 opens.1.local_ref
  12.7 1.5 %convert_element_type.3 = bf16[256,1536]{1,0:T(8,128)(2,1)S(1)} convert(s32[256,1536]{1,0:T(8,128)} %param.9) | non-fusion elementwise | flops 393216 | bytes 2359296 | tf_op jit(solution)/shard_map/convert_element_type | solution.py:369
  14.4 1.9 %collective-permute-start = (bf16[4,16,1536]{2,1,0:T(8,128)(2,1)S(1)}, bf16[4,16,1536]{2,1,0:T(8,128)(2,1)S(1)}, u32[]{:S(2)}, u32[]{:S(2)}) collective-permute-start(bf16[4,16,1536]{2,1,0:T(8,128)(2,1)S(1)} %get-tuple-element.69), channel_id=1, source_target_pairs={{0,8},{2,10},{4,12},{6,14},{8,16},{10,18},{12,20},{14,22},{16,24},... | collective-permute-start | bytes 589832 | tf_op jit(solution)/shard_map/ppermute | solution.py:319
  16.3 2.4 %collective-permute-start.1 = (bf16[4,16,1536]{2,1,0:T(8,128)(2,1)S(1)}, bf16[4,16,1536]{2,1,0:T(8,128)(2,1)S(1)}, u32[]{:S(2)}, u32[]{:S(2)}) collective-permute-start(bf16[4,16,1536]{2,1,0:T(8,128)(2,1)S(1)} %get-tuple-element.68), channel_id=1, source_target_pairs={{0,16},{2,18},{4,20},{6,22},{8,24},{10,26},{12,28},{14,30},{16,0},... | collective-permute-start | bytes 589832 | tf_op jit(solution)/shard_map/ppermute | solution.py:319
  18.7 1.5 %collective-permute-start.2 = (bf16[4,16,1536]{2,1,0:T(8,128)(2,1)S(1)}, bf16[4,16,1536]{2,1,0:T(8,128)(2,1)S(1)}, u32[]{:S(2)}, u32[]{:S(2)}) collective-permute-start(bf16[4,16,1536]{2,1,0:T(8,128)(2,1)S(1)} %get-tuple-element.67), channel_id=1, source_target_pairs={{0,24},{2,26},{4,28},{6,30},{8,0},{10,2},{12,4},{14,6},{16,8},{18,... | collective-permute-start | bytes 589832 | tf_op jit(solution)/shard_map/ppermute | solution.py:319
  20.1 1.7 %events.1 = (f32[16,1536]{1,0:T(8,128)S(1)}, f32[16,1536]{1,0:T(8,128)S(1)}, f32[16,1,128]{2,1,0:T(1,128)}) custom-call(s32[1]{0:T(128)} %bitcast.place_ref, f32[16,1536]{1,0:T(8,128)S(1)} %opens.1.local_ref, f32[16,16,128]{2,1,0:T(8,128)S(1)} %all-to-all-done.parts_ref, s32[16,1536]{1,0:T(8,128)S(1)} %copy-done.2), custom_call_target="tpu_custom_call" | custom-call | tf_op jit(solution)/shard_map/events/pallas_call | solution.py:279
  21.9 3.7 %all-to-all-start.1 = ((f32[16,1,128]{2,1,0:T(1,128)}), f32[16,1,128]{2,1,0:T(1,128)S(1)}, u32[]{:S(2)}, u32[]{:S(2)}) async-start(f32[16,1,128]{2,1,0:T(1,128)} %get-tuple-element.44), calls=%async_computation.1 | async-start | bytes 16384 | tf_op jit(solution)/shard_map/all_to_all | solution.py:363
  25.6 2.0 %collective-permute-start.4 = (bf16[16,1536]{1,0:T(8,128)(2,1)S(1)}, bf16[16,1536]{1,0:T(8,128)(2,1)S(1)}, u32[]{:S(2)}, u32[]{:S(2)}) collective-permute-start(bf16[16,1536]{1,0:T(8,128)(2,1)S(1)} %get-tuple-element.85), channel_id=1, source_target_pairs={{0,2},{2,0},{4,6},{6,4},{8,10},{10,8},{12,14},{14,12},{16,18},{18,... | collective-permute-start | bytes 147464 | tf_op jit(solution)/shard_map/ppermute | solution.py:383
  27.6 1.5 %collective-permute-start.5 = (bf16[16,1536]{1,0:T(8,128)(2,1)S(1)}, bf16[16,1536]{1,0:T(8,128)(2,1)S(1)}, u32[]{:S(2)}, u32[]{:S(2)}) collective-permute-start(bf16[16,1536]{1,0:T(8,128)(2,1)S(1)} %get-tuple-element.84), channel_id=1, source_target_pairs={{0,4},{2,6},{4,0},{6,2},{8,12},{10,14},{12,8},{14,10},{16,20},{18,... | collective-permute-start | bytes 147464 | tf_op jit(solution)/shard_map/ppermute | solution.py:383
  29.9 1.3 %collective-permute-done.1 = bf16[4,16,1536]{2,1,0:T(8,128)(2,1)S(1)} collective-permute-done((bf16[4,16,1536]{2,1,0:T(8,128)(2,1)S(1)}, bf16[4,16,1536]{2,1,0:T(8,128)(2,1)S(1)}, u32[]{:S(2)}, u32[]{:S(2)}) %collective-permute-start.1) | collective-permute-done | bytes 196640 | tf_op jit(solution)/shard_map/ppermute | solution.py:319
  31.2 6.1 %all-to-all-done.1.parts_ref = f32[16,1,128]{2,1,0:T(1,128)S(1)} async-done(((f32[16,1,128]{2,1,0:T(1,128)}), f32[16,1,128]{2,1,0:T(1,128)S(1)}, u32[]{:S(2)}, u32[]{:S(2)}) %all-to-all-start.1) | async-done | bytes 8224 | tf_op jit(solution)/shard_map/all_to_all | solution.py:363
  37.5 0.9 grads.1
  39.6 2.4 %collective-permute-start.12 = (bf16[32,1536]{1,0:T(8,128)(2,1)S(1)}, bf16[32,1536]{1,0:T(8,128)(2,1)S(1)}, u32[]{:S(2)}, u32[]{:S(2)}) collective-permute-start(bf16[32,1536]{1,0:T(8,128)(2,1)S(1)} %get-tuple-element.61), channel_id=1, source_target_pairs={{0,6},{2,4},{4,2},{6,0},{8,14},{10,12},{12,10},{14,8},{16,22},{18,... | collective-permute-start | bytes 294920 | tf_op jit(solution)/shard_map/ppermute | solution.py:327
  42.6 1.5 %collective-permute-start.8 = (bf16[32,1536]{1,0:T(8,128)(2,1)S(1)}, bf16[32,1536]{1,0:T(8,128)(2,1)S(1)}, u32[]{:S(2)}, u32[]{:S(2)}) collective-permute-start(bf16[32,1536]{1,0:T(8,128)(2,1)S(1)} %get-tuple-element.61), channel_id=1, source_target_pairs={{0,16},{2,18},{4,20},{6,22},{8,24},{10,26},{12,28},{14,30},{16,0},... | collective-permute-start | bytes 294920 | tf_op jit(solution)/shard_map/ppermute | solution.py:326
  44.0 1.8 %collective-permute-start.9 = (bf16[32,1536]{1,0:T(8,128)(2,1)S(1)}, bf16[32,1536]{1,0:T(8,128)(2,1)S(1)}, u32[]{:S(2)}, u32[]{:S(2)}) collective-permute-start(bf16[32,1536]{1,0:T(8,128)(2,1)S(1)} %get-tuple-element.61), channel_id=1, source_target_pairs={{0,24},{2,26},{4,28},{6,30},{8,0},{10,2},{12,4},{14,6},{16,8},{18,... | collective-permute-start | bytes 294920 | tf_op jit(solution)/shard_map/ppermute | solution.py:326
  45.8 1.1 %collective-permute-start.18 = (bf16[3,16,1536]{2,1,0:T(8,128)(2,1)S(1)}, bf16[3,16,1536]{2,1,0:T(8,128)(2,1)S(1)}, u32[]{:S(2)}, u32[]{:S(2)}) collective-permute-start(bf16[3,16,1536]{2,1,0:T(8,128)(2,1)S(1)} %pad_maximum_fusion.6), channel_id=1, source_target_pairs={{0,2},{2,0},{4,6},{6,4},{8,10},{10,8},{12,14},{14,12},{16,18},{18,... | collective-permute-start | bytes 442376 | tf_op jit(solution)/shard_map/ppermute | solution.py:331
  46.9 1.2 %collective-permute-start.15 = (bf16[3,16,1536]{2,1,0:T(8,128)(2,1)S(1)}, bf16[3,16,1536]{2,1,0:T(8,128)(2,1)S(1)}, u32[]{:S(2)}, u32[]{:S(2)}) collective-permute-start(bf16[3,16,1536]{2,1,0:T(8,128)(2,1)S(1)} %pad_maximum_fusion.5), channel_id=1, source_target_pairs={{0,4},{2,6},{4,0},{6,2},{8,12},{10,14},{12,8},{14,10},{16,20},{18,... | collective-permute-start | bytes 442376 | tf_op jit(solution)/shard_map/ppermute | solution.py:331
  48.1 1.4 %collective-permute-done.7 = bf16[32,1536]{1,0:T(8,128)(2,1)S(1)} collective-permute-done((bf16[32,1536]{1,0:T(8,128)(2,1)S(1)}, bf16[32,1536]{1,0:T(8,128)(2,1)S(1)}, u32[]{:S(2)}, u32[]{:S(2)}) %collective-permute-start.7) | collective-permute-done | bytes 98336 | tf_op jit(solution)/shard_map/ppermute | solution.py:326
  49.5 2.2 %collective-permute-done.8 = bf16[32,1536]{1,0:T(8,128)(2,1)S(1)} collective-permute-done((bf16[32,1536]{1,0:T(8,128)(2,1)S(1)}, bf16[32,1536]{1,0:T(8,128)(2,1)S(1)}, u32[]{:S(2)}, u32[]{:S(2)}) %collective-permute-start.8) | collective-permute-done | bytes 98336 | tf_op jit(solution)/shard_map/ppermute | solution.py:326
  53.1 0.8 collective-permute-done.20
  54.6 1.6 %collective-permute-start.13 = (bf16[3,32,1536]{2,1,0:T(8,128)(2,1)S(1)}, bf16[3,32,1536]{2,1,0:T(8,128)(2,1)S(1)}, u32[]{:S(2)}, u32[]{:S(2)}) collective-permute-start(bf16[3,32,1536]{2,1,0:T(8,128)(2,1)S(1)} %pad_maximum_fusion.1), channel_id=1, source_target_pairs={{0,6},{2,4},{4,2},{6,0},{8,14},{10,12},{12,10},{14,8},{16,22},{18,... | collective-permute-start | bytes 884744 | tf_op jit(solution)/shard_map/ppermute | solution.py:336
  56.3 7.2 %hist.6.refs_3_ = f32[16,128,128]{2,1,0:T(8,128)S(1)} custom-call(bf16[4,16,1536]{2,1,0:T(8,128)(2,1)S(1)} %pad_maximum_fusion.3.refs_0_, bf16[4,32,1536]{2,1,0:T(8,128)(2,1)S(1)} %pad_maximum_fusion.refs_1_, bf16[4,32,1536]{2,1,0:T(8,128)(2,1)S(1)} %collective-permute-done.21.refs_2_), custom_call_target="tpu_custom_call" | custom-call | flops 12884901888 | bytes 983040 | tf_op jit(solution)/shard_map/hist/pallas_call | solution.py:259
  63.4 3.6 %hist.7.refs_3_ = f32[16,128,128]{2,1,0:T(8,128)S(1)} custom-call(bf16[2,16,1536]{2,1,0:T(8,128)(2,1)S(1)} %pad_maximum_fusion.7.refs_0_, bf16[2,32,1536]{2,1,0:T(8,128)(2,1)S(1)} %pad_maximum_fusion.2.refs_1_, bf16[2,32,1536]{2,1,0:T(8,128)(2,1)S(1)} %slice.10.refs_2_, f32[16,128,128]{2,1,0:T(8,128)S(1)} %hist.6.refs_3_), custom_call_target="tpu_custom_call", output_to_operand_aliasing={{}: (3, {})} | custom-call | flops 6442450944 | bytes 491520 | tf_op jit(solution)/shard_map/hist/pallas_call | solution.py:259
  67.1 1.9 %hist.8.refs_3_ = f32[16,128,128]{2,1,0:T(8,128)S(1)} custom-call(bf16[1,16,1536]{2,1,0:T(8,128)(2,1)S(1)} %get-tuple-element.71.refs_0_, bf16[1,32,1536]{2,1,0:T(8,128)(2,1)S(1)} %bitcast.28, bf16[1,32,1536]{2,1,0:T(8,128)(2,1)S(1)} %slice.11.refs_2_, f32[16,128,128]{2,1,0:T(8,128)S(1)} %hist.7.refs_3_), custom_call_target="tpu_custom_call", output_to_operand_aliasing={{}: (3, {})} | custom-call | flops 3221225472 | bytes 245760 | tf_op jit(solution)/shard_map/hist/pallas_call | solution.py:259
  69.0 1.4 %collective-permute-start.3 = (bf16[3,16,1536]{2,1,0:T(8,128)(2,1)S(1)}, bf16[3,16,1536]{2,1,0:T(8,128)(2,1)S(1)}, u32[]{:S(2)}, u32[]{:S(2)}) collective-permute-start(bf16[3,16,1536]{2,1,0:T(8,128)(2,1)S(1)} %pad_maximum_fusion.4), channel_id=1, source_target_pairs={{0,6},{2,4},{4,2},{6,0},{8,14},{10,12},{12,10},{14,8},{16,22},{18,... | collective-permute-start | bytes 442376 | tf_op jit(solution)/shard_map/ppermute | solution.py:331
  70.9 5.2 %hist.9.refs_3_ = f32[16,128,128]{2,1,0:T(8,128)S(1)} custom-call(bf16[3,16,1536]{2,1,0:T(8,128)(2,1)S(1)} %collective-permute-done.18.refs_0_, bf16[3,32,1536]{2,1,0:T(8,128)(2,1)S(1)} %collective-permute-done.19.refs_1_, bf16[3,32,1536]{2,1,0:T(8,128)(2,1)S(1)} %collective-permute-done.22.refs_2_, ...), custom_call_target="tpu_custom_call", output_to_operand_aliasing={{}: (3, {})} | custom-call | flops 9663676416 | bytes 737280 | tf_op jit(solution)/shard_map/hist/pallas_call | solution.py:259
  76.1 5.4 %hist.10.refs_3_ = f32[16,128,128]{2,1,0:T(8,128)S(1)} custom-call(bf16[3,16,1536]{2,1,0:T(8,128)(2,1)S(1)} %collective-permute-done.15.refs_0_, bf16[3,32,1536]{2,1,0:T(8,128)(2,1)S(1)} %collective-permute-done.16.refs_1_, bf16[3,32,1536]{2,1,0:T(8,128)(2,1)S(1)} %collective-permute-done.17.refs_2_, ...), custom_call_target="tpu_custom_call", output_to_operand_aliasing={{}: (3, {})} | custom-call | flops 9663676416 | bytes 737280 | tf_op jit(solution)/shard_map/hist/pallas_call | solution.py:259
  81.6 5.9 %hist.11 = f32[16,256]{1,0:T(8,128)} custom-call(bf16[3,16,1536]{2,1,0:T(8,128)(2,1)S(1)} %collective-permute-done.3.refs_0_, bf16[3,32,1536]{2,1,0:T(8,128)(2,1)S(1)} %collective-permute-done.13.refs_1_, bf16[3,32,1536]{2,1,0:T(8,128)(2,1)S(1)} %collective-permute-done.14.refs_2_, f32[16,128,128]{2,1,0:T(8,128)S(1)} %hist.10.refs_3_), custom_call_target="tpu_custom_call" | custom-call | flops 9663676416 | bytes 737280 | tf_op jit(solution)/shard_map/hist/pallas_call | solution.py:259
  (57 shorter events, 5.5 us)
Async XLA Ops:
  0.6 0.9 %copy-start = (f32[16,1536]{1,0:T(8,128)S(1)}, f32[16,1536]{1,0:T(8,128)}, u32[]{:S(2)}) copy-start(f32[16,1536]{1,0:T(8,128)} %margins_ref.3) | copy-start | bytes 294916
  3.0 17.2 %all-to-all-start = ((f32[16,16,128]{2,1,0:T(8,128)}), f32[16,16,128]{2,1,0:T(8,128)S(1)}, u32[]{:S(2)}, u32[]{:S(2)}) async-start(f32[16,16,128]{2,1,0:T(8,128)} %get-tuple-element.37), calls=%async_computation | async-start | bytes 262144 | tf_op jit(solution)/shard_map/all_to_all | solution.py:363
  11.4 0.7 copy-start.3
  12.7 7.4 %copy-start.2 = (s32[16,1536]{1,0:T(8,128)S(1)}, s32[16,1536]{1,0:T(8,128)}, u32[]{:S(2)}) copy-start(s32[16,1536]{1,0:T(8,128)} %events_ref.3) | copy-start | bytes 294916
  14.3 14.8 %copy-start.4 = (s32[1536]{0:T(1024)S(1)}, s32[1536]{0:T(1024)}, u32[]{:S(2)}) copy-start(s32[1536]{0:T(1024)} %tie_ref.3) | copy-start | bytes 18436
  14.4 23.1 %copy-start.1 = (f32[16,1536]{1,0:T(8,128)S(1)}, f32[16,1536]{1,0:T(8,128)}, u32[]{:S(2)}) copy-start(f32[16,1536]{1,0:T(8,128)} %margins_ref.3) | copy-start | bytes 294916
  14.4 23.1 %copy-start.5 = (s32[1536]{0:T(1024)S(1)}, s32[1536]{0:T(1024)}, u32[]{:S(2)}) copy-start(s32[1536]{0:T(1024)} %node_ref.1) | copy-start | bytes 18436
  14.4 15.3 %collective-permute-start = (bf16[4,16,1536]{2,1,0:T(8,128)(2,1)S(1)}, bf16[4,16,1536]{2,1,0:T(8,128)(2,1)S(1)}, u32[]{:S(2)}, u32[]{:S(2)}) collective-permute-start(bf16[4,16,1536]{2,1,0:T(8,128)(2,1)S(1)} %get-tuple-element.69), channel_id=1, source_target_pairs={{0,8},{2,10},{4,12},{6,14},{8,16},{10,18},{12,20},{14,22},{16,24},... | collective-permute-start | bytes 589832 | tf_op jit(solution)/shard_map/ppermute | solution.py:319
  16.3 14.9 %collective-permute-start.1 = (bf16[4,16,1536]{2,1,0:T(8,128)(2,1)S(1)}, bf16[4,16,1536]{2,1,0:T(8,128)(2,1)S(1)}, u32[]{:S(2)}, u32[]{:S(2)}) collective-permute-start(bf16[4,16,1536]{2,1,0:T(8,128)(2,1)S(1)} %get-tuple-element.68), channel_id=1, source_target_pairs={{0,16},{2,18},{4,20},{6,22},{8,24},{10,26},{12,28},{14,30},{16,0},... | collective-permute-start | bytes 589832 | tf_op jit(solution)/shard_map/ppermute | solution.py:319
  18.7 12.5 %collective-permute-start.2 = (bf16[4,16,1536]{2,1,0:T(8,128)(2,1)S(1)}, bf16[4,16,1536]{2,1,0:T(8,128)(2,1)S(1)}, u32[]{:S(2)}, u32[]{:S(2)}) collective-permute-start(bf16[4,16,1536]{2,1,0:T(8,128)(2,1)S(1)} %get-tuple-element.67), channel_id=1, source_target_pairs={{0,24},{2,26},{4,28},{6,30},{8,0},{10,2},{12,4},{14,6},{16,8},{18,... | collective-permute-start | bytes 589832 | tf_op jit(solution)/shard_map/ppermute | solution.py:319
  21.9 15.4 %all-to-all-start.1 = ((f32[16,1,128]{2,1,0:T(1,128)}), f32[16,1,128]{2,1,0:T(1,128)S(1)}, u32[]{:S(2)}, u32[]{:S(2)}) async-start(f32[16,1,128]{2,1,0:T(1,128)} %get-tuple-element.44), calls=%async_computation.1 | async-start | bytes 16384 | tf_op jit(solution)/shard_map/all_to_all | solution.py:363
  25.6 12.7 %collective-permute-start.4 = (bf16[16,1536]{1,0:T(8,128)(2,1)S(1)}, bf16[16,1536]{1,0:T(8,128)(2,1)S(1)}, u32[]{:S(2)}, u32[]{:S(2)}) collective-permute-start(bf16[16,1536]{1,0:T(8,128)(2,1)S(1)} %get-tuple-element.85), channel_id=1, source_target_pairs={{0,2},{2,0},{4,6},{6,4},{8,10},{10,8},{12,14},{14,12},{16,18},{18,... | collective-permute-start | bytes 147464 | tf_op jit(solution)/shard_map/ppermute | solution.py:383
  27.6 10.7 %collective-permute-start.5 = (bf16[16,1536]{1,0:T(8,128)(2,1)S(1)}, bf16[16,1536]{1,0:T(8,128)(2,1)S(1)}, u32[]{:S(2)}, u32[]{:S(2)}) collective-permute-start(bf16[16,1536]{1,0:T(8,128)(2,1)S(1)} %get-tuple-element.84), channel_id=1, source_target_pairs={{0,4},{2,6},{4,0},{6,2},{8,12},{10,14},{12,8},{14,10},{16,20},{18,... | collective-permute-start | bytes 147464 | tf_op jit(solution)/shard_map/ppermute | solution.py:383
  29.8 8.6 %collective-permute-start.6 = (bf16[16,1536]{1,0:T(8,128)(2,1)S(1)}, bf16[16,1536]{1,0:T(8,128)(2,1)S(1)}, u32[]{:S(2)}, u32[]{:S(2)}) collective-permute-start(bf16[16,1536]{1,0:T(8,128)(2,1)S(1)} %get-tuple-element.83), channel_id=1, source_target_pairs={{0,6},{2,4},{4,2},{6,0},{8,14},{10,12},{12,10},{14,8},{16,22},{18,... | collective-permute-start | bytes 147464 | tf_op jit(solution)/shard_map/ppermute | solution.py:383
  38.4 5.7 %collective-permute-start.10 = (bf16[32,1536]{1,0:T(8,128)(2,1)S(1)}, bf16[32,1536]{1,0:T(8,128)(2,1)S(1)}, u32[]{:S(2)}, u32[]{:S(2)}) collective-permute-start(bf16[32,1536]{1,0:T(8,128)(2,1)S(1)} %get-tuple-element.61), channel_id=1, source_target_pairs={{0,2},{2,0},{4,6},{6,4},{8,10},{10,8},{12,14},{14,12},{16,18},{18,... | collective-permute-start | bytes 294920 | tf_op jit(solution)/shard_map/ppermute | solution.py:327
  39.0 6.8 %collective-permute-start.11 = (bf16[32,1536]{1,0:T(8,128)(2,1)S(1)}, bf16[32,1536]{1,0:T(8,128)(2,1)S(1)}, u32[]{:S(2)}, u32[]{:S(2)}) collective-permute-start(bf16[32,1536]{1,0:T(8,128)(2,1)S(1)} %get-tuple-element.61), channel_id=1, source_target_pairs={{0,4},{2,6},{4,0},{6,2},{8,12},{10,14},{12,8},{14,10},{16,20},{18,... | collective-permute-start | bytes 294920 | tf_op jit(solution)/shard_map/ppermute | solution.py:327
  39.6 7.3 %collective-permute-start.12 = (bf16[32,1536]{1,0:T(8,128)(2,1)S(1)}, bf16[32,1536]{1,0:T(8,128)(2,1)S(1)}, u32[]{:S(2)}, u32[]{:S(2)}) collective-permute-start(bf16[32,1536]{1,0:T(8,128)(2,1)S(1)} %get-tuple-element.61), channel_id=1, source_target_pairs={{0,6},{2,4},{4,2},{6,0},{8,14},{10,12},{12,10},{14,8},{16,22},{18,... | collective-permute-start | bytes 294920 | tf_op jit(solution)/shard_map/ppermute | solution.py:327
  42.0 7.5 %collective-permute-start.7 = (bf16[32,1536]{1,0:T(8,128)(2,1)S(1)}, bf16[32,1536]{1,0:T(8,128)(2,1)S(1)}, u32[]{:S(2)}, u32[]{:S(2)}) collective-permute-start(bf16[32,1536]{1,0:T(8,128)(2,1)S(1)} %get-tuple-element.61), channel_id=1, source_target_pairs={{0,8},{2,10},{4,12},{6,14},{8,16},{10,18},{12,20},{14,22},{16,24},... | collective-permute-start | bytes 294920 | tf_op jit(solution)/shard_map/ppermute | solution.py:326
  42.6 9.2 %collective-permute-start.8 = (bf16[32,1536]{1,0:T(8,128)(2,1)S(1)}, bf16[32,1536]{1,0:T(8,128)(2,1)S(1)}, u32[]{:S(2)}, u32[]{:S(2)}) collective-permute-start(bf16[32,1536]{1,0:T(8,128)(2,1)S(1)} %get-tuple-element.61), channel_id=1, source_target_pairs={{0,16},{2,18},{4,20},{6,22},{8,24},{10,26},{12,28},{14,30},{16,0},... | collective-permute-start | bytes 294920 | tf_op jit(solution)/shard_map/ppermute | solution.py:326
  44.0 7.7 %collective-permute-start.9 = (bf16[32,1536]{1,0:T(8,128)(2,1)S(1)}, bf16[32,1536]{1,0:T(8,128)(2,1)S(1)}, u32[]{:S(2)}, u32[]{:S(2)}) collective-permute-start(bf16[32,1536]{1,0:T(8,128)(2,1)S(1)} %get-tuple-element.61), channel_id=1, source_target_pairs={{0,24},{2,26},{4,28},{6,30},{8,0},{10,2},{12,4},{14,6},{16,8},{18,... | collective-permute-start | bytes 294920 | tf_op jit(solution)/shard_map/ppermute | solution.py:326
  45.8 23.1 %collective-permute-start.18 = (bf16[3,16,1536]{2,1,0:T(8,128)(2,1)S(1)}, bf16[3,16,1536]{2,1,0:T(8,128)(2,1)S(1)}, u32[]{:S(2)}, u32[]{:S(2)}) collective-permute-start(bf16[3,16,1536]{2,1,0:T(8,128)(2,1)S(1)} %pad_maximum_fusion.6), channel_id=1, source_target_pairs={{0,2},{2,0},{4,6},{6,4},{8,10},{10,8},{12,14},{14,12},{16,18},{18,... | collective-permute-start | bytes 442376 | tf_op jit(solution)/shard_map/ppermute | solution.py:331
  46.9 29.2 %collective-permute-start.15 = (bf16[3,16,1536]{2,1,0:T(8,128)(2,1)S(1)}, bf16[3,16,1536]{2,1,0:T(8,128)(2,1)S(1)}, u32[]{:S(2)}, u32[]{:S(2)}) collective-permute-start(bf16[3,16,1536]{2,1,0:T(8,128)(2,1)S(1)} %pad_maximum_fusion.5), channel_id=1, source_target_pairs={{0,4},{2,6},{4,0},{6,2},{8,12},{10,14},{12,8},{14,10},{16,20},{18,... | collective-permute-start | bytes 442376 | tf_op jit(solution)/shard_map/ppermute | solution.py:331
  51.8 2.8 %collective-permute-start.21 = (bf16[4,32,1536]{2,1,0:T(8,128)(2,1)S(1)}, bf16[4,32,1536]{2,1,0:T(8,128)(2,1)S(1)}, u32[]{:S(2)}, u32[]{:S(2)}) collective-permute-start(bf16[4,32,1536]{2,1,0:T(8,128)(2,1)S(1)} %pad_maximum_fusion.refs_1_), channel_id=1, source_target_pairs={{0,1},{1,0},{2,3},{3,2},{4,5},{5,4},{6,7},{7,6},{8,9},{9,8},{10,11... | collective-permute-start | bytes 1179656 | tf_op jit(solution)/shard_map/ppermute | solution.py:306
  51.9 2.1 %collective-permute-start.20 = (bf16[3,32,1536]{2,1,0:T(8,128)(2,1)S(1)}, bf16[3,32,1536]{2,1,0:T(8,128)(2,1)S(1)}, u32[]{:S(2)}, u32[]{:S(2)}) collective-permute-start(bf16[3,32,1536]{2,1,0:T(8,128)(2,1)S(1)} %pad_maximum_fusion.1), channel_id=1, source_target_pairs={{0,1},{1,0},{2,3},{3,2},{4,5},{5,4},{6,7},{7,6},{8,9},{9,8},{10,11... | collective-permute-start | bytes 884744 | tf_op jit(solution)/shard_map/ppermute | solution.py:306
  52.5 14.5 %collective-permute-start.19 = (bf16[3,32,1536]{2,1,0:T(8,128)(2,1)S(1)}, bf16[3,32,1536]{2,1,0:T(8,128)(2,1)S(1)}, u32[]{:S(2)}, u32[]{:S(2)}) collective-permute-start(bf16[3,32,1536]{2,1,0:T(8,128)(2,1)S(1)} %pad_maximum_fusion.1), channel_id=1, source_target_pairs={{0,2},{2,0},{4,6},{6,4},{8,10},{10,8},{12,14},{14,12},{16,18},{18,... | collective-permute-start | bytes 884744 | tf_op jit(solution)/shard_map/ppermute | solution.py:336
  54.0 16.4 %collective-permute-start.16 = (bf16[3,32,1536]{2,1,0:T(8,128)(2,1)S(1)}, bf16[3,32,1536]{2,1,0:T(8,128)(2,1)S(1)}, u32[]{:S(2)}, u32[]{:S(2)}) collective-permute-start(bf16[3,32,1536]{2,1,0:T(8,128)(2,1)S(1)} %pad_maximum_fusion.1), channel_id=1, source_target_pairs={{0,4},{2,6},{4,0},{6,2},{8,12},{10,14},{12,8},{14,10},{16,20},{18,... | collective-permute-start | bytes 884744 | tf_op jit(solution)/shard_map/ppermute | solution.py:336
  54.6 16.0 %collective-permute-start.13 = (bf16[3,32,1536]{2,1,0:T(8,128)(2,1)S(1)}, bf16[3,32,1536]{2,1,0:T(8,128)(2,1)S(1)}, u32[]{:S(2)}, u32[]{:S(2)}) collective-permute-start(bf16[3,32,1536]{2,1,0:T(8,128)(2,1)S(1)} %pad_maximum_fusion.1), channel_id=1, source_target_pairs={{0,6},{2,4},{4,2},{6,0},{8,14},{10,12},{12,10},{14,8},{16,22},{18,... | collective-permute-start | bytes 884744 | tf_op jit(solution)/shard_map/ppermute | solution.py:336
  67.0 3.9 %collective-permute-start.22 = (bf16[3,32,1536]{2,1,0:T(8,128)(2,1)S(1)}, bf16[3,32,1536]{2,1,0:T(8,128)(2,1)S(1)}, u32[]{:S(2)}, u32[]{:S(2)}) collective-permute-start(bf16[3,32,1536]{2,1,0:T(8,128)(2,1)S(1)} %collective-permute-done.19.refs_1_), channel_id=1, source_target_pairs={{0,1},{1,0},{2,3},{3,2},{4,5},{5,4},{6,7},{7,6},{8,9},{9,8},{10,11... | collective-permute-start | bytes 884744 | tf_op jit(solution)/shard_map/ppermute | solution.py:306
  69.0 12.6 %collective-permute-start.3 = (bf16[3,16,1536]{2,1,0:T(8,128)(2,1)S(1)}, bf16[3,16,1536]{2,1,0:T(8,128)(2,1)S(1)}, u32[]{:S(2)}, u32[]{:S(2)}) collective-permute-start(bf16[3,16,1536]{2,1,0:T(8,128)(2,1)S(1)} %pad_maximum_fusion.4), channel_id=1, source_target_pairs={{0,6},{2,4},{4,2},{6,0},{8,14},{10,12},{12,10},{14,8},{16,22},{18,... | collective-permute-start | bytes 442376 | tf_op jit(solution)/shard_map/ppermute | solution.py:331
  70.4 5.7 %collective-permute-start.17 = (bf16[3,32,1536]{2,1,0:T(8,128)(2,1)S(1)}, bf16[3,32,1536]{2,1,0:T(8,128)(2,1)S(1)}, u32[]{:S(2)}, u32[]{:S(2)}) collective-permute-start(bf16[3,32,1536]{2,1,0:T(8,128)(2,1)S(1)} %collective-permute-done.16.refs_1_), channel_id=1, source_target_pairs={{0,1},{1,0},{2,3},{3,2},{4,5},{5,4},{6,7},{7,6},{8,9},{9,8},{10,11... | collective-permute-start | bytes 884744 | tf_op jit(solution)/shard_map/ppermute | solution.py:306
  70.6 11.0 %collective-permute-start.14 = (bf16[3,32,1536]{2,1,0:T(8,128)(2,1)S(1)}, bf16[3,32,1536]{2,1,0:T(8,128)(2,1)S(1)}, u32[]{:S(2)}, u32[]{:S(2)}) collective-permute-start(bf16[3,32,1536]{2,1,0:T(8,128)(2,1)S(1)} %collective-permute-done.13.refs_1_), channel_id=1, source_target_pairs={{0,1},{1,0},{2,3},{3,2},{4,5},{5,4},{6,7},{7,6},{8,9},{9,8},{10,11... | collective-permute-start | bytes 884744 | tf_op jit(solution)/shard_map/ppermute | solution.py:306
